TPU v7x, 512 devices: a whole 4x4x16 slice. The times are simulated.
512 devices in a mesh: row: 16 (over z_hi, y), col: 32 (over z_lo, x, core).
Axes of the slice: x: 4, y: 4, z: 16 (z_hi: 4, z_lo: 4; z = z_hi * 4 + z_lo), core: 2. Of those that a mesh axis runs over, the one named last changes fastest.
Arguments:
- grad_out: bfloat16 [65536, 512], P(('row', 'col'))
- relu_mask: int32 [65536, 512], P(('row', 'col')), may hold values 0 or 1
- aggregated: bfloat16 [65536, 512], P(('row', 'col')), may hold values from -6 to 6
- weight: bfloat16 [512, 512], replicated, may hold values from -0.25 to 0.25
- adj_blocks: bfloat16 [16, 32, 85, 128, 128], P('row', 'col'), may hold values from 0 to 0.02876383
- block_pos: int32 [16, 32, 85], P('row', 'col'), may hold values from 0 to 511, as said below
- block_live: int32 [16, 32], P('row', 'col'), may hold values from 1 to 85, as said below
Outputs:
- grad_input: bfloat16 [32, 2048, 512], P('col', 'row')
- grad_weight: float32 [512, 512], replicated
- grad_bias: float32 [512], replicated
Inputs may be any that keep to these rules, and one draw needn't show every extreme that they name: `block_pos`: within one tile the 85 slots name different positions; position p is block row p // 16, block column p % 16. `block_live`: some tile uses all 85 slots.
All inputs are finite; a program needn't handle non-finite values. No bound on the sum of `relu_mask` on one device may be relied on, other than what follows from the above.
Results may differ from a plain program's by a relative error of at most 0.005.
Values may be sent and summed in bfloat16 or wider, within the bound.
No kernel may reach another device: no remote copies, remote signals or barrier semaphores. Data moves between devices by JAX's collectives and lax.ppermute only.
A program may use at most 64 MiB of HBM per device.

v0:
```python
import math

import jax
import jax.numpy as jnp
from jax import lax
from jax.sharding import PartitionSpec as P


def body(grad_out, relu_mask, aggregated, weight, adj_blocks, block_pos, block_live):
    rows_dev, feat_dim = grad_out.shape
    grad_pre = grad_out * relu_mask.astype(jnp.bfloat16)
    projected = jnp.einsum(
        "ng,fg->nf", grad_pre, weight, preferred_element_type=jnp.float32
    ).astype(jnp.bfloat16)
    row_block = lax.all_gather(projected, "col", axis=0, tiled=True)
    blocks = adj_blocks[0, 0]
    positions = block_pos[0, 0]
    live_count = block_live[0, 0]
    capacity = blocks.shape[0]
    block_width = blocks.shape[-1]
    tile_cols = lax.axis_size("row") * rows_dev // block_width
    tile_row_count = row_block.shape[0] // block_width
    stacked_tiles = row_block.reshape(tile_row_count, block_width, feat_dim)
    group_size = max((divisor for divisor in range(1, 17) if capacity % divisor == 0))
    group_turns = capacity // group_size
    column_ids = jnp.arange(tile_cols, dtype=jnp.int32)

    def add_group(running_total, turn_index):
        first_slot = turn_index * group_size
        part_blocks = lax.dynamic_slice_in_dim(blocks, first_slot, group_size, 0)
        part_slots = lax.dynamic_slice_in_dim(positions, first_slot, group_size, 0)
        selected_row_set = stacked_tiles[part_slots // tile_cols]
        partial_products = jnp.einsum(
            "kab,kaf->kbf", part_blocks, selected_row_set, preferred_element_type=jnp.float32
        )
        alive = first_slot + jnp.arange(group_size, dtype=jnp.int32) < live_count
        insert_position = ((part_slots % tile_cols)[:, None] == column_ids[None, :]) & alive[
            :, None
        ]
        update = jnp.einsum(
            "lj,lsu->jsu",
            insert_position.astype(jnp.float32),
            partial_products,
            precision=lax.Precision.HIGHEST,
        )
        return (running_total + update, None)

    start_sum = jnp.zeros((tile_cols, block_width, feat_dim), jnp.float32)
    running_total, _ = lax.scan(add_group, start_sum, jnp.arange(group_turns, dtype=jnp.int32))
    column_terms = running_total.reshape(tile_cols * block_width, feat_dim)
    summed = lax.psum_scatter(column_terms, "row", scatter_dimension=0, tiled=True)
    grad_input = summed.astype(jnp.bfloat16).reshape(1, rows_dev, feat_dim)
    weight_terms = jnp.einsum("nf,ng->fg", aggregated, grad_pre, preferred_element_type=jnp.float32)
    bias_terms = jnp.sum(grad_pre.astype(jnp.float32), axis=0)
    factor = 1.0 / math.sqrt(rows_dev * lax.axis_size("row") * lax.axis_size("col"))
    weight_gradient_total, bias_total = lax.psum((weight_terms, bias_terms), ("row", "col"))
    return (grad_input, weight_gradient_total * factor, bias_total * factor)


def solution(mesh):
    return jax.shard_map(
        body,
        mesh=mesh,
        in_specs=(
            P(("row", "col"), None),
            P(("row", "col"), None),
            P(("row", "col"), None),
            P(),
            P("row", "col", None, None, None),
            P("row", "col", None),
            P("row", "col"),
        ),
        out_specs=(P("col", "row", None), P(), P()),
        check_vma=False,
    )
```

profile of v0, /device:TPU:1, one launch (start us, length us, event | category | flops | bytes accessed | tf_op | source)
XLA Modules:
  0.0 523.1 jit_solution(11455040609310705814)
XLA Ops:
  12.5 73.2 %all-gather.2.cloned.1.call-done = bf16[4096,512]{1,0:T(8,128)(2,1)} async-done(((bf16[128,512]{1,0:T(8,128)(2,1)}), bf16[4096,512]{1,0:T(8,128)(2,1)}) %all-gather.2.cloned.1.call-update) | async-done | bytes 4194320 | tf_op jit(solution)/shard_map/all_gather | solution.py:15
  85.7 228.2 %while.13 = (s32[]{:T(128)}, f32[16,128,512]{2,0,1:T(8,128)}, s32[17]{0:T(128)S(1)}, s32[85]{0:T(128)}, s32[]{:T(128)}, /*index=5*/bf16[85,128,128]{2,1,0:T(8,12...) while((s32[]{:T(128)}, f32[16,128,512]{2,0,1:T(8,128)}, ...), condition=%wide.region_1.2_spmd.clone, body=%wide.region_0.1_spmd.clone.sunk | while | flops 148899120 | bytes 13144451 | solution.py:49
  93.2 4.5 select_add_fusion.2
  105.2 6.0 %select_add_fusion.2 = f32[16,128,512]{2,0,1:T(8,128)} fusion(f32[16,128,512]{2,0,1:T(8,128)} %get-tuple-element.214, f32[5,128,512]{2,1,0:T(8,128)S(1)} %fusion.25, pred[]{:T(512)S(6)} %compare.10, s32[5]{0:T(128)S(1)} %get-tuple-element.201, pred[5]{0:T(512)(128)(4,1)S(1)} %add_compare_fusion.2), kind=kOutput, calls=%fused_computation.2.clone.1 | convolution fusion | flops 65011872 | bytes 9699354 | tf_op jit(solution)/shard_map/while/body/eval_jaxpr/lj,lsu->jsu/dot_general | solution.py:40
  113.9 2.8 gather_fusion
  118.7 6.0 %select_add_fusion.2 = f32[16,128,512]{2,0,1:T(8,128)} fusion(f32[16,128,512]{2,0,1:T(8,128)} %get-tuple-element.214, f32[5,128,512]{2,1,0:T(8,128)S(1)} %fusion.25, pred[]{:T(512)S(6)} %compare.10, s32[5]{0:T(128)S(1)} %get-tuple-element.201, pred[5]{0:T(512)(128)(4,1)S(1)} %add_compare_fusion.2), kind=kOutput, calls=%fused_computation.2.clone.1 | convolution fusion | flops 65011872 | bytes 9699354 | tf_op jit(solution)/shard_map/while/body/eval_jaxpr/lj,lsu->jsu/dot_general | solution.py:40
  127.5 2.8 gather_fusion
  132.2 6.0 %select_add_fusion.2 = f32[16,128,512]{2,0,1:T(8,128)} fusion(f32[16,128,512]{2,0,1:T(8,128)} %get-tuple-element.214, f32[5,128,512]{2,1,0:T(8,128)S(1)} %fusion.25, pred[]{:T(512)S(6)} %compare.10, s32[5]{0:T(128)S(1)} %get-tuple-element.201, pred[5]{0:T(512)(128)(4,1)S(1)} %add_compare_fusion.2), kind=kOutput, calls=%fused_computation.2.clone.1 | convolution fusion | flops 65011872 | bytes 9699354 | tf_op jit(solution)/shard_map/while/body/eval_jaxpr/lj,lsu->jsu/dot_general | solution.py:40
  145.8 6.0 %select_add_fusion.2 = f32[16,128,512]{2,0,1:T(8,128)} fusion(f32[16,128,512]{2,0,1:T(8,128)} %get-tuple-element.214, f32[5,128,512]{2,1,0:T(8,128)S(1)} %fusion.25, pred[]{:T(512)S(6)} %compare.10, s32[5]{0:T(128)S(1)} %get-tuple-element.201, pred[5]{0:T(512)(128)(4,1)S(1)} %add_compare_fusion.2), kind=kOutput, calls=%fused_computation.2.clone.1 | convolution fusion | flops 65011872 | bytes 9699354 | tf_op jit(solution)/shard_map/while/body/eval_jaxpr/lj,lsu->jsu/dot_general | solution.py:40
  159.3 6.0 %select_add_fusion.2 = f32[16,128,512]{2,0,1:T(8,128)} fusion(f32[16,128,512]{2,0,1:T(8,128)} %get-tuple-element.214, f32[5,128,512]{2,1,0:T(8,128)S(1)} %fusion.25, pred[]{:T(512)S(6)} %compare.10, s32[5]{0:T(128)S(1)} %get-tuple-element.201, pred[5]{0:T(512)(128)(4,1)S(1)} %add_compare_fusion.2), kind=kOutput, calls=%fused_computation.2.clone.1 | convolution fusion | flops 65011872 | bytes 9699354 | tf_op jit(solution)/shard_map/while/body/eval_jaxpr/lj,lsu->jsu/dot_general | solution.py:40
  172.8 6.0 %select_add_fusion.2 = f32[16,128,512]{2,0,1:T(8,128)} fusion(f32[16,128,512]{2,0,1:T(8,128)} %get-tuple-element.214, f32[5,128,512]{2,1,0:T(8,128)S(1)} %fusion.25, pred[]{:T(512)S(6)} %compare.10, s32[5]{0:T(128)S(1)} %get-tuple-element.201, pred[5]{0:T(512)(128)(4,1)S(1)} %add_compare_fusion.2), kind=kOutput, calls=%fused_computation.2.clone.1 | convolution fusion | flops 65011872 | bytes 9699354 | tf_op jit(solution)/shard_map/while/body/eval_jaxpr/lj,lsu->jsu/dot_general | solution.py:40
  186.3 6.0 %select_add_fusion.2 = f32[16,128,512]{2,0,1:T(8,128)} fusion(f32[16,128,512]{2,0,1:T(8,128)} %get-tuple-element.214, f32[5,128,512]{2,1,0:T(8,128)S(1)} %fusion.25, pred[]{:T(512)S(6)} %compare.10, s32[5]{0:T(128)S(1)} %get-tuple-element.201, pred[5]{0:T(512)(128)(4,1)S(1)} %add_compare_fusion.2), kind=kOutput, calls=%fused_computation.2.clone.1 | convolution fusion | flops 65011872 | bytes 9699354 | tf_op jit(solution)/shard_map/while/body/eval_jaxpr/lj,lsu->jsu/dot_general | solution.py:40
  199.8 6.0 %select_add_fusion.2 = f32[16,128,512]{2,0,1:T(8,128)} fusion(f32[16,128,512]{2,0,1:T(8,128)} %get-tuple-element.214, f32[5,128,512]{2,1,0:T(8,128)S(1)} %fusion.25, pred[]{:T(512)S(6)} %compare.10, s32[5]{0:T(128)S(1)} %get-tuple-element.201, pred[5]{0:T(512)(128)(4,1)S(1)} %add_compare_fusion.2), kind=kOutput, calls=%fused_computation.2.clone.1 | convolution fusion | flops 65011872 | bytes 9699354 | tf_op jit(solution)/shard_map/while/body/eval_jaxpr/lj,lsu->jsu/dot_general | solution.py:40
  213.3 6.0 %select_add_fusion.2 = f32[16,128,512]{2,0,1:T(8,128)} fusion(f32[16,128,512]{2,0,1:T(8,128)} %get-tuple-element.214, f32[5,128,512]{2,1,0:T(8,128)S(1)} %fusion.25, pred[]{:T(512)S(6)} %compare.10, s32[5]{0:T(128)S(1)} %get-tuple-element.201, pred[5]{0:T(512)(128)(4,1)S(1)} %add_compare_fusion.2), kind=kOutput, calls=%fused_computation.2.clone.1 | convolution fusion | flops 65011872 | bytes 9699354 | tf_op jit(solution)/shard_map/while/body/eval_jaxpr/lj,lsu->jsu/dot_general | solution.py:40
  226.8 6.0 %select_add_fusion.2 = f32[16,128,512]{2,0,1:T(8,128)} fusion(f32[16,128,512]{2,0,1:T(8,128)} %get-tuple-element.214, f32[5,128,512]{2,1,0:T(8,128)S(1)} %fusion.25, pred[]{:T(512)S(6)} %compare.10, s32[5]{0:T(128)S(1)} %get-tuple-element.201, pred[5]{0:T(512)(128)(4,1)S(1)} %add_compare_fusion.2), kind=kOutput, calls=%fused_computation.2.clone.1 | convolution fusion | flops 65011872 | bytes 9699354 | tf_op jit(solution)/shard_map/while/body/eval_jaxpr/lj,lsu->jsu/dot_general | solution.py:40
  240.3 6.0 %select_add_fusion.2 = f32[16,128,512]{2,0,1:T(8,128)} fusion(f32[16,128,512]{2,0,1:T(8,128)} %get-tuple-element.214, f32[5,128,512]{2,1,0:T(8,128)S(1)} %fusion.25, pred[]{:T(512)S(6)} %compare.10, s32[5]{0:T(128)S(1)} %get-tuple-element.201, pred[5]{0:T(512)(128)(4,1)S(1)} %add_compare_fusion.2), kind=kOutput, calls=%fused_computation.2.clone.1 | convolution fusion | flops 65011872 | bytes 9699354 | tf_op jit(solution)/shard_map/while/body/eval_jaxpr/lj,lsu->jsu/dot_general | solution.py:40
  253.9 6.0 %select_add_fusion.2 = f32[16,128,512]{2,0,1:T(8,128)} fusion(f32[16,128,512]{2,0,1:T(8,128)} %get-tuple-element.214, f32[5,128,512]{2,1,0:T(8,128)S(1)} %fusion.25, pred[]{:T(512)S(6)} %compare.10, s32[5]{0:T(128)S(1)} %get-tuple-element.201, pred[5]{0:T(512)(128)(4,1)S(1)} %add_compare_fusion.2), kind=kOutput, calls=%fused_computation.2.clone.1 | convolution fusion | flops 65011872 | bytes 9699354 | tf_op jit(solution)/shard_map/while/body/eval_jaxpr/lj,lsu->jsu/dot_general | solution.py:40
  267.4 6.0 %select_add_fusion.2 = f32[16,128,512]{2,0,1:T(8,128)} fusion(f32[16,128,512]{2,0,1:T(8,128)} %get-tuple-element.214, f32[5,128,512]{2,1,0:T(8,128)S(1)} %fusion.25, pred[]{:T(512)S(6)} %compare.10, s32[5]{0:T(128)S(1)} %get-tuple-element.201, pred[5]{0:T(512)(128)(4,1)S(1)} %add_compare_fusion.2), kind=kOutput, calls=%fused_computation.2.clone.1 | convolution fusion | flops 65011872 | bytes 9699354 | tf_op jit(solution)/shard_map/while/body/eval_jaxpr/lj,lsu->jsu/dot_general | solution.py:40
  280.9 6.0 %select_add_fusion.2 = f32[16,128,512]{2,0,1:T(8,128)} fusion(f32[16,128,512]{2,0,1:T(8,128)} %get-tuple-element.214, f32[5,128,512]{2,1,0:T(8,128)S(1)} %fusion.25, pred[]{:T(512)S(6)} %compare.10, s32[5]{0:T(128)S(1)} %get-tuple-element.201, pred[5]{0:T(512)(128)(4,1)S(1)} %add_compare_fusion.2), kind=kOutput, calls=%fused_computation.2.clone.1 | convolution fusion | flops 65011872 | bytes 9699354 | tf_op jit(solution)/shard_map/while/body/eval_jaxpr/lj,lsu->jsu/dot_general | solution.py:40
  294.4 6.0 %select_add_fusion.2 = f32[16,128,512]{2,0,1:T(8,128)} fusion(f32[16,128,512]{2,0,1:T(8,128)} %get-tuple-element.214, f32[5,128,512]{2,1,0:T(8,128)S(1)} %fusion.25, pred[]{:T(512)S(6)} %compare.10, s32[5]{0:T(128)S(1)} %get-tuple-element.201, pred[5]{0:T(512)(128)(4,1)S(1)} %add_compare_fusion.2), kind=kOutput, calls=%fused_computation.2.clone.1 | convolution fusion | flops 65011872 | bytes 9699354 | tf_op jit(solution)/shard_map/while/body/eval_jaxpr/lj,lsu->jsu/dot_general | solution.py:40
  307.9 6.0 %select_add_fusion.2 = f32[16,128,512]{2,0,1:T(8,128)} fusion(f32[16,128,512]{2,0,1:T(8,128)} %get-tuple-element.214, f32[5,128,512]{2,1,0:T(8,128)S(1)} %fusion.25, pred[]{:T(512)S(6)} %compare.10, s32[5]{0:T(128)S(1)} %get-tuple-element.201, pred[5]{0:T(512)(128)(4,1)S(1)} %add_compare_fusion.2), kind=kOutput, calls=%fused_computation.2.clone.1 | convolution fusion | flops 65011872 | bytes 9699354 | tf_op jit(solution)/shard_map/while/body/eval_jaxpr/lj,lsu->jsu/dot_general | solution.py:40
  313.9 6.5 %copy.10 = f32[16,128,512]{2,1,0:T(8,128)} copy(f32[16,128,512]{2,0,1:T(8,128)} %get-tuple-element.107) | data formatting | bytes 8388608 | tf_op jit(solution)/shard_map/while | solution.py:49
  320.5 122.6 %psum.15 = f32[512]{0:T(512)S(1)} all-reduce(f32[512]{0:T(512)S(1)} %get-tuple-element.153), channel_id=1, replica_groups=mesh['row'=16,'col'=32] {'row','col'}, use_global_device_ids=true, to_apply=%region_5.6 | all-reduce | flops 512 | bytes 4096 | tf_op jit(solution)/shard_map/psum | solution.py:56
  443.7 67.7 %all-reduce.2.cloned.1.call-done = f32[512,512]{0,1:T(8,128)} async-done(((f32[512,512]{0,1:T(8,128)}), f32[512,512]{0,1:T(8,128)}) %all-reduce.2.cloned.1.call-update) | async-done | bytes 1048592 | tf_op jit(solution)/shard_map/psum | solution.py:56
  (135 shorter events, 119.3 us)
Async XLA Ops:
  8.0 1.2 copy-start
  8.0 77.7 %all-gather.2.cloned.1.call-start = ((), (), s32[]{:S(2)}) async-start(), calls=%async_computation.1 | async-start | bytes 4325376 | tf_op jit(solution)/shard_map/all_gather | solution.py:15
  10.2 501.3 %all-reduce.2.cloned.1.call-start = ((), (), s32[]{:S(2)}) async-start(), calls=%async_computation.3 | async-start | bytes 2097152 | tf_op jit(solution)/shard_map/psum | solution.py:56
  12.4 501.6 %reduce-scatter.2.cloned.1.call-start = ((), (), s32[]{:S(2)}) async-start(), calls=%async_computation.2 | async-start | bytes 4456448 | tf_op jit(solution)/shard_map/reduce_scatter | solution.py:51
Sparse Core Ops, SparseCore 0:
  11.6 74.1 all-gather.1
  320.6 151.5 reduce-scatter.1
Sparse Core Ops, SparseCore 1:
  17.6 493.8 all-reduce.1
where the time goes:
time: 525 us; the launch traced here: 523 us
  waiting for transfers between devices  141 us (27%)
  matrix products  126 us (24%)
  blocking collectives  123 us (23%)
  local copies, waits for them, and re-layouts  65 us (12%)
  other arithmetic  41 us (8%)
  between operations  15.5 us (3%)
  loops' own time  11.6 us (2%)
    psum x1, blocking collectives, body(): lax.psum((weight_terms, bias_terms), ('row', 'col'))  123 us
    dot_general x17, matrix products, add_group(): jnp.einsum('lj,lsu->jsu', insert_position.astype(jnp.float32), partial_pr...  101 us
    all_gather x1, waiting for transfers between devices, body(): row_block = lax.all_gather(projected, 'col', axis=0, tiled=True)  73.2 us
    psum x1, waiting for transfers between devices, body(): lax.psum((weight_terms, bias_terms), ('row', 'col'))  67.7 us
    gather x17, local copies, waits for them, and re-layouts, add_group(): selected_row_set = stacked_tiles[part_slots // tile_cols]  47.2 us
    dot_general x17, matrix products, add_group(): jnp.einsum('kab,kaf->kbf', part_blocks, selected_row_set, preferred_eleme...  22.1 us
    select_n x17, other arithmetic, add_group(): part_slots % tile_cols  12.6 us
    select_n x17, other arithmetic, add_group(): selected_row_set = stacked_tiles[part_slots // tile_cols]  12.5 us
  transfers between devices with their start and end apart: 3, of which 2 were waited for; matrix products, arithmetic and copies ran while one was open for 44% of the time, Pallas kernels for 0%

commit v1 on v0

v1 whole, which is shorter than its diff:
```python
import math

import jax
import jax.numpy as jnp
from jax import lax
from jax.experimental import pallas as pl
from jax.experimental.pallas import tpu as pltpu
from jax.sharding import Mesh, PartitionSpec as P

F32 = jnp.float32
BF16 = jnp.bfloat16
VMEM_LIMIT = 48 * 1024 * 1024


def split_terms(value):
    high = value.astype(BF16)
    low = (value - high.astype(F32)).astype(BF16)
    return high, low


def tile_kernel(pos_ref, live_ref, core_ref, blocks_ref, own_ref, other_ref, out_ref, acc_ref):
    n_zh = 4
    blk = blocks_ref.shape[-1]
    n_x = own_ref.shape[0]
    gathered = out_ref.shape[0]
    n_feat = own_ref.shape[-1]
    tile_cols = acc_ref.shape[0]
    n_rows = own_ref.shape[1] - (out_ref.shape[1] - n_zh * blk - 16) // 2
    acc_ref[...] = jnp.zeros_like(acc_ref)
    my_core = core_ref[0]

    def add_block(slot, carry):
        position = pos_ref[slot]
        source = position // tile_cols
        column = position % tile_cols
        z_part = source // (2 * n_x)
        x_part = (source // 2) % n_x
        mine = source % 2 == my_core
        first = pl.multiple_of(z_part * blk, blk)
        rows = jnp.where(mine, own_ref[x_part, pl.ds(first, blk), :], other_ref[x_part, pl.ds(first, blk), :])
        acc_ref[column] += lax.dot_general(
            blocks_ref[slot], rows, (((0,), (0,)), ((), ())), preferred_element_type=F32
        )
        return carry

    lax.fori_loop(0, live_ref[0], add_block, 0)

    n_slice = own_ref.shape[1] - n_rows
    weight_terms = jnp.zeros((n_slice, n_feat), F32)
    bias_terms = jnp.zeros((8, n_feat), F32)
    ones = jnp.ones((8, n_rows), BF16)
    for ref in (own_ref, other_ref):
        for x in range(n_x):
            rows = ref[x, :n_rows, :]
            weight_terms += jnp.dot(ref[x, n_rows:, :], rows, preferred_element_type=F32)
            bias_terms += jnp.dot(ones, rows, preferred_element_type=F32)
    terms = jnp.concatenate([weight_terms, bias_terms], axis=0)
    high, low = split_terms(terms)
    both = jnp.concatenate([high, low], axis=0)
    for y in range(gathered):
        for z in range(n_zh):
            out_ref[y, z * blk : (z + 1) * blk, :] = acc_ref[z * gathered + y].astype(BF16)
        out_ref[y, n_zh * blk :, :] = both


def fold_kernel(in_ref, out_ref):
    n_src = in_ref.shape[0]
    n_dst, width, _ = out_ref.shape
    n_terms = (in_ref.shape[1] - n_dst * (width - (in_ref.shape[1] - n_dst * 128))) // 2
    blk = width - 2 * n_terms
    for z in range(n_dst):
        total = in_ref[0, z * blk : (z + 1) * blk, :].astype(F32)
        for s in range(1, n_src):
            total += in_ref[s, z * blk : (z + 1) * blk, :].astype(F32)
        out_ref[z, :blk, :] = total.astype(BF16)
    base = n_dst * blk
    terms = jnp.zeros((n_terms, in_ref.shape[2]), F32)
    for s in range(n_src):
        terms += in_ref[s, base : base + n_terms, :].astype(F32) + in_ref[s, base + n_terms :, :].astype(F32)
    high, low = split_terms(terms)
    both = jnp.concatenate([high, low], axis=0)
    for z in range(n_dst):
        out_ref[z, blk:, :] = both


def last_kernel(in_ref, weight_ref, rows_ref, grad_ref, bias_ref, *, factor):
    n_src, width, _ = in_ref.shape
    blk = rows_ref.shape[0]
    n_terms = (width - blk) // 2
    total = in_ref[0, :blk, :].astype(F32)
    for s in range(1, n_src):
        total += in_ref[s, :blk, :].astype(F32)
    high, low = split_terms(total)
    dims = (((1,), (1,)), ((), ()))
    product = lax.dot_general(high, weight_ref[...], dims, preferred_element_type=F32)
    product += lax.dot_general(low, weight_ref[...], dims, preferred_element_type=F32)
    rows_ref[...] = product.astype(BF16)
    terms = jnp.zeros((n_terms, in_ref.shape[2]), F32)
    for s in range(n_src):
        terms += in_ref[s, blk : blk + n_terms, :].astype(F32) + in_ref[s, blk + n_terms :, :].astype(F32)
    terms = terms * factor
    n_slice = n_terms - 8
    slice_rows = terms[:n_slice].astype(BF16)
    for z in range(grad_ref.shape[0]):
        grad_ref[z] = slice_rows
    bias_ref[...] = terms[n_slice:]


def call(kernel, out_shape, scratch=(), n_scalar=0, n_in=1):
    smem = pl.BlockSpec(memory_space=pltpu.SMEM)
    vmem = pl.BlockSpec(memory_space=pltpu.VMEM)
    return pl.pallas_call(
        kernel,
        out_shape=out_shape,
        in_specs=[smem] * n_scalar + [vmem] * n_in,
        out_specs=jax.tree.map(lambda _: vmem, out_shape),
        scratch_shapes=list(scratch),
        compiler_params=pltpu.CompilerParams(vmem_limit_bytes=VMEM_LIMIT),
    )


def swap(value, axis):
    return lax.all_to_all(value, axis, split_axis=0, concat_axis=0, tiled=True)


def body(grad_out, relu_mask, aggregated, weight, adj_blocks, block_pos, block_live):
    blk, n_feat = grad_out.shape
    n_zh, n_y, n_zl, n_x, n_core = (lax.axis_size(a) for a in ("zh", "y", "zl", "x", "core"))
    n_rows = n_zl * blk
    n_slice = n_feat // (n_zl * n_x)
    n_terms = n_slice + 8
    grad_pre = grad_out * relu_mask.astype(BF16)
    columns = aggregated.T.reshape(n_zl, n_x, n_slice, blk).transpose(0, 2, 1, 3)
    columns = columns.reshape(n_zl, n_slice, n_x * blk)
    sent = jnp.concatenate([jnp.broadcast_to(grad_pre, (n_zl, blk, n_feat)), columns], axis=1)
    got = swap(sent, "zl")
    rows = got[:, :blk].reshape(n_rows, n_feat)
    columns = got[:, blk:].reshape(n_zl, n_slice, n_x, blk).transpose(2, 1, 0, 3)
    columns = columns.reshape(n_x, n_slice, n_rows)
    sent = jnp.concatenate([jnp.broadcast_to(rows, (n_x, n_rows, n_feat)), columns], axis=1)
    own = swap(sent, "x")
    other = lax.ppermute(own, "core", [(0, 1), (1, 0)])
    sent = call(
        tile_kernel,
        jax.ShapeDtypeStruct((n_y, n_zh * blk + 2 * n_terms, n_feat), BF16),
        scratch=[pltpu.VMEM((n_zh * n_y, blk, n_feat), F32)],
        n_scalar=3,
        n_in=3,
    )(
        block_pos.reshape(-1),
        block_live.reshape(-1),
        lax.axis_index("core").astype(jnp.int32).reshape(1),
        adj_blocks[0, 0],
        own,
        other,
    )
    got = swap(sent, "y")
    sent = call(fold_kernel, jax.ShapeDtypeStruct((n_zh, blk + 2 * n_terms, n_feat), BF16))(got)
    got = swap(sent, "zh")
    factor = 1.0 / math.sqrt(blk * n_zh * n_y * n_zl * n_x * n_core)

    def last(in_ref, weight_ref, rows_ref, grad_ref, bias_ref):
        last_kernel(in_ref, weight_ref, rows_ref, grad_ref, bias_ref, factor=factor)

    out_rows, part, bias = call(
        last,
        (
            jax.ShapeDtypeStruct((blk, n_feat), BF16),
            jax.ShapeDtypeStruct((n_zl, n_slice, n_feat), BF16),
            jax.ShapeDtypeStruct((8, n_feat), F32),
        ),
        n_in=2,
    )(got, weight)
    part = swap(part, "zl").reshape(n_rows // blk * n_slice, n_feat)
    part = swap(jnp.broadcast_to(part, (n_x,) + part.shape), "x")
    part = part.reshape(n_x, n_zl, n_slice, n_feat).transpose(1, 0, 2, 3)
    return out_rows[None], part.reshape(n_feat, n_feat).astype(F32), bias[0]


def solution(mesh):
    fine = Mesh(mesh.devices.reshape(4, 4, 4, 4, 2), ("zh", "y", "zl", "x", "core"))
    row, col = ("zh", "y"), ("zl", "x", "core")
    return jax.shard_map(
        body,
        mesh=fine,
        in_specs=(
            P(row + col, None),
            P(row + col, None),
            P(row + col, None),
            P(),
            P(row, col, None, None, None),
            P(row, col, None),
            P(row, col),
        ),
        out_specs=(P(col, row, None), P(), P()),
        check_vma=False,
    )
```

time: 525 us -> 193 us (0.37)
  waiting for transfers between devices: 141 us -> 9.82 us
  matrix products: 126 us -> 0 us
  local copies, waits for them, and re-layouts: 65 us -> 3.98 us
  other arithmetic: 41 us -> 1.36 us
  blocking collectives: 123 us -> 156 us
  between operations: 15.5 us -> 1.39 us
  loops' own time: 11.6 us -> 0 us
  starting transfers between devices: 0.12 us -> 10.9 us
  Pallas kernels: 0 us -> 7.35 us
    all_to_all x0 -> x5, blocking collectives: none -> 156 us  [swap(): return lax.all_to_all(value, axis, split_axis=0, concat_axis=0, tiled=True)]
    dot_general x36 -> x0, matrix products: 126 us -> none  [the longest x17 101 us: add_group(): jnp.einsum('lj,lsu->jsu', insert_position.astype(jnp.float32), partial_pr...]
    psum x1 -> x0, blocking collectives: 123 us -> none  [body(): lax.psum((weight_terms, bias_terms), ('row', 'col'))]
    all_gather x1 -> x0, waiting for transfers between devices: 73.2 us -> none  [body(): row_block = lax.all_gather(projected, 'col', axis=0, tiled=True)]
    psum x1 -> x0, waiting for transfers between devices: 67.7 us -> none  [body(): lax.psum((weight_terms, bias_terms), ('row', 'col'))]
    gather x17 -> x0, local copies, waits for them, and re-layouts: 47.2 us -> none  [add_group(): selected_row_set = stacked_tiles[part_slots // tile_cols]]
    select_n x34 -> x0, other arithmetic: 25.1 us -> none  [the longest x17 12.6 us: add_group(): part_slots % tile_cols]
    another operation x1 -> x0, loops' own time: 11.6 us -> none  [body(): lax.scan(add_group, start_sum, jnp.arange(group_turns, dtype=jnp.int32))]
  transfers between devices with their start and end apart: 3 -> 2, of which waited for: 2 -> 2; matrix products, arithmetic and copies ran while one was open for 44% -> 0% of each run, Pallas kernels for 0% -> 0%
where the time goes in v1:
time: 193 us; the launch traced here: 191 us
  blocking collectives  156 us (81%)
  starting transfers between devices  10.9 us (6%)
  waiting for transfers between devices  9.82 us (5%)
  Pallas kernels  7.35 us (4%)
  local copies, waits for them, and re-layouts  3.98 us (2%)
    all_to_all x5, blocking collectives, swap(): return lax.all_to_all(value, axis, split_axis=0, concat_axis=0, tiled=True)  156 us
    all_to_all x1, waiting for transfers between devices, swap(): return lax.all_to_all(value, axis, split_axis=0, concat_axis=0, tiled=True)  6.39 us
    pallas_call x1, Pallas kernels, body(): call(tile_kernel, jax.ShapeDtypeStruct((n_y, n_zh * blk + 2 * n_terms, n_...  5.91 us
    all_to_all x1, starting transfers between devices, swap(): return lax.all_to_all(value, axis, split_axis=0, concat_axis=0, tiled=True)  5.72 us
    ppermute x1, starting transfers between devices, body(): other = lax.ppermute(own, 'core', [(0, 1), (1, 0)])  5.2 us
  transfers between devices with their start and end apart: 2, of which 2 were waited for; matrix products, arithmetic and copies ran while one was open for 0% of the time, Pallas kernels for 0%

profile of v1, /device:TPU:1, one launch (start us, length us, event | category | flops | bytes accessed | tf_op | source)
XLA Modules:
  0.0 191.1 jit_solution(12760531722481374005)
XLA Ops:
  0.6 1.0 copy.13
  1.7 1.0 convert_multiply_fusion
  2.8 22.0 %all_to_all.30 = bf16[4,160,512]{2,1,0:T(8,128)(2,1)S(1)} all-to-all(bf16[4,160,512]{2,1,0:T(8,128)(2,1)S(1)} %pad_maximum_fusion.1), channel_id=1, replica_groups=mesh['zh'=4,'y'=4,'zl'=4,'x'=4,'core'=2] {'zl'}, dimensions={0} | all-to-all | bytes 1310720 | tf_op jit(solution)/shard_map/all_to_all | solution.py:123
  24.9 0.1 copy.15
  25.0 0.1 reshape.46
  25.1 0.2 broadcast_in_dim.13
  25.3 0.1 pad_maximum_fusion
  25.4 0.0 copy-start.1
  25.4 29.9 %all_to_all.31.own_ref = bf16[4,544,512]{2,1,0:T(8,128)(2,1)S(1)} all-to-all(bf16[4,544,512]{2,1,0:T(8,128)(2,1)S(1)} %pad_maximum_fusion), channel_id=1, replica_groups=mesh['zh'=4,'y'=4,'zl'=4,'x'=4,'core'=2] {'x'}, dimensions={0} | all-to-all | bytes 4456448 | tf_op jit(solution)/shard_map/all_to_all | solution.py:123
  55.3 5.2 %collective-permute-start = (bf16[4,544,512]{2,1,0:T(8,128)(2,1)S(1)}, bf16[4,544,512]{2,1,0:T(8,128)(2,1)}, u32[]{:S(2)}, u32[]{:S(2)}) collective-permute-start(bf16[4,544,512]{2,1,0:T(8,128)(2,1)S(1)} %all_to_all.31.own_ref), channel_id=1, source_target_pairs={{0,1},{1,0},{2,3},{3,2},{4,5},{5,4},{6,7},{7,6},{8,9},{9,8},{10,11... | collective-permute-start | bytes 6684680 | tf_op jit(solution)/shard_map/ppermute | solution.py:142
  61.2 3.4 %collective-permute-done.other_ref = bf16[4,544,512]{2,1,0:T(8,128)(2,1)} collective-permute-done((bf16[4,544,512]{2,1,0:T(8,128)(2,1)S(1)}, bf16[4,544,512]{2,1,0:T(8,128)(2,1)}, u32[]{:S(2)}, u32[]{:S(2)}) %collective-permute-start) | collective-permute-done | bytes 2228256 | tf_op jit(solution)/shard_map/ppermute | solution.py:142
  64.6 5.9 %shard_map.94 = bf16[4,592,512]{2,1,0:T(8,128)(2,1)} custom-call(s32[85]{0:T(128)S(1)} %bitcast.24, s32[1]{0:T(128)} %bitcast.23.live_ref, s32[1]{0:T(128)} %bitcast.2.core_ref, bf16[85,128,128]{2,1,0:T(8,128)(2,1)} %bitcast.25, bf16[4,544,512]{2,1,0:T(8,128)(2,1)S(1)} %all_to_all.31.own_ref, bf16[4,544,512]{2,1,0:T(8,128)(2,1)} %collective-permute-done.other_ref), custom_call_target="tpu_custom_call" | custom-call | tf_op jit(solution)/shard_map/pallas_call | solution.py:143
  70.5 47.3 %all_to_all.32.in_ref = bf16[4,592,512]{2,1,0:T(8,128)(2,1)S(1)} all-to-all(bf16[4,592,512]{2,1,0:T(8,128)(2,1)} %shard_map.94), channel_id=1, replica_groups=mesh['zh'=4,'y'=4,'zl'=4,'x'=4,'core'=2] {'y'}, dimensions={0} | all-to-all | bytes 4849664 | tf_op jit(solution)/shard_map/all_to_all | solution.py:123
  117.9 0.3 shard_map.95
  118.2 46.6 %all_to_all.33.in_ref = bf16[4,208,512]{2,1,0:T(8,128)(2,1)S(1)} all-to-all(bf16[4,208,512]{2,1,0:T(8,128)(2,1)S(1)} %shard_map.95), channel_id=1, replica_groups=mesh['zh'=4,'y'=4,'zl'=4,'x'=4,'core'=2] {'zh'}, dimensions={0} | all-to-all | bytes 1703936 | tf_op jit(solution)/shard_map/all_to_all | solution.py:123
  164.8 0.0 copy-done
  164.8 1.1 shard_map.96
  165.9 10.5 %all_to_all.34 = bf16[4,32,512]{2,1,0:T(8,128)(2,1)S(1)} all-to-all(bf16[4,32,512]{2,1,0:T(8,128)(2,1)S(1)} %get-tuple-element.7), channel_id=1, replica_groups=mesh['zh'=4,'y'=4,'zl'=4,'x'=4,'core'=2] {'zl'}, dimensions={0} | all-to-all | bytes 262144 | tf_op jit(solution)/shard_map/all_to_all | solution.py:123
  176.4 0.8 broadcast_in_dim.15
  177.2 5.7 %all-to-all-start.5 = ((bf16[4,128,512]{2,1,0:T(8,128)(2,1)}), bf16[4,128,512]{2,1,0:T(8,128)(2,1)S(1)}, u32[]{:S(2)}, u32[]{:S(2)}) async-start(bf16[4,128,512]{2,1,0:T(8,128)(2,1)} %broadcast_in_dim.15), calls=%async_computation.5 | async-start | bytes 1048576 | tf_op jit(solution)/shard_map/all_to_all | solution.py:123
  182.9 0.6 slice.11
  183.5 6.4 %all-to-all-done.5 = bf16[4,128,512]{2,1,0:T(8,128)(2,1)S(1)} async-done(((bf16[4,128,512]{2,1,0:T(8,128)(2,1)}), bf16[4,128,512]{2,1,0:T(8,128)(2,1)S(1)}, u32[]{:S(2)}, u32[]{:S(2)}) %all-to-all-start.5) | async-done | bytes 524320 | tf_op jit(solution)/shard_map/all_to_all | solution.py:123
  189.9 0.1 convert_bitcast_fusion
  190.0 1.1 copy.16
  (8 shorter events, 0.2 us)
Async XLA Ops:
  25.4 39.2 %copy-start.1 = (s32[1,1,85]{2,1,0:T(1,128)S(1)}, s32[1,1,85]{2,1,0:T(1,128)}, u32[]{:S(2)}) copy-start(s32[1,1,85]{2,1,0:T(1,128)} %param.12) | copy-start | bytes 1024
  55.3 9.3 %collective-permute-start = (bf16[4,544,512]{2,1,0:T(8,128)(2,1)S(1)}, bf16[4,544,512]{2,1,0:T(8,128)(2,1)}, u32[]{:S(2)}, u32[]{:S(2)}) collective-permute-start(bf16[4,544,512]{2,1,0:T(8,128)(2,1)S(1)} %all_to_all.31.own_ref), channel_id=1, source_target_pairs={{0,1},{1,0},{2,3},{3,2},{4,5},{5,4},{6,7},{7,6},{8,9},{9,8},{10,11... | collective-permute-start | bytes 6684680 | tf_op jit(solution)/shard_map/ppermute | solution.py:142
  117.9 46.9 %copy-start = (bf16[512,512]{1,0:T(8,128)(2,1)S(1)}, bf16[512,512]{1,0:T(8,128)(2,1)}, u32[]{:S(2)}) copy-start(bf16[512,512]{1,0:T(8,128)(2,1)} %weight_ref.1) | copy-start | bytes 1572868
  177.2 12.7 %all-to-all-start.5 = ((bf16[4,128,512]{2,1,0:T(8,128)(2,1)}), bf16[4,128,512]{2,1,0:T(8,128)(2,1)S(1)}, u32[]{:S(2)}, u32[]{:S(2)}) async-start(bf16[4,128,512]{2,1,0:T(8,128)(2,1)} %broadcast_in_dim.15), calls=%async_computation.5 | async-start | bytes 1048576 | tf_op jit(solution)/shard_map/all_to_all | solution.py:123

commit v2 on v1

v2 whole, which is shorter than its diff:
```python
import functools
import math

import jax
import jax.numpy as jnp
from jax import lax
from jax.experimental import pallas as pl
from jax.experimental.pallas import tpu as pltpu
from jax.sharding import Mesh, PartitionSpec as P

F32 = jnp.float32
BF16 = jnp.bfloat16
VMEM_LIMIT = 48 * 1024 * 1024


def tile_kernel(pos_ref, live_ref, core_ref, blocks_ref, own_ref, other_ref, out_ref, acc_ref, *, group, n_x):
    n_y, width, _ = out_ref.shape
    blk = blocks_ref.shape[-1]
    tile_cols = acc_ref.shape[0]
    acc_ref[...] = jnp.zeros_like(acc_ref)
    my_core = core_ref[0]
    live = live_ref[0]

    def add_group(turn, carry):
        found = []
        for k in range(group):
            slot = turn * group + k
            position = pos_ref[slot]
            source = position // tile_cols
            first = pl.multiple_of(source // (2 * n_x) * blk, blk)
            x_part = (source // 2) % n_x
            rows = jnp.where(
                source % 2 == my_core, own_ref[x_part, pl.ds(first, blk), :], other_ref[x_part, pl.ds(first, blk), :]
            )
            block = blocks_ref[slot]
            block = jnp.where(slot < live, block, jnp.zeros_like(block))
            product = lax.dot_general(block, rows, (((0,), (0,)), ((), ())), preferred_element_type=F32)
            found.append((position % tile_cols, product))
        for column, product in found:
            acc_ref[column] += product
        return carry

    lax.fori_loop(0, (live + group - 1) // group, add_group, 0)
    for y in range(n_y):
        for z in range(width // blk):
            out_ref[y, z * blk : (z + 1) * blk, :] = acc_ref[z * n_y + y].astype(BF16)


def terms_kernel(core_ref, own_ref, other_ref, out_ref, *, n_rows):
    n_x, _, n_feat = own_ref.shape
    n_slice = out_ref.shape[1] - 8
    first = pl.multiple_of(n_rows + core_ref[0] * n_slice, n_slice)
    weight_terms = jnp.zeros((n_slice, n_feat), F32)
    bias_terms = jnp.zeros((8, n_feat), F32)
    ones = jnp.ones((8, n_rows), BF16)
    for ref in (own_ref, other_ref):
        for x in range(n_x):
            rows = ref[x, :n_rows, :]
            weight_terms += jnp.dot(ref[x, pl.ds(first, n_slice), :], rows, preferred_element_type=F32)
            bias_terms += jnp.dot(ones, rows, preferred_element_type=F32)
    for y in range(out_ref.shape[0]):
        out_ref[y, :n_slice, :] = weight_terms
        out_ref[y, n_slice:, :] = bias_terms


def fold_kernel(in_ref, out_ref):
    total = in_ref[0].astype(F32)
    for s in range(1, in_ref.shape[0]):
        total += in_ref[s].astype(F32)
    out_ref[...] = total.astype(BF16)


def fold_terms_kernel(in_ref, out_ref):
    total = in_ref[0]
    for s in range(1, in_ref.shape[0]):
        total += in_ref[s]
    for z in range(out_ref.shape[0]):
        out_ref[z] = total


def last_kernel(in_ref, weight_ref, rows_ref):
    total = in_ref[0].astype(F32)
    for s in range(1, in_ref.shape[0]):
        total += in_ref[s].astype(F32)
    high = total.astype(BF16)
    low = (total - high.astype(F32)).astype(BF16)
    dims = (((1,), (1,)), ((), ()))
    product = lax.dot_general(high, weight_ref[...], dims, preferred_element_type=F32)
    product += lax.dot_general(low, weight_ref[...], dims, preferred_element_type=F32)
    rows_ref[...] = product.astype(BF16)


def call(kernel, out_shape, scratch=(), n_scalar=0, n_in=1):
    smem = pl.BlockSpec(memory_space=pltpu.SMEM)
    vmem = pl.BlockSpec(memory_space=pltpu.VMEM)
    return pl.pallas_call(
        kernel,
        out_shape=out_shape,
        in_specs=[smem] * n_scalar + [vmem] * n_in,
        out_specs=jax.tree.map(lambda _: vmem, out_shape),
        scratch_shapes=list(scratch),
        compiler_params=pltpu.CompilerParams(vmem_limit_bytes=VMEM_LIMIT),
    )


def swap(value, axis):
    return lax.all_to_all(value, axis, split_axis=0, concat_axis=0, tiled=True)


def body(grad_out, relu_mask, aggregated, weight, adj_blocks, block_pos, block_live):
    blk, n_feat = grad_out.shape
    n_zh, n_y, n_zl, n_x, n_core = (lax.axis_size(a) for a in ("zh", "y", "zl", "x", "core"))
    n_rows = n_zl * blk
    n_pair = n_feat // (n_zl * n_x)
    n_slice = n_pair // n_core
    n_terms = n_slice + 8
    grad_pre = grad_out * relu_mask.astype(BF16)
    columns = aggregated.T.reshape(n_zl, n_x, n_pair, blk).transpose(0, 2, 1, 3)
    columns = columns.reshape(n_zl, n_pair, n_x * blk)
    sent = jnp.concatenate([jnp.broadcast_to(grad_pre, (n_zl, blk, n_feat)), columns], axis=1)
    got = swap(sent, "zl")
    rows = got[:, :blk].reshape(n_rows, n_feat)
    columns = got[:, blk:].reshape(n_zl, n_pair, n_x, blk).transpose(2, 1, 0, 3)
    columns = columns.reshape(n_x, n_pair, n_rows)
    sent = jnp.concatenate([jnp.broadcast_to(rows, (n_x, n_rows, n_feat)), columns], axis=1)
    own = swap(sent, "x")
    other = lax.ppermute(own, "core", [(0, 1), (1, 0)])
    core = lax.axis_index("core").astype(jnp.int32).reshape(1)
    terms = call(
        functools.partial(terms_kernel, n_rows=n_rows),
        jax.ShapeDtypeStruct((n_y, n_terms, n_feat), F32),
        n_scalar=1,
        n_in=2,
    )(core, own, other)
    terms = swap(terms, "y")
    slots = adj_blocks.shape[2]
    group = max(d for d in range(1, 9) if slots % d == 0)
    sent = call(
        functools.partial(tile_kernel, group=group, n_x=n_x),
        jax.ShapeDtypeStruct((n_y, n_zh * blk, n_feat), BF16),
        scratch=[pltpu.VMEM((n_zh * n_y, blk, n_feat), F32)],
        n_scalar=3,
        n_in=3,
    )(block_pos.reshape(-1), block_live.reshape(-1), core, adj_blocks[0, 0], own, other)
    terms, sent = lax.optimization_barrier((terms, sent))
    terms = call(fold_terms_kernel, jax.ShapeDtypeStruct((n_zh, n_terms, n_feat), F32))(terms)
    terms = swap(terms, "zh").sum(axis=0)
    factor = 1.0 / math.sqrt(blk * n_zh * n_y * n_zl * n_x * n_core)
    terms = terms * factor
    terms, sent = lax.optimization_barrier((terms, sent))
    grad_weight = lax.all_gather(terms[:n_slice], ("zl", "x", "core"), axis=0, tiled=True)
    got = swap(sent, "y")
    sent = call(fold_kernel, jax.ShapeDtypeStruct((n_zh * blk, n_feat), BF16))(got)
    got = swap(sent.reshape(n_zh, blk, n_feat), "zh")
    out_rows = call(last_kernel, jax.ShapeDtypeStruct((blk, n_feat), BF16), n_in=2)(got, weight)
    return out_rows[None], grad_weight, terms[n_slice]


def solution(mesh):
    fine = Mesh(mesh.devices.reshape(4, 4, 4, 4, 2), ("zh", "y", "zl", "x", "core"))
    row, col = ("zh", "y"), ("zl", "x", "core")
    return jax.shard_map(
        body,
        mesh=fine,
        in_specs=(
            P(row + col, None),
            P(row + col, None),
            P(row + col, None),
            P(),
            P(row, col, None, None, None),
            P(row, col, None),
            P(row, col),
        ),
        out_specs=(P(col, row, None), P(), P()),
        check_vma=False,
    )
```

time: 193 us -> 210 us (1.088)
  blocking collectives: 156 us -> 79.4 us
  waiting for transfers between devices: 9.82 us -> 77.9 us
  between operations: 1.39 us -> 14.8 us
  starting transfers between devices: 10.9 us -> 20.4 us
  local copies, waits for them, and re-layouts: 3.98 us -> 6.28 us
    all_to_all x5 -> x3, blocking collectives: 156 us -> 79.4 us  [swap(): return lax.all_to_all(value, axis, split_axis=0, concat_axis=0, tiled=True)]
    all_gather x0 -> x1, waiting for transfers between devices: none -> 48.9 us  [body(): lax.all_gather(terms[:n_slice], ('zl', 'x', 'core'), axis=0, tiled=True)]
    all_to_all x1 -> x3, waiting for transfers between devices: 6.39 us -> 24.8 us  [swap(): return lax.all_to_all(value, axis, split_axis=0, concat_axis=0, tiled=True)]
    all_to_all x1 -> x3, starting transfers between devices: 5.72 us -> 15.2 us  [swap(): return lax.all_to_all(value, axis, split_axis=0, concat_axis=0, tiled=True)]
    unnamed x5 -> x8, local copies, waits for them, and re-layouts: 1.03 us -> 4.62 us
    pallas_call x3 -> x5, Pallas kernels: 7.35 us -> 9.02 us  [the longest x1 3.51 us: body(): call(functools.partial(terms_kernel, n_rows=n_rows), jax.ShapeDtypeStruct...]
  transfers between devices with their start and end apart: 2 -> 5, of which waited for: 2 -> 3; matrix products, arithmetic and copies ran while one was open for 0% -> 1% of each run, Pallas kernels for 0% -> 2%
where the time goes in v2:
time: 210 us; the launch traced here: 209 us
  blocking collectives  79.4 us (38%)
  waiting for transfers between devices  77.9 us (37%)
  starting transfers between devices  20.4 us (10%)
  between operations  14.8 us (7%)
  Pallas kernels  9.02 us (4%)
  local copies, waits for them, and re-layouts  6.28 us (3%)
    all_to_all x3, blocking collectives, swap(): return lax.all_to_all(value, axis, split_axis=0, concat_axis=0, tiled=True)  79.4 us
    all_gather x1, waiting for transfers between devices, body(): lax.all_gather(terms[:n_slice], ('zl', 'x', 'core'), axis=0, tiled=True)  48.9 us
    all_to_all x3, waiting for transfers between devices, swap(): return lax.all_to_all(value, axis, split_axis=0, concat_axis=0, tiled=True)  24.8 us
    all_to_all x3, starting transfers between devices, swap(): return lax.all_to_all(value, axis, split_axis=0, concat_axis=0, tiled=True)  15.2 us
    ppermute x1, starting transfers between devices, body(): other = lax.ppermute(own, 'core', [(0, 1), (1, 0)])  5.2 us
    unnamed x8, local copies, waits for them, and re-layouts  4.62 us
  transfers between devices with their start and end apart: 5, of which 3 were waited for; matrix products, arithmetic and copies ran while one was open for 1% of the time, Pallas kernels for 2%

profile of v2, /device:TPU:1, one launch (start us, length us, event | category | flops | bytes accessed | tf_op | source)
XLA Modules:
  0.0 209.1 jit_solution(15634972993135846953)
XLA Ops:
  7.2 1.0 copy.10
  8.2 1.0 convert_multiply_fusion
  9.4 22.0 %all_to_all.30 = bf16[4,160,512]{2,1,0:T(8,128)(2,1)S(1)} all-to-all(bf16[4,160,512]{2,1,0:T(8,128)(2,1)S(1)} %pad_maximum_fusion.1), channel_id=1, replica_groups=mesh['zh'=4,'y'=4,'zl'=4,'x'=4,'core'=2] {'zl'}, dimensions={0} | all-to-all | bytes 1310720 | tf_op jit(solution)/shard_map/all_to_all | solution.py:107
  31.4 0.1 copy.12
  31.6 0.2 broadcast_in_dim.10
  31.8 0.1 pad_maximum_fusion
  32.0 29.9 %all_to_all.31.own_ref = bf16[4,544,512]{2,1,0:T(8,128)(2,1)S(1)} all-to-all(bf16[4,544,512]{2,1,0:T(8,128)(2,1)S(1)} %pad_maximum_fusion), channel_id=1, replica_groups=mesh['zh'=4,'y'=4,'zl'=4,'x'=4,'core'=2] {'x'}, dimensions={0} | all-to-all | bytes 4456448 | tf_op jit(solution)/shard_map/all_to_all | solution.py:107
  61.9 5.2 %collective-permute-start = (bf16[4,544,512]{2,1,0:T(8,128)(2,1)S(1)}, bf16[4,544,512]{2,1,0:T(8,128)(2,1)}, u32[]{:S(2)}, u32[]{:S(2)}) collective-permute-start(bf16[4,544,512]{2,1,0:T(8,128)(2,1)S(1)} %all_to_all.31.own_ref), channel_id=1, source_target_pairs={{0,1},{1,0},{2,3},{3,2},{4,5},{5,4},{6,7},{7,6},{8,9},{9,8},{10,11... | collective-permute-start | bytes 6684680 | tf_op jit(solution)/shard_map/ppermute | solution.py:127
  67.1 4.1 %collective-permute-done.other_ref = bf16[4,544,512]{2,1,0:T(8,128)(2,1)} collective-permute-done((bf16[4,544,512]{2,1,0:T(8,128)(2,1)S(1)}, bf16[4,544,512]{2,1,0:T(8,128)(2,1)}, u32[]{:S(2)}, u32[]{:S(2)}) %collective-permute-start) | collective-permute-done | bytes 2228256 | tf_op jit(solution)/shard_map/ppermute | solution.py:127
  71.1 3.5 %shard_map.94 = f32[4,24,512]{2,1,0:T(8,128)} custom-call(s32[1]{0:T(128)} %bitcast.core_ref, bf16[4,544,512]{2,1,0:T(8,128)(2,1)S(1)} %all_to_all.31.own_ref, bf16[4,544,512]{2,1,0:T(8,128)(2,1)} %collective-permute-done.other_ref), custom_call_target="tpu_custom_call" | custom-call | tf_op jit(solution)/shard_map/pallas_call | solution.py:129
  74.7 4.2 %all-to-all-start.2 = ((f32[4,24,512]{2,1,0:T(8,128)}), f32[4,24,512]{2,1,0:T(8,128)S(1)}, u32[]{:S(2)}, u32[]{:S(2)}) async-start(f32[4,24,512]{2,1,0:T(8,128)} %shard_map.94), calls=%async_computation.2 | async-start | bytes 393216 | tf_op jit(solution)/shard_map/all_to_all | solution.py:107
  79.5 3.3 %shard_map.95 = bf16[4,512,512]{2,1,0:T(8,128)(2,1)S(1)} custom-call(s32[85]{0:T(128)S(1)} %bitcast.19, s32[1]{0:T(128)} %bitcast.18.live_ref, s32[1]{0:T(128)} %bitcast.core_ref, bf16[85,128,128]{2,1,0:T(8,128)(2,1)} %bitcast.20, bf16[4,544,512]{2,1,0:T(8,128)(2,1)S(1)} %all_to_all.31.own_ref, bf16[4,544,512]{2,1,0:T(8,128)(2,1)} %collective-permute-done.other_ref), custom_call_target="tpu_custom_call" | custom-call | tf_op jit(solution)/shard_map/pallas_call | solution.py:138
  82.8 1.3 copy-done
  84.2 27.5 %all_to_all.32 = f32[4,24,512]{2,1,0:T(8,128)S(1)} all-to-all(f32[4,24,512]{2,1,0:T(8,128)S(1)} %shard_map.96), channel_id=1, replica_groups=mesh['zh'=4,'y'=4,'zl'=4,'x'=4,'core'=2] {'zh'}, dimensions={0} | all-to-all | bytes 393216 | tf_op jit(solution)/shard_map/all_to_all | solution.py:107
  111.7 7.5 %all-to-all-start.4 = ((bf16[4,512,512]{2,1,0:T(8,128)(2,1)}), bf16[4,512,512]{2,1,0:T(8,128)(2,1)S(1)}, u32[]{:S(2)}, u32[]{:S(2)}) async-start(bf16[4,512,512]{2,1,0:T(8,128)(2,1)} %copy-done), calls=%async_computation.4 | async-start | bytes 4194304 | tf_op jit(solution)/shard_map/all_to_all | solution.py:107
  119.2 0.6 slice.14
  119.8 0.1 all-gather.2.cloned.1.call-update
  119.9 24.8 %all-to-all-done.4.in_ref = bf16[4,512,512]{2,1,0:T(8,128)(2,1)S(1)} async-done(((bf16[4,512,512]{2,1,0:T(8,128)(2,1)}), bf16[4,512,512]{2,1,0:T(8,128)(2,1)S(1)}, u32[]{:S(2)}, u32[]{:S(2)}) %all-to-all-start.4) | async-done | bytes 2097184 | tf_op jit(solution)/shard_map/all_to_all | solution.py:107
  144.8 1.0 shard_map.97
  145.8 3.5 %all-to-all-start.5 = ((bf16[4,128,512]{2,1,0:T(8,128)(2,1)}), bf16[4,128,512]{2,1,0:T(8,128)(2,1)S(1)}, u32[]{:S(2)}, u32[]{:S(2)}) async-start(bf16[4,128,512]{2,1,0:T(8,128)(2,1)} %bitcast.9), calls=%async_computation.5 | async-start | bytes 1048576 | tf_op jit(solution)/shard_map/all_to_all | solution.py:107
  149.3 0.6 slice.15
  149.9 48.9 %all-gather.2.cloned.1.call-done = f32[512,512]{1,0:T(8,128)} async-done(((f32[16,512]{1,0:T(8,128)}), f32[512,512]{1,0:T(8,128)}) %all-gather.2.cloned.1.call-update) | async-done | bytes 1048592 | tf_op jit(solution)/shard_map/all_gather | solution.py:151
  198.8 1.1 shard_map.98
  200.0 2.3 %copy.18 = f32[512,512]{1,0:T(8,128)} copy(f32[512,512]{1,0:T(8,128)} %all-gather.2.cloned.1.call-done) | data formatting | bytes 2097152
  (18 shorter events, 0.3 us)
Async XLA Ops:
  61.9 9.3 %collective-permute-start = (bf16[4,544,512]{2,1,0:T(8,128)(2,1)S(1)}, bf16[4,544,512]{2,1,0:T(8,128)(2,1)}, u32[]{:S(2)}, u32[]{:S(2)}) collective-permute-start(bf16[4,544,512]{2,1,0:T(8,128)(2,1)S(1)} %all_to_all.31.own_ref), channel_id=1, source_target_pairs={{0,1},{1,0},{2,3},{3,2},{4,5},{5,4},{6,7},{7,6},{8,9},{9,8},{10,11... | collective-permute-start | bytes 6684680 | tf_op jit(solution)/shard_map/ppermute | solution.py:127
  71.1 8.4 %copy-start.2 = (s32[1,1,85]{2,1,0:T(1,128)S(1)}, s32[1,1,85]{2,1,0:T(1,128)}, u32[]{:S(2)}) copy-start(s32[1,1,85]{2,1,0:T(1,128)} %param.12) | copy-start | bytes 1024
  74.7 9.5 %all-to-all-start.2 = ((f32[4,24,512]{2,1,0:T(8,128)}), f32[4,24,512]{2,1,0:T(8,128)S(1)}, u32[]{:S(2)}, u32[]{:S(2)}) async-start(f32[4,24,512]{2,1,0:T(8,128)} %shard_map.94), calls=%async_computation.2 | async-start | bytes 393216 | tf_op jit(solution)/shard_map/all_to_all | solution.py:107
  82.8 1.3 copy-start
  111.7 33.0 %all-to-all-start.4 = ((bf16[4,512,512]{2,1,0:T(8,128)(2,1)}), bf16[4,512,512]{2,1,0:T(8,128)(2,1)S(1)}, u32[]{:S(2)}, u32[]{:S(2)}) async-start(bf16[4,512,512]{2,1,0:T(8,128)(2,1)} %copy-done), calls=%async_computation.4 | async-start | bytes 4194304 | tf_op jit(solution)/shard_map/all_to_all | solution.py:107
  119.2 79.6 %copy-start.1 = (bf16[512,512]{1,0:T(8,128)(2,1)S(1)}, bf16[512,512]{1,0:T(8,128)(2,1)}, u32[]{:S(2)}) copy-start(bf16[512,512]{1,0:T(8,128)(2,1)} %weight_ref.1) | copy-start | bytes 1572868
  119.2 79.6 %all-gather.2.cloned.1.call-start = ((), (), s32[]{:S(2)}) async-start(), calls=%async_computation.6 | async-start | bytes 1081344 | tf_op jit(solution)/shard_map/all_gather | solution.py:151
  145.8 53.0 %all-to-all-start.5 = ((bf16[4,128,512]{2,1,0:T(8,128)(2,1)}), bf16[4,128,512]{2,1,0:T(8,128)(2,1)S(1)}, u32[]{:S(2)}, u32[]{:S(2)}) async-start(bf16[4,128,512]{2,1,0:T(8,128)(2,1)} %bitcast.9), calls=%async_computation.5 | async-start | bytes 1048576 | tf_op jit(solution)/shard_map/all_to_all | solution.py:107
Sparse Core Ops, SparseCore 0:
  122.8 76.0 all-gather.1

commit v3 on v2

--- a/solution.py
+++ b/solution.py
@@ -48,7 +48,7 @@
 
 def terms_kernel(core_ref, own_ref, other_ref, out_ref, *, n_rows):
     n_x, _, n_feat = own_ref.shape
-    n_slice = out_ref.shape[1] - 8
+    n_slice = out_ref.shape[0] - 8
     first = pl.multiple_of(n_rows + core_ref[0] * n_slice, n_slice)
     weight_terms = jnp.zeros((n_slice, n_feat), F32)
     bias_terms = jnp.zeros((8, n_feat), F32)
@@ -58,9 +58,8 @@
             rows = ref[x, :n_rows, :]
             weight_terms += jnp.dot(ref[x, pl.ds(first, n_slice), :], rows, preferred_element_type=F32)
             bias_terms += jnp.dot(ones, rows, preferred_element_type=F32)
-    for y in range(out_ref.shape[0]):
-        out_ref[y, :n_slice, :] = weight_terms
-        out_ref[y, n_slice:, :] = bias_terms
+    out_ref[:n_slice, :] = weight_terms
+    out_ref[n_slice:, :] = bias_terms
 
 
 def fold_kernel(in_ref, out_ref):
@@ -70,12 +69,15 @@
     out_ref[...] = total.astype(BF16)
 
 
-def fold_terms_kernel(in_ref, out_ref):
-    total = in_ref[0]
-    for s in range(1, in_ref.shape[0]):
-        total += in_ref[s]
-    for z in range(out_ref.shape[0]):
-        out_ref[z] = total
+def place_kernel(index_ref, *refs):
+    out_ref = refs[-1]
+    n_slice = refs[0].shape[0]
+    offset = 0
+    for ref in refs[:-1]:
+        for k in range(ref.shape[0] // n_slice):
+            first = pl.multiple_of((index_ref[0] ^ index_ref[1 + offset]) * n_slice, n_slice)
+            out_ref[pl.ds(first, n_slice), :] = ref[k * n_slice : (k + 1) * n_slice, :]
+            offset += 1
 
 
 def last_kernel(in_ref, weight_ref, rows_ref):
@@ -107,6 +109,10 @@
     return lax.all_to_all(value, axis, split_axis=0, concat_axis=0, tiled=True)
 
 
+def trade(value, axis, bit):
+    return lax.ppermute(value, axis, [(i, i ^ bit) for i in range(lax.axis_size(axis))])
+
+
 def body(grad_out, relu_mask, aggregated, weight, adj_blocks, block_pos, block_live):
     blk, n_feat = grad_out.shape
     n_zh, n_y, n_zl, n_x, n_core = (lax.axis_size(a) for a in ("zh", "y", "zl", "x", "core"))
@@ -126,13 +132,6 @@
     own = swap(sent, "x")
     other = lax.ppermute(own, "core", [(0, 1), (1, 0)])
     core = lax.axis_index("core").astype(jnp.int32).reshape(1)
-    terms = call(
-        functools.partial(terms_kernel, n_rows=n_rows),
-        jax.ShapeDtypeStruct((n_y, n_terms, n_feat), F32),
-        n_scalar=1,
-        n_in=2,
-    )(core, own, other)
-    terms = swap(terms, "y")
     slots = adj_blocks.shape[2]
     group = max(d for d in range(1, 9) if slots % d == 0)
     sent = call(
@@ -142,13 +141,33 @@
         n_scalar=3,
         n_in=3,
     )(block_pos.reshape(-1), block_live.reshape(-1), core, adj_blocks[0, 0], own, other)
-    terms, sent = lax.optimization_barrier((terms, sent))
-    terms = call(fold_terms_kernel, jax.ShapeDtypeStruct((n_zh, n_terms, n_feat), F32))(terms)
-    terms = swap(terms, "zh").sum(axis=0)
+    own, other, sent = lax.optimization_barrier((own, other, sent))
+    terms = call(
+        functools.partial(terms_kernel, n_rows=n_rows),
+        jax.ShapeDtypeStruct((n_terms, n_feat), F32),
+        n_scalar=1,
+        n_in=2,
+    )(core, own, other)
+    for axis in ("y", "zh"):
+        for bit in (1, 2):
+            terms = terms + trade(terms, axis, bit)
     factor = 1.0 / math.sqrt(blk * n_zh * n_y * n_zl * n_x * n_core)
     terms = terms * factor
-    terms, sent = lax.optimization_barrier((terms, sent))
-    grad_weight = lax.all_gather(terms[:n_slice], ("zl", "x", "core"), axis=0, tiled=True)
+    pieces = [terms[:n_slice]]
+    offsets = [0]
+    for axis, bit, stride in (
+        ("zl", 1, n_x * n_core),
+        ("zl", 2, n_x * n_core),
+        ("x", 1, n_core),
+        ("x", 2, n_core),
+        ("core", 1, 1),
+    ):
+        pieces.append(trade(jnp.concatenate(pieces, axis=0), axis, bit))
+        offsets += [o ^ (bit * stride) for o in offsets]
+    place = lax.axis_index(("zl", "x", "core")).astype(jnp.int32)
+    grad_weight = call(place_kernel, jax.ShapeDtypeStruct((n_feat, n_feat), F32), n_scalar=1, n_in=len(pieces))(
+        jnp.concatenate([place.reshape(1), jnp.array(offsets, jnp.int32)]), *pieces
+    )
     got = swap(sent, "y")
     sent = call(fold_kernel, jax.ShapeDtypeStruct((n_zh * blk, n_feat), BF16))(got)
     got = swap(sent.reshape(n_zh, blk, n_feat), "zh")

time: 210 us -> 204 us (0.971)
  starting transfers between devices: 20.4 us -> 61.6 us
  blocking collectives: 79.4 us -> 51.9 us
  between operations: 14.8 us -> 1.55 us
  waiting for transfers between devices: 77.9 us -> 70.1 us
  Pallas kernels: 9.02 us -> 11.9 us
  local copies, waits for them, and re-layouts: 6.28 us -> 3.48 us
    ppermute x0 -> x9, waiting for transfers between devices: none -> 66.6 us  [trade(): lax.ppermute(value, axis, [(i, i ^ bit) for i in range(lax.axis_size(axis...]
    all_gather x1 -> x0, waiting for transfers between devices: 48.9 us -> none  [body(): lax.all_gather(terms[:n_slice], ('zl', 'x', 'core'), axis=0, tiled=True)]
    ppermute x0 -> x9, starting transfers between devices: none -> 37.6 us  [trade(): lax.ppermute(value, axis, [(i, i ^ bit) for i in range(lax.axis_size(axis...]
    all_to_all x3 -> x2, blocking collectives: 79.4 us -> 51.9 us  [swap(): return lax.all_to_all(value, axis, split_axis=0, concat_axis=0, tiled=True)]
    all_to_all x3 -> x2, waiting for transfers between devices: 24.8 us -> 0.01 us  [swap(): return lax.all_to_all(value, axis, split_axis=0, concat_axis=0, tiled=True)]
    all_to_all x3 -> x2, starting transfers between devices: 15.2 us -> 18.8 us  [swap(): return lax.all_to_all(value, axis, split_axis=0, concat_axis=0, tiled=True)]
    unnamed x8 -> x13, local copies, waits for them, and re-layouts: 4.62 us -> 2.42 us
  transfers between devices with their start and end apart: 5 -> 12, of which waited for: 3 -> 10; matrix products, arithmetic and copies ran while one was open for 1% -> 0% of each run, Pallas kernels for 2% -> 2%
where the time goes in v3:
time: 204 us; the launch traced here: 202 us
  waiting for transfers between devices  70.1 us (34%)
  starting transfers between devices  61.6 us (30%)
  blocking collectives  51.9 us (25%)
  Pallas kernels  11.9 us (6%)
  local copies, waits for them, and re-layouts  3.48 us (2%)
    ppermute x9, waiting for transfers between devices, trade(): lax.ppermute(value, axis, [(i, i ^ bit) for i in range(lax.axis_size(axis...  66.6 us
    all_to_all x2, blocking collectives, swap(): return lax.all_to_all(value, axis, split_axis=0, concat_axis=0, tiled=True)  51.9 us
    ppermute x9, starting transfers between devices, trade(): lax.ppermute(value, axis, [(i, i ^ bit) for i in range(lax.axis_size(axis...  37.6 us
    all_to_all x2, starting transfers between devices, swap(): return lax.all_to_all(value, axis, split_axis=0, concat_axis=0, tiled=True)  18.8 us
    ppermute x1, starting transfers between devices, body(): other = lax.ppermute(own, 'core', [(0, 1), (1, 0)])  5.2 us
  transfers between devices with their start and end apart: 12, of which 10 were waited for; matrix products, arithmetic and copies ran while one was open for 0% of the time, Pallas kernels for 2%

profile of v3, /device:TPU:1, one launch (start us, length us, event | category | flops | bytes accessed | tf_op | source)
XLA Modules:
  0.0 201.8 jit_solution(553136862484732853)
XLA Ops:
  2.8 22.0 %all_to_all.20 = bf16[4,160,512]{2,1,0:T(8,128)(2,1)S(1)} all-to-all(bf16[4,160,512]{2,1,0:T(8,128)(2,1)S(1)} %pad_maximum_fusion.1), channel_id=1, replica_groups=mesh['zh'=4,'y'=4,'zl'=4,'x'=4,'core'=2] {'zl'}, dimensions={0} | all-to-all | bytes 1310720 | tf_op jit(solution)/shard_map/all_to_all | solution.py:109
  25.4 29.9 %all_to_all.21.own_ref = bf16[4,544,512]{2,1,0:T(8,128)(2,1)S(1)} all-to-all(bf16[4,544,512]{2,1,0:T(8,128)(2,1)S(1)} %pad_maximum_fusion), channel_id=1, replica_groups=mesh['zh'=4,'y'=4,'zl'=4,'x'=4,'core'=2] {'x'}, dimensions={0} | all-to-all | bytes 4456448 | tf_op jit(solution)/shard_map/all_to_all | solution.py:109
  55.3 5.2 %collective-permute-start = (bf16[4,544,512]{2,1,0:T(8,128)(2,1)S(1)}, bf16[4,544,512]{2,1,0:T(8,128)(2,1)}, u32[]{:S(2)}, u32[]{:S(2)}) collective-permute-start(bf16[4,544,512]{2,1,0:T(8,128)(2,1)S(1)} %all_to_all.21.own_ref), channel_id=1, source_target_pairs={{0,1},{1,0},{2,3},{3,2},{4,5},{5,4},{6,7},{7,6},{8,9},{9,8},{10,11... | collective-permute-start | bytes 6684680 | tf_op jit(solution)/shard_map/ppermute | solution.py:133
  61.2 3.4 %collective-permute-done.other_ref = bf16[4,544,512]{2,1,0:T(8,128)(2,1)} collective-permute-done((bf16[4,544,512]{2,1,0:T(8,128)(2,1)S(1)}, bf16[4,544,512]{2,1,0:T(8,128)(2,1)}, u32[]{:S(2)}, u32[]{:S(2)}) %collective-permute-start) | collective-permute-done | bytes 2228256 | tf_op jit(solution)/shard_map/ppermute | solution.py:133
  64.6 3.7 %shard_map.103 = bf16[4,512,512]{2,1,0:T(8,128)(2,1)S(1)} custom-call(s32[85]{0:T(128)S(1)} %bitcast.20, s32[1]{0:T(128)} %bitcast.19.live_ref, s32[1]{0:T(128)} %bitcast.7.core_ref, bf16[85,128,128]{2,1,0:T(8,128)(2,1)} %bitcast.21, bf16[4,544,512]{2,1,0:T(8,128)(2,1)S(1)} %all_to_all.21.own_ref, bf16[4,544,512]{2,1,0:T(8,128)(2,1)} %collective-permute-done.other_ref), custom_call_target="tpu_custom_call" | custom-call | tf_op jit(solution)/shard_map/pallas_call | solution.py:137
  69.7 5.9 %all-to-all-start.2 = ((bf16[4,512,512]{2,1,0:T(8,128)(2,1)}), bf16[4,512,512]{2,1,0:T(8,128)(2,1)}, u32[]{:S(2)}, u32[]{:S(2)}) async-start(bf16[4,512,512]{2,1,0:T(8,128)(2,1)} %copy-done), calls=%async_computation.2 | async-start | bytes 4194304 | tf_op jit(solution)/shard_map/all_to_all | solution.py:109
  75.6 2.8 %shard_map.106 = f32[24,512]{1,0:T(8,128)S(1)} custom-call(s32[1]{0:T(128)} %bitcast.7.core_ref, bf16[4,544,512]{2,1,0:T(8,128)(2,1)S(1)} %all_to_all.21.own_ref, bf16[4,544,512]{2,1,0:T(8,128)(2,1)} %collective-permute-done.other_ref), custom_call_target="tpu_custom_call" | custom-call | tf_op jit(solution)/shard_map/pallas_call | solution.py:145
  78.4 5.1 %collective-permute-start.1 = (f32[24,512]{1,0:T(8,128)S(1)}, f32[24,512]{1,0:T(8,128)S(1)}, u32[]{:S(2)}, u32[]{:S(2)}) collective-permute-start(f32[24,512]{1,0:T(8,128)S(1)} %shard_map.106), channel_id=1, source_target_pairs={{0,32},{32,0},{64,96},{96,64},{1,33},{33,1},{65,97},{97,65},{2,34}... | collective-permute-start | bytes 147464 | tf_op jit(solution)/shard_map/ppermute | solution.py:113
  83.5 18.2 %collective-permute-done.1 = f32[24,512]{1,0:T(8,128)S(1)} collective-permute-done((f32[24,512]{1,0:T(8,128)S(1)}, f32[24,512]{1,0:T(8,128)S(1)}, u32[]{:S(2)}, u32[]{:S(2)}) %collective-permute-start.1) | collective-permute-done | bytes 49184 | tf_op jit(solution)/shard_map/ppermute | solution.py:113
  101.7 3.9 %collective-permute-start.2 = (f32[24,512]{1,0:T(8,128)S(1)}, f32[24,512]{1,0:T(8,128)S(1)}, u32[]{:S(2)}, u32[]{:S(2)}) collective-permute-start(f32[24,512]{1,0:T(8,128)S(1)} %add.20), channel_id=1, source_target_pairs={{0,64},{32,96},{64,0},{96,32},{1,65},{33,97},{65,1},{97,33},{2,66}... | collective-permute-start | bytes 147464 | tf_op jit(solution)/shard_map/ppermute | solution.py:113
  105.7 2.5 %collective-permute-done.2 = f32[24,512]{1,0:T(8,128)S(1)} collective-permute-done((f32[24,512]{1,0:T(8,128)S(1)}, f32[24,512]{1,0:T(8,128)S(1)}, u32[]{:S(2)}, u32[]{:S(2)}) %collective-permute-start.2) | collective-permute-done | bytes 49184 | tf_op jit(solution)/shard_map/ppermute | solution.py:113
  108.2 2.6 %collective-permute-start.3 = (f32[24,512]{1,0:T(8,128)S(1)}, f32[24,512]{1,0:T(8,128)S(1)}, u32[]{:S(2)}, u32[]{:S(2)}) collective-permute-start(f32[24,512]{1,0:T(8,128)S(1)} %add.21), channel_id=1, source_target_pairs={{0,128},{128,0},{256,384},{384,256},{1,129},{129,1},{257,385},{385... | collective-permute-start | bytes 147464 | tf_op jit(solution)/shard_map/ppermute | solution.py:113
  110.8 6.1 %collective-permute-done.3 = f32[24,512]{1,0:T(8,128)S(1)} collective-permute-done((f32[24,512]{1,0:T(8,128)S(1)}, f32[24,512]{1,0:T(8,128)S(1)}, u32[]{:S(2)}, u32[]{:S(2)}) %collective-permute-start.3) | collective-permute-done | bytes 49184 | tf_op jit(solution)/shard_map/ppermute | solution.py:113
  117.0 12.3 %collective-permute-start.4 = (f32[24,512]{1,0:T(8,128)S(1)}, f32[24,512]{1,0:T(8,128)S(1)}, u32[]{:S(2)}, u32[]{:S(2)}) collective-permute-start(f32[24,512]{1,0:T(8,128)S(1)} %add.22), channel_id=1, source_target_pairs={{0,256},{128,384},{256,0},{384,128},{1,257},{129,385},{257,1},{385... | collective-permute-start | bytes 147464 | tf_op jit(solution)/shard_map/ppermute | solution.py:113
  130.8 2.7 %shard_map.104 = bf16[512,512]{1,0:T(8,128)(2,1)} custom-call(bf16[4,512,512]{2,1,0:T(8,128)(2,1)} %all-to-all-done.2.in_ref), custom_call_target="tpu_custom_call" | custom-call | tf_op jit(solution)/shard_map/pallas_call | solution.py:172
  133.4 12.9 %all-to-all-start.3 = ((bf16[4,128,512]{2,1,0:T(8,128)(2,1)}), bf16[4,128,512]{2,1,0:T(8,128)(2,1)S(1)}, u32[]{:S(2)}, u32[]{:S(2)}) async-start(bf16[4,128,512]{2,1,0:T(8,128)(2,1)} %bitcast.9), calls=%async_computation.3 | async-start | bytes 1048576 | tf_op jit(solution)/shard_map/all_to_all | solution.py:109
  146.3 3.8 %collective-permute-start.5 = (f32[16,512]{1,0:T(8,128)S(1)}, f32[16,512]{1,0:T(8,128)S(1)}, u32[]{:S(2)}, u32[]{:S(2)}) collective-permute-start(f32[16,512]{1,0:T(8,128)S(1)} %get-tuple-element.10.refs_0_), channel_id=1, source_target_pairs={{0,8},{8,0},{16,24},{24,16},{1,9},{9,1},{17,25},{25,17},{2,10},{10... | collective-permute-start | bytes 98312 | tf_op jit(solution)/shard_map/ppermute | solution.py:113
  150.1 14.6 %collective-permute-done.5.refs_1_ = f32[16,512]{1,0:T(8,128)S(1)} collective-permute-done((f32[16,512]{1,0:T(8,128)S(1)}, f32[16,512]{1,0:T(8,128)S(1)}, u32[]{:S(2)}, u32[]{:S(2)}) %collective-permute-start.5) | collective-permute-done | bytes 32800 | tf_op jit(solution)/shard_map/ppermute | solution.py:113
  166.7 10.4 %collective-permute-done.6.refs_2_ = f32[32,512]{1,0:T(8,128)S(1)} collective-permute-done((f32[32,512]{1,0:T(8,128)S(1)}, f32[32,512]{1,0:T(8,128)S(1)}, u32[]{:S(2)}, u32[]{:S(2)}) %collective-permute-start.6) | collective-permute-done | bytes 65568 | tf_op jit(solution)/shard_map/ppermute | solution.py:113
  177.0 1.9 collective-permute-start.7
  179.0 4.5 %collective-permute-done.7.refs_3_ = f32[64,512]{1,0:T(8,128)S(1)} collective-permute-done((f32[64,512]{1,0:T(8,128)S(1)}, f32[64,512]{1,0:T(8,128)S(1)}, u32[]{:S(2)}, u32[]{:S(2)}) %collective-permute-start.7) | collective-permute-done | bytes 131104 | tf_op jit(solution)/shard_map/ppermute | solution.py:113
  183.5 1.9 collective-permute-start.8
  185.5 7.9 %collective-permute-done.8.refs_4_ = f32[128,512]{1,0:T(8,128)S(1)} collective-permute-done((f32[128,512]{1,0:T(8,128)S(1)}, f32[128,512]{1,0:T(8,128)S(1)}, u32[]{:S(2)}, u32[]{:S(2)}) %collective-permute-start.8) | collective-permute-done | bytes 262176 | tf_op jit(solution)/shard_map/ppermute | solution.py:113
  193.4 4.2 %collective-permute-start.9 = (f32[256,512]{1,0:T(8,128)S(1)}, f32[256,512]{1,0:T(8,128)S(1)}, u32[]{:S(2)}, u32[]{:S(2)}) collective-permute-start(f32[256,512]{1,0:T(8,128)S(1)} %constant_dynamic-update-slice_fusion), channel_id=1, source_target_pairs={{0,1},{1,0},{2,3},{3,2},{4,5},{5,4},{6,7},{7,6},{8,9},{9,8},{10,11... | collective-permute-start | bytes 1572872 | tf_op jit(solution)/shard_map/ppermute | solution.py:113
  (41 shorter events, 11.8 us)
Async XLA Ops:
  25.4 39.2 %copy-start.2 = (s32[1,1,85]{2,1,0:T(1,128)S(1)}, s32[1,1,85]{2,1,0:T(1,128)}, u32[]{:S(2)}) copy-start(s32[1,1,85]{2,1,0:T(1,128)} %param.13) | copy-start | bytes 1024
  55.3 9.3 %collective-permute-start = (bf16[4,544,512]{2,1,0:T(8,128)(2,1)S(1)}, bf16[4,544,512]{2,1,0:T(8,128)(2,1)}, u32[]{:S(2)}, u32[]{:S(2)}) collective-permute-start(bf16[4,544,512]{2,1,0:T(8,128)(2,1)S(1)} %all_to_all.21.own_ref), channel_id=1, source_target_pairs={{0,1},{1,0},{2,3},{3,2},{4,5},{5,4},{6,7},{7,6},{8,9},{9,8},{10,11... | collective-permute-start | bytes 6684680 | tf_op jit(solution)/shard_map/ppermute | solution.py:133
  68.3 1.4 copy-start
  69.7 61.1 %all-to-all-start.2 = ((bf16[4,512,512]{2,1,0:T(8,128)(2,1)}), bf16[4,512,512]{2,1,0:T(8,128)(2,1)}, u32[]{:S(2)}, u32[]{:S(2)}) async-start(bf16[4,512,512]{2,1,0:T(8,128)(2,1)} %copy-done), calls=%async_computation.2 | async-start | bytes 4194304 | tf_op jit(solution)/shard_map/all_to_all | solution.py:109
  78.4 23.3 %collective-permute-start.1 = (f32[24,512]{1,0:T(8,128)S(1)}, f32[24,512]{1,0:T(8,128)S(1)}, u32[]{:S(2)}, u32[]{:S(2)}) collective-permute-start(f32[24,512]{1,0:T(8,128)S(1)} %shard_map.106), channel_id=1, source_target_pairs={{0,32},{32,0},{64,96},{96,64},{1,33},{33,1},{65,97},{97,65},{2,34}... | collective-permute-start | bytes 147464 | tf_op jit(solution)/shard_map/ppermute | solution.py:113
  101.7 6.5 %collective-permute-start.2 = (f32[24,512]{1,0:T(8,128)S(1)}, f32[24,512]{1,0:T(8,128)S(1)}, u32[]{:S(2)}, u32[]{:S(2)}) collective-permute-start(f32[24,512]{1,0:T(8,128)S(1)} %add.20), channel_id=1, source_target_pairs={{0,64},{32,96},{64,0},{96,32},{1,65},{33,97},{65,1},{97,33},{2,66}... | collective-permute-start | bytes 147464 | tf_op jit(solution)/shard_map/ppermute | solution.py:113
  108.2 8.7 %collective-permute-start.3 = (f32[24,512]{1,0:T(8,128)S(1)}, f32[24,512]{1,0:T(8,128)S(1)}, u32[]{:S(2)}, u32[]{:S(2)}) collective-permute-start(f32[24,512]{1,0:T(8,128)S(1)} %add.21), channel_id=1, source_target_pairs={{0,128},{128,0},{256,384},{384,256},{1,129},{129,1},{257,385},{385... | collective-permute-start | bytes 147464 | tf_op jit(solution)/shard_map/ppermute | solution.py:113
  117.0 13.8 %collective-permute-start.4 = (f32[24,512]{1,0:T(8,128)S(1)}, f32[24,512]{1,0:T(8,128)S(1)}, u32[]{:S(2)}, u32[]{:S(2)}) collective-permute-start(f32[24,512]{1,0:T(8,128)S(1)} %add.22), channel_id=1, source_target_pairs={{0,256},{128,384},{256,0},{384,128},{1,257},{129,385},{257,1},{385... | collective-permute-start | bytes 147464 | tf_op jit(solution)/shard_map/ppermute | solution.py:113
  130.7 66.9 %copy-start.3 = (s32[32]{0:T(128)S(1)}, s32[32]{0:T(128)}, u32[]{:S(2)}) copy-start(s32[32]{0:T(128)} %constant.19.clone) | copy-start | bytes 388
  133.4 67.3 %all-to-all-start.3 = ((bf16[4,128,512]{2,1,0:T(8,128)(2,1)}), bf16[4,128,512]{2,1,0:T(8,128)(2,1)S(1)}, u32[]{:S(2)}, u32[]{:S(2)}) async-start(bf16[4,128,512]{2,1,0:T(8,128)(2,1)} %bitcast.9), calls=%async_computation.3 | async-start | bytes 1048576 | tf_op jit(solution)/shard_map/all_to_all | solution.py:109
  146.3 54.4 %copy-start.1 = (bf16[512,512]{1,0:T(8,128)(2,1)S(1)}, bf16[512,512]{1,0:T(8,128)(2,1)}, u32[]{:S(2)}) copy-start(bf16[512,512]{1,0:T(8,128)(2,1)} %weight_ref.1) | copy-start | bytes 1572868
  146.3 18.4 %collective-permute-start.5 = (f32[16,512]{1,0:T(8,128)S(1)}, f32[16,512]{1,0:T(8,128)S(1)}, u32[]{:S(2)}, u32[]{:S(2)}) collective-permute-start(f32[16,512]{1,0:T(8,128)S(1)} %get-tuple-element.10.refs_0_), channel_id=1, source_target_pairs={{0,8},{8,0},{16,24},{24,16},{1,9},{9,1},{17,25},{25,17},{2,10},{10... | collective-permute-start | bytes 98312 | tf_op jit(solution)/shard_map/ppermute | solution.py:113
  164.7 12.3 %collective-permute-start.6 = (f32[32,512]{1,0:T(8,128)S(1)}, f32[32,512]{1,0:T(8,128)S(1)}, u32[]{:S(2)}, u32[]{:S(2)}) collective-permute-start(f32[32,512]{1,0:T(8,128)S(1)} %pad_maximum_fusion.4), channel_id=1, source_target_pairs={{0,16},{8,24},{16,0},{24,8},{1,17},{9,25},{17,1},{25,9},{2,18},{10... | collective-permute-start | bytes 196616 | tf_op jit(solution)/shard_map/ppermute | solution.py:113
  177.0 6.5 %collective-permute-start.7 = (f32[64,512]{1,0:T(8,128)S(1)}, f32[64,512]{1,0:T(8,128)S(1)}, u32[]{:S(2)}, u32[]{:S(2)}) collective-permute-start(f32[64,512]{1,0:T(8,128)S(1)} %pad_maximum_fusion.3), channel_id=1, source_target_pairs={{0,2},{2,0},{4,6},{6,4},{1,3},{3,1},{5,7},{7,5},{8,10},{10,8},{12,... | collective-permute-start | bytes 393224 | tf_op jit(solution)/shard_map/ppermute | solution.py:113
  183.5 9.9 %collective-permute-start.8 = (f32[128,512]{1,0:T(8,128)S(1)}, f32[128,512]{1,0:T(8,128)S(1)}, u32[]{:S(2)}, u32[]{:S(2)}) collective-permute-start(f32[128,512]{1,0:T(8,128)S(1)} %pad_maximum_fusion.2), channel_id=1, source_target_pairs={{0,4},{2,6},{4,0},{6,2},{1,5},{3,7},{5,1},{7,3},{8,12},{10,14},{12... | collective-permute-start | bytes 786440 | tf_op jit(solution)/shard_map/ppermute | solution.py:113
  193.4 5.7 %collective-permute-start.9 = (f32[256,512]{1,0:T(8,128)S(1)}, f32[256,512]{1,0:T(8,128)S(1)}, u32[]{:S(2)}, u32[]{:S(2)}) collective-permute-start(f32[256,512]{1,0:T(8,128)S(1)} %constant_dynamic-update-slice_fusion), channel_id=1, source_target_pairs={{0,1},{1,0},{2,3},{3,2},{4,5},{5,4},{6,7},{7,6},{8,9},{9,8},{10,11... | collective-permute-start | bytes 1572872 | tf_op jit(solution)/shard_map/ppermute | solution.py:113

commit v4 on v3

--- a/solution.py
+++ b/solution.py
@@ -10,10 +10,11 @@
 
 F32 = jnp.float32
 BF16 = jnp.bfloat16
+MARK = jax.ShapeDtypeStruct((8, 128), F32)
 VMEM_LIMIT = 48 * 1024 * 1024
 
 
-def tile_kernel(pos_ref, live_ref, core_ref, blocks_ref, own_ref, other_ref, out_ref, acc_ref, *, group, n_x):
+def tile_kernel(pos_ref, live_ref, core_ref, blocks_ref, own_ref, other_ref, out_ref, mark_ref, acc_ref, low_ref, sems, *, group, n_x):
     n_y, width, _ = out_ref.shape
     blk = blocks_ref.shape[-1]
     tile_cols = acc_ref.shape[0]
@@ -41,9 +42,15 @@
         return carry
 
     lax.fori_loop(0, (live + group - 1) // group, add_group, 0)
+    copies = []
     for y in range(n_y):
         for z in range(width // blk):
-            out_ref[y, z * blk : (z + 1) * blk, :] = acc_ref[z * n_y + y].astype(BF16)
+            low_ref[y, z * blk : (z + 1) * blk, :] = acc_ref[z * n_y + y].astype(BF16)
+        copies.append(pltpu.make_async_copy(low_ref.at[y], out_ref.at[y], sems.at[y]))
+        copies[-1].start()
+    mark_ref[...] = jnp.zeros_like(mark_ref)
+    for copy in copies:
+        copy.wait()
 
 
 def terms_kernel(core_ref, own_ref, other_ref, out_ref, *, n_rows):
@@ -62,16 +69,16 @@
     out_ref[n_slice:, :] = bias_terms
 
 
-def fold_kernel(in_ref, out_ref):
+def fold_kernel(in_ref, out_ref, mark_ref):
+    mark_ref[...] = jnp.zeros_like(mark_ref)
     total = in_ref[0].astype(F32)
     for s in range(1, in_ref.shape[0]):
         total += in_ref[s].astype(F32)
     out_ref[...] = total.astype(BF16)
 
 
-def place_kernel(index_ref, *refs):
+def place_kernel(index_ref, *refs, n_slice):
     out_ref = refs[-1]
-    n_slice = refs[0].shape[0]
     offset = 0
     for ref in refs[:-1]:
         for k in range(ref.shape[0] // n_slice):
@@ -92,14 +99,17 @@
     rows_ref[...] = product.astype(BF16)
 
 
-def call(kernel, out_shape, scratch=(), n_scalar=0, n_in=1):
+def call(kernel, out_shape, scratch=(), n_scalar=0, n_in=1, marked=False, out_space=pltpu.VMEM):
     smem = pl.BlockSpec(memory_space=pltpu.SMEM)
     vmem = pl.BlockSpec(memory_space=pltpu.VMEM)
+    out_specs = pl.BlockSpec(memory_space=out_space)
+    if marked:
+        out_shape, out_specs = (out_shape, MARK), (out_specs, vmem)
     return pl.pallas_call(
         kernel,
         out_shape=out_shape,
         in_specs=[smem] * n_scalar + [vmem] * n_in,
-        out_specs=jax.tree.map(lambda _: vmem, out_shape),
+        out_specs=out_specs,
         scratch_shapes=list(scratch),
         compiler_params=pltpu.CompilerParams(vmem_limit_bytes=VMEM_LIMIT),
     )
@@ -134,45 +144,53 @@
     core = lax.axis_index("core").astype(jnp.int32).reshape(1)
     slots = adj_blocks.shape[2]
     group = max(d for d in range(1, 9) if slots % d == 0)
-    sent = call(
+    sent, mark = call(
         functools.partial(tile_kernel, group=group, n_x=n_x),
         jax.ShapeDtypeStruct((n_y, n_zh * blk, n_feat), BF16),
-        scratch=[pltpu.VMEM((n_zh * n_y, blk, n_feat), F32)],
+        scratch=[
+            pltpu.VMEM((n_zh * n_y, blk, n_feat), F32),
+            pltpu.VMEM((n_y, n_zh * blk, n_feat), BF16),
+            pltpu.SemaphoreType.DMA((n_y,)),
+        ],
+        out_space=pltpu.HBM,
+        marked=True,
         n_scalar=3,
         n_in=3,
     )(block_pos.reshape(-1), block_live.reshape(-1), core, adj_blocks[0, 0], own, other)
-    own, other, sent = lax.optimization_barrier((own, other, sent))
+    later, _ = lax.optimization_barrier((core, mark))
     terms = call(
         functools.partial(terms_kernel, n_rows=n_rows),
         jax.ShapeDtypeStruct((n_terms, n_feat), F32),
         n_scalar=1,
         n_in=2,
-    )(core, own, other)
-    for axis in ("y", "zh"):
-        for bit in (1, 2):
-            terms = terms + trade(terms, axis, bit)
+    )(later, own, other)
+    for bit in (1, 2):
+        terms = terms + trade(terms, "zh", bit)
     factor = 1.0 / math.sqrt(blk * n_zh * n_y * n_zl * n_x * n_core)
     terms = terms * factor
-    pieces = [terms[:n_slice]]
+    slices, bias = terms[:n_slice], terms[n_slice:]
     offsets = [0]
-    for axis, bit, stride in (
-        ("zl", 1, n_x * n_core),
-        ("zl", 2, n_x * n_core),
-        ("x", 1, n_core),
-        ("x", 2, n_core),
-        ("core", 1, 1),
-    ):
+    for bit in (1, 2):
+        slices = jnp.concatenate([slices, trade(slices, "zl", bit)], axis=0)
+        offsets += [o ^ (bit * n_x * n_core) for o in offsets]
+    terms = jnp.concatenate([slices, bias], axis=0)
+    got = swap(sent, "y")
+    sent, mark = call(fold_kernel, jax.ShapeDtypeStruct((n_zh * blk, n_feat), BF16), marked=True)(got)
+    terms, _ = lax.optimization_barrier((terms, mark))
+    for bit in (1, 2):
+        terms = terms + trade(terms, "y", bit)
+    pieces = [terms[: n_zl * n_slice]]
+    for axis, bit, stride in (("x", 1, n_core), ("x", 2, n_core), ("core", 1, 1)):
         pieces.append(trade(jnp.concatenate(pieces, axis=0), axis, bit))
         offsets += [o ^ (bit * stride) for o in offsets]
-    place = lax.axis_index(("zl", "x", "core")).astype(jnp.int32)
-    grad_weight = call(place_kernel, jax.ShapeDtypeStruct((n_feat, n_feat), F32), n_scalar=1, n_in=len(pieces))(
-        jnp.concatenate([place.reshape(1), jnp.array(offsets, jnp.int32)]), *pieces
+    mine = lax.axis_index(("zl", "x", "core")).astype(jnp.int32)
+    place = functools.partial(place_kernel, n_slice=n_slice)
+    grad_weight = call(place, jax.ShapeDtypeStruct((n_feat, n_feat), F32), n_scalar=1, n_in=len(pieces))(
+        jnp.concatenate([mine.reshape(1), jnp.array(offsets, jnp.int32)]), *pieces
     )
-    got = swap(sent, "y")
-    sent = call(fold_kernel, jax.ShapeDtypeStruct((n_zh * blk, n_feat), BF16))(got)
     got = swap(sent.reshape(n_zh, blk, n_feat), "zh")
     out_rows = call(last_kernel, jax.ShapeDtypeStruct((blk, n_feat), BF16), n_in=2)(got, weight)
-    return out_rows[None], grad_weight, terms[n_slice]
+    return out_rows[None], grad_weight, terms[n_zl * n_slice]
 
 
 def solution(mesh):

time: 204 us -> 172 us (0.84)
  waiting for transfers between devices: 70.1 us -> 34.3 us
  starting transfers between devices: 61.6 us -> 64.8 us
    ppermute x9, waiting for transfers between devices: 66.6 us -> 30.9 us  [trade(): lax.ppermute(value, axis, [(i, i ^ bit) for i in range(lax.axis_size(axis...]
    ppermute x9, starting transfers between devices: 37.6 us -> 46.4 us  [trade(): lax.ppermute(value, axis, [(i, i ^ bit) for i in range(lax.axis_size(axis...]
    all_to_all x2, starting transfers between devices: 18.8 us -> 13.1 us  [swap(): return lax.all_to_all(value, axis, split_axis=0, concat_axis=0, tiled=True)]
  transfers between devices with their start and end apart: 12 -> 12, of which waited for: 10 -> 9; matrix products, arithmetic and copies ran while one was open for 0% -> 0% of each run, Pallas kernels for 2% -> 4%
where the time goes in v4:
time: 172 us; the launch traced here: 171 us
  starting transfers between devices  64.8 us (38%)
  blocking collectives  51.9 us (30%)
  waiting for transfers between devices  34.3 us (20%)
  Pallas kernels  13.4 us (8%)
  local copies, waits for them, and re-layouts  3.45 us (2%)
    all_to_all x2, blocking collectives, swap(): return lax.all_to_all(value, axis, split_axis=0, concat_axis=0, tiled=True)  51.9 us
    ppermute x9, starting transfers between devices, trade(): lax.ppermute(value, axis, [(i, i ^ bit) for i in range(lax.axis_size(axis...  46.4 us
    ppermute x9, waiting for transfers between devices, trade(): lax.ppermute(value, axis, [(i, i ^ bit) for i in range(lax.axis_size(axis...  30.9 us
    all_to_all x2, starting transfers between devices, swap(): return lax.all_to_all(value, axis, split_axis=0, concat_axis=0, tiled=True)  13.1 us
    pallas_call x1, Pallas kernels, body(): call(functools.partial(tile_kernel, group=group, n_x=n_x), jax.ShapeDtype...  5.24 us
    ppermute x1, starting transfers between devices, body(): other = lax.ppermute(own, 'core', [(0, 1), (1, 0)])  5.2 us
  transfers between devices with their start and end apart: 12, of which 9 were waited for; matrix products, arithmetic and copies ran while one was open for 0% of the time, Pallas kernels for 4%

profile of v4, /device:TPU:1, one launch (start us, length us, event | category | flops | bytes accessed | tf_op | source)
XLA Modules:
  0.0 170.8 jit_solution(2352295964474648404)
XLA Ops:
  2.8 22.0 %all_to_all.20 = bf16[4,160,512]{2,1,0:T(8,128)(2,1)S(1)} all-to-all(bf16[4,160,512]{2,1,0:T(8,128)(2,1)S(1)} %pad_maximum_fusion.1), channel_id=1, replica_groups=mesh['zh'=4,'y'=4,'zl'=4,'x'=4,'core'=2] {'zl'}, dimensions={0} | all-to-all | bytes 1310720 | tf_op jit(solution)/shard_map/all_to_all | solution.py:119
  25.4 29.9 %all_to_all.21.own_ref = bf16[4,544,512]{2,1,0:T(8,128)(2,1)S(1)} all-to-all(bf16[4,544,512]{2,1,0:T(8,128)(2,1)S(1)} %pad_maximum_fusion), channel_id=1, replica_groups=mesh['zh'=4,'y'=4,'zl'=4,'x'=4,'core'=2] {'x'}, dimensions={0} | all-to-all | bytes 4456448 | tf_op jit(solution)/shard_map/all_to_all | solution.py:119
  55.3 5.2 %collective-permute-start = (bf16[4,544,512]{2,1,0:T(8,128)(2,1)S(1)}, bf16[4,544,512]{2,1,0:T(8,128)(2,1)}, u32[]{:S(2)}, u32[]{:S(2)}) collective-permute-start(bf16[4,544,512]{2,1,0:T(8,128)(2,1)S(1)} %all_to_all.21.own_ref), channel_id=1, source_target_pairs={{0,1},{1,0},{2,3},{3,2},{4,5},{5,4},{6,7},{7,6},{8,9},{9,8},{10,11... | collective-permute-start | bytes 6684680 | tf_op jit(solution)/shard_map/ppermute | solution.py:143
  61.2 3.4 %collective-permute-done.other_ref = bf16[4,544,512]{2,1,0:T(8,128)(2,1)} collective-permute-done((bf16[4,544,512]{2,1,0:T(8,128)(2,1)S(1)}, bf16[4,544,512]{2,1,0:T(8,128)(2,1)}, u32[]{:S(2)}, u32[]{:S(2)}) %collective-permute-start) | collective-permute-done | bytes 2228256 | tf_op jit(solution)/shard_map/ppermute | solution.py:143
  64.6 5.2 %shard_map.103 = (bf16[4,512,512]{2,1,0:T(8,128)(2,1)S(1)}, f32[8,128]{1,0:T(8,128)}) custom-call(s32[85]{0:T(128)S(1)} %bitcast.20, s32[1]{0:T(128)} %bitcast.19.live_ref, s32[1]{0:T(128)} %bitcast.2.core_ref, bf16[85,128,128]{2,1,0:T(8,128)(2,1)} %bitcast.21, bf16[4,544,512]{2,1,0:T(8,128)(2,1)S(1)} %all_to_all.21.own_ref, ...), custom_call_target="tpu_custom_call" | custom-call | tf_op jit(solution)/shard_map/pallas_call | solution.py:147
  71.2 4.5 %all-to-all-start.2 = ((bf16[4,512,512]{2,1,0:T(8,128)(2,1)}), bf16[4,512,512]{2,1,0:T(8,128)(2,1)}, u32[]{:S(2)}, u32[]{:S(2)}) async-start(bf16[4,512,512]{2,1,0:T(8,128)(2,1)} %copy-done), calls=%async_computation.2 | async-start | bytes 4194304 | tf_op jit(solution)/shard_map/all_to_all | solution.py:119
  75.7 2.8 %shard_map.106 = f32[24,512]{1,0:T(8,128)S(1)} custom-call(s32[1]{0:T(128)} %bitcast.2.core_ref, bf16[4,544,512]{2,1,0:T(8,128)(2,1)S(1)} %all_to_all.21.own_ref, bf16[4,544,512]{2,1,0:T(8,128)(2,1)} %collective-permute-done.other_ref), custom_call_target="tpu_custom_call" | custom-call | tf_op jit(solution)/shard_map/pallas_call | solution.py:161
  78.5 13.1 %collective-permute-start.1 = (f32[24,512]{1,0:T(8,128)S(1)}, f32[24,512]{1,0:T(8,128)S(1)}, u32[]{:S(2)}, u32[]{:S(2)}) collective-permute-start(f32[24,512]{1,0:T(8,128)S(1)} %shard_map.106), channel_id=1, source_target_pairs={{0,128},{128,0},{256,384},{384,256},{1,129},{129,1},{257,385},{385... | collective-permute-start | bytes 147464 | tf_op jit(solution)/shard_map/ppermute | solution.py:123
  91.6 3.8 %collective-permute-done.1 = f32[24,512]{1,0:T(8,128)S(1)} collective-permute-done((f32[24,512]{1,0:T(8,128)S(1)}, f32[24,512]{1,0:T(8,128)S(1)}, u32[]{:S(2)}, u32[]{:S(2)}) %collective-permute-start.1) | collective-permute-done | bytes 49184 | tf_op jit(solution)/shard_map/ppermute | solution.py:123
  95.4 7.1 %collective-permute-start.2 = (f32[24,512]{1,0:T(8,128)S(1)}, f32[24,512]{1,0:T(8,128)S(1)}, u32[]{:S(2)}, u32[]{:S(2)}) collective-permute-start(f32[24,512]{1,0:T(8,128)S(1)} %add.20), channel_id=1, source_target_pairs={{0,256},{128,384},{256,0},{384,128},{1,257},{129,385},{257,1},{385... | collective-permute-start | bytes 147464 | tf_op jit(solution)/shard_map/ppermute | solution.py:123
  102.5 8.0 %collective-permute-done.2 = f32[24,512]{1,0:T(8,128)S(1)} collective-permute-done((f32[24,512]{1,0:T(8,128)S(1)}, f32[24,512]{1,0:T(8,128)S(1)}, u32[]{:S(2)}, u32[]{:S(2)}) %collective-permute-start.2) | collective-permute-done | bytes 49184 | tf_op jit(solution)/shard_map/ppermute | solution.py:123
  110.5 1.9 %collective-permute-start.3 = (f32[16,512]{1,0:T(8,128)S(1)}, f32[16,512]{1,0:T(8,128)S(1)}, u32[]{:S(2)}, u32[]{:S(2)}) collective-permute-start(f32[16,512]{1,0:T(8,128)S(1)} %slice.26), channel_id=1, source_target_pairs={{0,8},{8,0},{16,24},{24,16},{1,9},{9,1},{17,25},{25,17},{2,10},{10... | collective-permute-start | bytes 98312 | tf_op jit(solution)/shard_map/ppermute | solution.py:123
  112.5 2.7 %collective-permute-done.3 = f32[16,512]{1,0:T(8,128)S(1)} collective-permute-done((f32[16,512]{1,0:T(8,128)S(1)}, f32[16,512]{1,0:T(8,128)S(1)}, u32[]{:S(2)}, u32[]{:S(2)}) %collective-permute-start.3) | collective-permute-done | bytes 32800 | tf_op jit(solution)/shard_map/ppermute | solution.py:123
  117.1 2.6 %shard_map.104 = (bf16[512,512]{1,0:T(8,128)(2,1)}, f32[8,128]{1,0:T(8,128)}) custom-call(bf16[4,512,512]{2,1,0:T(8,128)(2,1)} %all-to-all-done.2.in_ref), custom_call_target="tpu_custom_call" | custom-call | tf_op jit(solution)/shard_map/pallas_call | solution.py:178
  119.8 8.7 %all-to-all-start.3 = ((bf16[4,128,512]{2,1,0:T(8,128)(2,1)}), bf16[4,128,512]{2,1,0:T(8,128)(2,1)S(1)}, u32[]{:S(2)}, u32[]{:S(2)}) async-start(bf16[4,128,512]{2,1,0:T(8,128)(2,1)} %bitcast.9), calls=%async_computation.3 | async-start | bytes 1048576 | tf_op jit(solution)/shard_map/all_to_all | solution.py:119
  128.5 1.9 %collective-permute-start.5 = (f32[72,512]{1,0:T(8,128)S(1)}, f32[72,512]{1,0:T(8,128)S(1)}, u32[]{:S(2)}, u32[]{:S(2)}) collective-permute-start(f32[72,512]{1,0:T(8,128)S(1)} %pad_maximum_fusion.4), channel_id=1, source_target_pairs={{0,32},{32,0},{64,96},{96,64},{1,33},{33,1},{65,97},{97,65},{2,34}... | collective-permute-start | bytes 442376 | tf_op jit(solution)/shard_map/ppermute | solution.py:123
  130.4 4.0 %collective-permute-done.5 = f32[72,512]{1,0:T(8,128)S(1)} collective-permute-done((f32[72,512]{1,0:T(8,128)S(1)}, f32[72,512]{1,0:T(8,128)S(1)}, u32[]{:S(2)}, u32[]{:S(2)}) %collective-permute-start.5) | collective-permute-done | bytes 147488 | tf_op jit(solution)/shard_map/ppermute | solution.py:123
  134.4 5.2 %collective-permute-start.6 = (f32[72,512]{1,0:T(8,128)S(1)}, f32[72,512]{1,0:T(8,128)S(1)}, u32[]{:S(2)}, u32[]{:S(2)}) collective-permute-start(f32[72,512]{1,0:T(8,128)S(1)} %add.22), channel_id=1, source_target_pairs={{0,64},{32,96},{64,0},{96,32},{1,65},{33,97},{65,1},{97,33},{2,66}... | collective-permute-start | bytes 442376 | tf_op jit(solution)/shard_map/ppermute | solution.py:123
  139.6 2.8 %collective-permute-done.6 = f32[72,512]{1,0:T(8,128)S(1)} collective-permute-done((f32[72,512]{1,0:T(8,128)S(1)}, f32[72,512]{1,0:T(8,128)S(1)}, u32[]{:S(2)}, u32[]{:S(2)}) %collective-permute-start.6) | collective-permute-done | bytes 147488 | tf_op jit(solution)/shard_map/ppermute | solution.py:123
  142.4 3.0 %collective-permute-start.7 = (f32[64,512]{1,0:T(8,128)S(1)}, f32[64,512]{1,0:T(8,128)S(1)}, u32[]{:S(2)}, u32[]{:S(2)}) collective-permute-start(f32[64,512]{1,0:T(8,128)S(1)} %slice.28.refs_0_), channel_id=1, source_target_pairs={{0,2},{2,0},{4,6},{6,4},{1,3},{3,1},{5,7},{7,5},{8,10},{10,8},{12,... | collective-permute-start | bytes 393224 | tf_op jit(solution)/shard_map/ppermute | solution.py:123
  145.4 3.0 %collective-permute-done.7.refs_1_ = f32[64,512]{1,0:T(8,128)S(1)} collective-permute-done((f32[64,512]{1,0:T(8,128)S(1)}, f32[64,512]{1,0:T(8,128)S(1)}, u32[]{:S(2)}, u32[]{:S(2)}) %collective-permute-start.7) | collective-permute-done | bytes 131104 | tf_op jit(solution)/shard_map/ppermute | solution.py:123
  148.5 3.3 %collective-permute-start.8 = (f32[128,512]{1,0:T(8,128)S(1)}, f32[128,512]{1,0:T(8,128)S(1)}, u32[]{:S(2)}, u32[]{:S(2)}) collective-permute-start(f32[128,512]{1,0:T(8,128)S(1)} %pad_maximum_fusion.3), channel_id=1, source_target_pairs={{0,4},{2,6},{4,0},{6,2},{1,5},{3,7},{5,1},{7,3},{8,12},{10,14},{12... | collective-permute-start | bytes 786440 | tf_op jit(solution)/shard_map/ppermute | solution.py:123
  151.8 5.8 %collective-permute-done.8.refs_2_ = f32[128,512]{1,0:T(8,128)S(1)} collective-permute-done((f32[128,512]{1,0:T(8,128)S(1)}, f32[128,512]{1,0:T(8,128)S(1)}, u32[]{:S(2)}, u32[]{:S(2)}) %collective-permute-start.8) | collective-permute-done | bytes 262176 | tf_op jit(solution)/shard_map/ppermute | solution.py:123
  157.6 9.0 %collective-permute-start.9 = (f32[256,512]{1,0:T(8,128)S(1)}, f32[256,512]{1,0:T(8,128)S(1)}, u32[]{:S(2)}, u32[]{:S(2)}) collective-permute-start(f32[256,512]{1,0:T(8,128)S(1)} %pad_maximum_fusion.2), channel_id=1, source_target_pairs={{0,1},{1,0},{2,3},{3,2},{4,5},{5,4},{6,7},{7,6},{8,9},{9,8},{10,11... | collective-permute-start | bytes 1572872 | tf_op jit(solution)/shard_map/ppermute | solution.py:123
  (40 shorter events, 10.4 us)
Async XLA Ops:
  25.4 39.2 %copy-start.2 = (s32[1,1,85]{2,1,0:T(1,128)S(1)}, s32[1,1,85]{2,1,0:T(1,128)}, u32[]{:S(2)}) copy-start(s32[1,1,85]{2,1,0:T(1,128)} %param.13) | copy-start | bytes 1024
  55.3 9.3 %collective-permute-start = (bf16[4,544,512]{2,1,0:T(8,128)(2,1)S(1)}, bf16[4,544,512]{2,1,0:T(8,128)(2,1)}, u32[]{:S(2)}, u32[]{:S(2)}) collective-permute-start(bf16[4,544,512]{2,1,0:T(8,128)(2,1)S(1)} %all_to_all.21.own_ref), channel_id=1, source_target_pairs={{0,1},{1,0},{2,3},{3,2},{4,5},{5,4},{6,7},{7,6},{8,9},{9,8},{10,11... | collective-permute-start | bytes 6684680 | tf_op jit(solution)/shard_map/ppermute | solution.py:143
  69.9 1.4 copy-start
  71.2 45.9 %all-to-all-start.2 = ((bf16[4,512,512]{2,1,0:T(8,128)(2,1)}), bf16[4,512,512]{2,1,0:T(8,128)(2,1)}, u32[]{:S(2)}, u32[]{:S(2)}) async-start(bf16[4,512,512]{2,1,0:T(8,128)(2,1)} %copy-done), calls=%async_computation.2 | async-start | bytes 4194304 | tf_op jit(solution)/shard_map/all_to_all | solution.py:119
  78.5 16.9 %collective-permute-start.1 = (f32[24,512]{1,0:T(8,128)S(1)}, f32[24,512]{1,0:T(8,128)S(1)}, u32[]{:S(2)}, u32[]{:S(2)}) collective-permute-start(f32[24,512]{1,0:T(8,128)S(1)} %shard_map.106), channel_id=1, source_target_pairs={{0,128},{128,0},{256,384},{384,256},{1,129},{129,1},{257,385},{385... | collective-permute-start | bytes 147464 | tf_op jit(solution)/shard_map/ppermute | solution.py:123
  95.4 15.1 %collective-permute-start.2 = (f32[24,512]{1,0:T(8,128)S(1)}, f32[24,512]{1,0:T(8,128)S(1)}, u32[]{:S(2)}, u32[]{:S(2)}) collective-permute-start(f32[24,512]{1,0:T(8,128)S(1)} %add.20), channel_id=1, source_target_pairs={{0,256},{128,384},{256,0},{384,128},{1,257},{129,385},{257,1},{385... | collective-permute-start | bytes 147464 | tf_op jit(solution)/shard_map/ppermute | solution.py:123
  110.5 4.7 %collective-permute-start.3 = (f32[16,512]{1,0:T(8,128)S(1)}, f32[16,512]{1,0:T(8,128)S(1)}, u32[]{:S(2)}, u32[]{:S(2)}) collective-permute-start(f32[16,512]{1,0:T(8,128)S(1)} %slice.26), channel_id=1, source_target_pairs={{0,8},{8,0},{16,24},{24,16},{1,9},{9,1},{17,25},{25,17},{2,10},{10... | collective-permute-start | bytes 98312 | tf_op jit(solution)/shard_map/ppermute | solution.py:123
  115.2 13.3 %collective-permute-start.4 = (f32[32,512]{1,0:T(8,128)S(1)}, f32[32,512]{1,0:T(8,128)S(1)}, u32[]{:S(2)}, u32[]{:S(2)}) collective-permute-start(f32[32,512]{1,0:T(8,128)S(1)} %pad_maximum_fusion.5), channel_id=1, source_target_pairs={{0,16},{8,24},{16,0},{24,8},{1,17},{9,25},{17,1},{25,9},{2,18},{10... | collective-permute-start | bytes 196616 | tf_op jit(solution)/shard_map/ppermute | solution.py:123
  119.8 46.8 %copy-start.3 = (s32[32]{0:T(128)S(1)}, s32[32]{0:T(128)}, u32[]{:S(2)}) copy-start(s32[32]{0:T(128)} %constant.19.clone) | copy-start | bytes 388
  119.8 49.9 %all-to-all-start.3 = ((bf16[4,128,512]{2,1,0:T(8,128)(2,1)}), bf16[4,128,512]{2,1,0:T(8,128)(2,1)S(1)}, u32[]{:S(2)}, u32[]{:S(2)}) async-start(bf16[4,128,512]{2,1,0:T(8,128)(2,1)} %bitcast.9), calls=%async_computation.3 | async-start | bytes 1048576 | tf_op jit(solution)/shard_map/all_to_all | solution.py:119
  128.5 5.9 %collective-permute-start.5 = (f32[72,512]{1,0:T(8,128)S(1)}, f32[72,512]{1,0:T(8,128)S(1)}, u32[]{:S(2)}, u32[]{:S(2)}) collective-permute-start(f32[72,512]{1,0:T(8,128)S(1)} %pad_maximum_fusion.4), channel_id=1, source_target_pairs={{0,32},{32,0},{64,96},{96,64},{1,33},{33,1},{65,97},{97,65},{2,34}... | collective-permute-start | bytes 442376 | tf_op jit(solution)/shard_map/ppermute | solution.py:123
  134.4 35.3 %copy-start.1 = (bf16[512,512]{1,0:T(8,128)(2,1)S(1)}, bf16[512,512]{1,0:T(8,128)(2,1)}, u32[]{:S(2)}) copy-start(bf16[512,512]{1,0:T(8,128)(2,1)} %weight_ref.1) | copy-start | bytes 1572868
  134.4 8.0 %collective-permute-start.6 = (f32[72,512]{1,0:T(8,128)S(1)}, f32[72,512]{1,0:T(8,128)S(1)}, u32[]{:S(2)}, u32[]{:S(2)}) collective-permute-start(f32[72,512]{1,0:T(8,128)S(1)} %add.22), channel_id=1, source_target_pairs={{0,64},{32,96},{64,0},{96,32},{1,65},{33,97},{65,1},{97,33},{2,66}... | collective-permute-start | bytes 442376 | tf_op jit(solution)/shard_map/ppermute | solution.py:123
  142.4 6.0 %collective-permute-start.7 = (f32[64,512]{1,0:T(8,128)S(1)}, f32[64,512]{1,0:T(8,128)S(1)}, u32[]{:S(2)}, u32[]{:S(2)}) collective-permute-start(f32[64,512]{1,0:T(8,128)S(1)} %slice.28.refs_0_), channel_id=1, source_target_pairs={{0,2},{2,0},{4,6},{6,4},{1,3},{3,1},{5,7},{7,5},{8,10},{10,8},{12,... | collective-permute-start | bytes 393224 | tf_op jit(solution)/shard_map/ppermute | solution.py:123
  148.5 9.1 %collective-permute-start.8 = (f32[128,512]{1,0:T(8,128)S(1)}, f32[128,512]{1,0:T(8,128)S(1)}, u32[]{:S(2)}, u32[]{:S(2)}) collective-permute-start(f32[128,512]{1,0:T(8,128)S(1)} %pad_maximum_fusion.3), channel_id=1, source_target_pairs={{0,4},{2,6},{4,0},{6,2},{1,5},{3,7},{5,1},{7,3},{8,12},{10,14},{12... | collective-permute-start | bytes 786440 | tf_op jit(solution)/shard_map/ppermute | solution.py:123
  157.6 10.5 %collective-permute-start.9 = (f32[256,512]{1,0:T(8,128)S(1)}, f32[256,512]{1,0:T(8,128)S(1)}, u32[]{:S(2)}, u32[]{:S(2)}) collective-permute-start(f32[256,512]{1,0:T(8,128)S(1)} %pad_maximum_fusion.2), channel_id=1, source_target_pairs={{0,1},{1,0},{2,3},{3,2},{4,5},{5,4},{6,7},{7,6},{8,9},{9,8},{10,11... | collective-permute-start | bytes 1572872 | tf_op jit(solution)/shard_map/ppermute | solution.py:123

commit v5 on v4

--- a/solution.py
+++ b/solution.py
@@ -53,20 +53,27 @@
         copy.wait()
 
 
-def terms_kernel(core_ref, own_ref, other_ref, out_ref, *, n_rows):
-    n_x, _, n_feat = own_ref.shape
-    n_slice = out_ref.shape[0] - 8
-    first = pl.multiple_of(n_rows + core_ref[0] * n_slice, n_slice)
-    weight_terms = jnp.zeros((n_slice, n_feat), F32)
+def terms_kernel(place_ref, got_ref, keep_ref, send_ref, sum_ref, *, blk):
+    n_src, width, n_feat = got_ref.shape
+    n_y = n_feat // blk
+    n_pair = width - blk
+    n_slice = n_pair // 2
+    ones = jnp.ones((8, blk), BF16)
     bias_terms = jnp.zeros((8, n_feat), F32)
-    ones = jnp.ones((8, n_rows), BF16)
-    for ref in (own_ref, other_ref):
-        for x in range(n_x):
-            rows = ref[x, :n_rows, :]
-            weight_terms += jnp.dot(ref[x, pl.ds(first, n_slice), :], rows, preferred_element_type=F32)
-            bias_terms += jnp.dot(ones, rows, preferred_element_type=F32)
-    out_ref[:n_slice, :] = weight_terms
-    out_ref[n_slice:, :] = bias_terms
+    for s in range(n_src):
+        bias_terms += jnp.dot(ones, got_ref[s, :blk, :], preferred_element_type=F32)
+    for y in range(n_y):
+        total = jnp.zeros((n_pair, n_feat), F32)
+        for s in range(n_src):
+            features = got_ref[s, blk:, y * blk : (y + 1) * blk]
+            total += jnp.dot(features, got_ref[s, :blk, :], preferred_element_type=F32)
+        sum_ref[y] = total
+    mine, my_y = place_ref[0], place_ref[1]
+    for ref, core in ((keep_ref, mine), (send_ref, 1 - mine)):
+        first = pl.multiple_of(core * n_slice, n_slice)
+        for y in range(n_y):
+            ref[y * n_slice : (y + 1) * n_slice, :] = sum_ref[my_y ^ y, pl.ds(first, n_slice), :]
+        ref[n_y * n_slice :, :] = bias_terms
 
 
 def fold_kernel(in_ref, out_ref, mark_ref):
@@ -102,7 +109,7 @@
 def call(kernel, out_shape, scratch=(), n_scalar=0, n_in=1, marked=False, out_space=pltpu.VMEM):
     smem = pl.BlockSpec(memory_space=pltpu.SMEM)
     vmem = pl.BlockSpec(memory_space=pltpu.VMEM)
-    out_specs = pl.BlockSpec(memory_space=out_space)
+    out_specs = jax.tree.map(lambda _: pl.BlockSpec(memory_space=out_space), out_shape)
     if marked:
         out_shape, out_specs = (out_shape, MARK), (out_specs, vmem)
     return pl.pallas_call(
@@ -127,21 +134,30 @@
     blk, n_feat = grad_out.shape
     n_zh, n_y, n_zl, n_x, n_core = (lax.axis_size(a) for a in ("zh", "y", "zl", "x", "core"))
     n_rows = n_zl * blk
-    n_pair = n_feat // (n_zl * n_x)
+    n_pair = n_feat // (n_zl * n_y)
     n_slice = n_pair // n_core
-    n_terms = n_slice + 8
     grad_pre = grad_out * relu_mask.astype(BF16)
-    columns = aggregated.T.reshape(n_zl, n_x, n_pair, blk).transpose(0, 2, 1, 3)
-    columns = columns.reshape(n_zl, n_pair, n_x * blk)
+    columns = aggregated.T.reshape(n_zl, n_y, n_pair, blk).transpose(0, 2, 1, 3)
+    columns = columns.reshape(n_zl, n_pair, n_y * blk)
     sent = jnp.concatenate([jnp.broadcast_to(grad_pre, (n_zl, blk, n_feat)), columns], axis=1)
     got = swap(sent, "zl")
+    core, y_index = (lax.axis_index(a).astype(jnp.int32).reshape(1) for a in ("core", "y"))
+    half = jax.ShapeDtypeStruct((n_y * n_slice + 8, n_feat), F32)
+    terms, away = call(
+        functools.partial(terms_kernel, blk=blk),
+        (half, half),
+        scratch=[pltpu.VMEM((n_y, n_pair, n_feat), F32)],
+        n_scalar=1,
+    )(jnp.concatenate([core, y_index]), got)
     rows = got[:, :blk].reshape(n_rows, n_feat)
-    columns = got[:, blk:].reshape(n_zl, n_pair, n_x, blk).transpose(2, 1, 0, 3)
-    columns = columns.reshape(n_x, n_pair, n_rows)
-    sent = jnp.concatenate([jnp.broadcast_to(rows, (n_x, n_rows, n_feat)), columns], axis=1)
-    own = swap(sent, "x")
+    own = swap(jnp.broadcast_to(rows, (n_x, n_rows, n_feat)), "x")
+    terms = terms + trade(away, "core", 1)
+    for bit, n in ((2, 2 * n_slice), (1, n_slice)):
+        kept, away, bias = terms[:n], terms[n : 2 * n], terms[2 * n :]
+        terms = jnp.concatenate([kept, bias], axis=0) + trade(jnp.concatenate([away, bias], axis=0), "y", bit)
+    terms = terms + trade(terms, "zh", 1)
+    own, terms = lax.optimization_barrier((own, terms))
     other = lax.ppermute(own, "core", [(0, 1), (1, 0)])
-    core = lax.axis_index("core").astype(jnp.int32).reshape(1)
     slots = adj_blocks.shape[2]
     group = max(d for d in range(1, 9) if slots % d == 0)
     sent, mark = call(
@@ -157,33 +173,26 @@
         n_scalar=3,
         n_in=3,
     )(block_pos.reshape(-1), block_live.reshape(-1), core, adj_blocks[0, 0], own, other)
-    later, _ = lax.optimization_barrier((core, mark))
-    terms = call(
-        functools.partial(terms_kernel, n_rows=n_rows),
-        jax.ShapeDtypeStruct((n_terms, n_feat), F32),
-        n_scalar=1,
-        n_in=2,
-    )(later, own, other)
-    for bit in (1, 2):
-        terms = terms + trade(terms, "zh", bit)
+    terms, _ = lax.optimization_barrier((terms, mark))
+    terms = terms + trade(terms, "zh", 2)
     factor = 1.0 / math.sqrt(blk * n_zh * n_y * n_zl * n_x * n_core)
     terms = terms * factor
     slices, bias = terms[:n_slice], terms[n_slice:]
     offsets = [0]
     for bit in (1, 2):
         slices = jnp.concatenate([slices, trade(slices, "zl", bit)], axis=0)
-        offsets += [o ^ (bit * n_x * n_core) for o in offsets]
+        offsets += [o ^ (bit * n_y * n_core) for o in offsets]
     terms = jnp.concatenate([slices, bias], axis=0)
     got = swap(sent, "y")
     sent, mark = call(fold_kernel, jax.ShapeDtypeStruct((n_zh * blk, n_feat), BF16), marked=True)(got)
     terms, _ = lax.optimization_barrier((terms, mark))
     for bit in (1, 2):
-        terms = terms + trade(terms, "y", bit)
+        terms = terms + trade(terms, "x", bit)
     pieces = [terms[: n_zl * n_slice]]
-    for axis, bit, stride in (("x", 1, n_core), ("x", 2, n_core), ("core", 1, 1)):
+    for axis, bit, stride in (("y", 1, n_core), ("y", 2, n_core), ("core", 1, 1)):
         pieces.append(trade(jnp.concatenate(pieces, axis=0), axis, bit))
         offsets += [o ^ (bit * stride) for o in offsets]
-    mine = lax.axis_index(("zl", "x", "core")).astype(jnp.int32)
+    mine = lax.axis_index(("zl", "y", "core")).astype(jnp.int32)
     place = functools.partial(place_kernel, n_slice=n_slice)
     grad_weight = call(place, jax.ShapeDtypeStruct((n_feat, n_feat), F32), n_scalar=1, n_in=len(pieces))(
         jnp.concatenate([mine.reshape(1), jnp.array(offsets, jnp.int32)]), *pieces

time: 172 us -> 164 us (0.953)
  blocking collectives: 51.9 us -> 22 us
  starting transfers between devices: 64.8 us -> 91.1 us
  Pallas kernels: 13.4 us -> 9.24 us
  waiting for transfers between devices: 34.3 us -> 31.6 us
  local copies, waits for them, and re-layouts: 3.45 us -> 5.9 us
    all_to_all x2 -> x1, blocking collectives: 51.9 us -> 22 us  [swap(): return lax.all_to_all(value, axis, split_axis=0, concat_axis=0, tiled=True)]
    ppermute x9 -> x12, starting transfers between devices: 46.4 us -> 64.1 us  [trade(): lax.ppermute(value, axis, [(i, i ^ bit) for i in range(lax.axis_size(axis...]
    all_to_all x2 -> x3, starting transfers between devices: 13.1 us -> 22.2 us  [swap(): return lax.all_to_all(value, axis, split_axis=0, concat_axis=0, tiled=True)]
    ppermute x9 -> x12, waiting for transfers between devices: 30.9 us -> 28.4 us  [trade(): lax.ppermute(value, axis, [(i, i ^ bit) for i in range(lax.axis_size(axis...]
    pallas_call x1, Pallas kernels: 2.81 us -> 1.01 us  [body(): call(functools.partial(terms_kernel, blk=blk), (half, half), scratch=[plt...]
    unnamed x9 -> x11, local copies, waits for them, and re-layouts: 2.39 us -> 3.68 us
  transfers between devices with their start and end apart: 12 -> 16, of which waited for: 9 -> 12; matrix products, arithmetic and copies ran while one was open for 0% -> 1% of each run, Pallas kernels for 4% -> 2%
where the time goes in v5:
time: 164 us; the launch traced here: 163 us
  starting transfers between devices  91.1 us (56%)
  waiting for transfers between devices  31.6 us (19%)
  blocking collectives  22 us (13%)
  Pallas kernels  9.24 us (6%)
  local copies, waits for them, and re-layouts  5.9 us (4%)
    ppermute x12, starting transfers between devices, trade(): lax.ppermute(value, axis, [(i, i ^ bit) for i in range(lax.axis_size(axis...  64.1 us
    ppermute x12, waiting for transfers between devices, trade(): lax.ppermute(value, axis, [(i, i ^ bit) for i in range(lax.axis_size(axis...  28.4 us
    all_to_all x3, starting transfers between devices, swap(): return lax.all_to_all(value, axis, split_axis=0, concat_axis=0, tiled=True)  22.2 us
    all_to_all x1, blocking collectives, swap(): return lax.all_to_all(value, axis, split_axis=0, concat_axis=0, tiled=True)  22 us
    ppermute x1, starting transfers between devices, body(): other = lax.ppermute(own, 'core', [(0, 1), (1, 0)])  4.83 us
    pallas_call x1, Pallas kernels, body(): call(functools.partial(tile_kernel, group=group, n_x=n_x), jax.ShapeDtype...  4.46 us
    unnamed x11, local copies, waits for them, and re-layouts  3.68 us
  transfers between devices with their start and end apart: 16, of which 12 were waited for; matrix products, arithmetic and copies ran while one was open for 1% of the time, Pallas kernels for 2%

profile of v5, /device:TPU:1, one launch (start us, length us, event | category | flops | bytes accessed | tf_op | source)
XLA Modules:
  0.0 162.8 jit_solution(12508864744945626541)
XLA Ops:
  2.8 22.0 %all_to_all.20.got_ref = bf16[4,160,512]{2,1,0:T(8,128)(2,1)S(1)} all-to-all(bf16[4,160,512]{2,1,0:T(8,128)(2,1)S(1)} %pad_maximum_fusion), channel_id=1, replica_groups=mesh['zh'=4,'y'=4,'zl'=4,'x'=4,'core'=2] {'zl'}, dimensions={0} | all-to-all | bytes 1310720 | tf_op jit(solution)/shard_map/all_to_all | solution.py:126
  26.4 4.7 %all-to-all-start.1 = ((bf16[4,512,512]{2,1,0:T(8,128)(2,1)}), bf16[4,512,512]{2,1,0:T(8,128)(2,1)S(1)}, u32[]{:S(2)}, u32[]{:S(2)}) async-start(bf16[4,512,512]{2,1,0:T(8,128)(2,1)} %broadcast_in_dim.10), calls=%async_computation.1 | async-start | bytes 4194304 | tf_op jit(solution)/shard_map/all_to_all | solution.py:126
  32.2 4.0 %collective-permute-start = (f32[72,512]{1,0:T(8,128)S(1)}, f32[72,512]{1,0:T(8,128)S(1)}, u32[]{:S(2)}, u32[]{:S(2)}) collective-permute-start(f32[72,512]{1,0:T(8,128)S(1)} %get-tuple-element.10), channel_id=1, source_target_pairs={{0,1},{1,0},{2,3},{3,2},{4,5},{5,4},{6,7},{7,6},{8,9},{9,8},{10,11... | collective-permute-start | bytes 442376 | tf_op jit(solution)/shard_map/ppermute | solution.py:130
  37.2 4.8 %collective-permute-start.1 = (f32[40,512]{1,0:T(8,128)S(1)}, f32[40,512]{1,0:T(8,128)S(1)}, u32[]{:S(2)}, u32[]{:S(2)}) collective-permute-start(f32[40,512]{1,0:T(8,128)S(1)} %concatenate.45), channel_id=1, source_target_pairs={{0,64},{32,96},{64,0},{96,32},{1,65},{33,97},{65,1},{97,33},{2,66}... | collective-permute-start | bytes 245768 | tf_op jit(solution)/shard_map/ppermute | solution.py:130
  42.1 2.2 %collective-permute-done.1 = f32[40,512]{1,0:T(8,128)S(1)} collective-permute-done((f32[40,512]{1,0:T(8,128)S(1)}, f32[40,512]{1,0:T(8,128)S(1)}, u32[]{:S(2)}, u32[]{:S(2)}) %collective-permute-start.1) | collective-permute-done | bytes 81952 | tf_op jit(solution)/shard_map/ppermute | solution.py:130
  44.3 3.2 %collective-permute-start.2 = (f32[24,512]{1,0:T(8,128)S(1)}, f32[24,512]{1,0:T(8,128)S(1)}, u32[]{:S(2)}, u32[]{:S(2)}) collective-permute-start(f32[24,512]{1,0:T(8,128)S(1)} %concatenate.46), channel_id=1, source_target_pairs={{0,32},{32,0},{64,96},{96,64},{1,33},{33,1},{65,97},{97,65},{2,34}... | collective-permute-start | bytes 147464 | tf_op jit(solution)/shard_map/ppermute | solution.py:130
  49.4 8.8 %collective-permute-start.3 = (f32[24,512]{1,0:T(8,128)S(1)}, f32[24,512]{1,0:T(8,128)S(1)}, u32[]{:S(2)}, u32[]{:S(2)}) collective-permute-start(f32[24,512]{1,0:T(8,128)S(1)} %maximum_add_fusion.1), channel_id=1, source_target_pairs={{0,128},{128,0},{256,384},{384,256},{1,129},{129,1},{257,385},{385... | collective-permute-start | bytes 147464 | tf_op jit(solution)/shard_map/ppermute | solution.py:130
  58.3 2.7 %collective-permute-done.3 = f32[24,512]{1,0:T(8,128)S(1)} collective-permute-done((f32[24,512]{1,0:T(8,128)S(1)}, f32[24,512]{1,0:T(8,128)S(1)}, u32[]{:S(2)}, u32[]{:S(2)}) %collective-permute-start.3) | collective-permute-done | bytes 49184 | tf_op jit(solution)/shard_map/ppermute | solution.py:130
  61.0 4.8 %collective-permute-start.4 = (bf16[4,512,512]{2,1,0:T(8,128)(2,1)S(1)}, bf16[4,512,512]{2,1,0:T(8,128)(2,1)S(1)}, u32[]{:S(2)}, u32[]{:S(2)}) collective-permute-start(bf16[4,512,512]{2,1,0:T(8,128)(2,1)S(1)} %all-to-all-done.1.own_ref), channel_id=1, source_target_pairs={{0,1},{1,0},{2,3},{3,2},{4,5},{5,4},{6,7},{7,6},{8,9},{9,8},{10,11... | collective-permute-start | bytes 6291464 | tf_op jit(solution)/shard_map/ppermute | solution.py:160
  66.5 3.1 %collective-permute-done.4.other_ref = bf16[4,512,512]{2,1,0:T(8,128)(2,1)S(1)} collective-permute-done((bf16[4,512,512]{2,1,0:T(8,128)(2,1)S(1)}, bf16[4,512,512]{2,1,0:T(8,128)(2,1)S(1)}, u32[]{:S(2)}, u32[]{:S(2)}) %collective-permute-start.4) | collective-permute-done | bytes 2097184 | tf_op jit(solution)/shard_map/ppermute | solution.py:160
  70.9 4.5 %shard_map.104 = (bf16[4,512,512]{2,1,0:T(8,128)(2,1)S(1)}, f32[8,128]{1,0:T(8,128)}) custom-call(s32[85]{0:T(128)S(1)} %bitcast.20, s32[1]{0:T(128)} %bitcast.19.live_ref, s32[1]{0:T(128)} %bitcast.2.core_ref, bf16[85,128,128]{2,1,0:T(8,128)(2,1)} %bitcast.21, bf16[4,512,512]{2,1,0:T(8,128)(2,1)S(1)} %all-to-all-done.1.own_ref, bf16[4,512,512]{2,1,0:T(8,128)(2,1)} %copy-done.3), custom_call_target="tpu_custom_call" | custom-call | tf_op jit(solution)/shard_map/pallas_call | solution.py:163
  76.7 3.8 %all-to-all-start.2 = ((bf16[4,512,512]{2,1,0:T(8,128)(2,1)}), bf16[4,512,512]{2,1,0:T(8,128)(2,1)S(1)}, u32[]{:S(2)}, u32[]{:S(2)}) async-start(bf16[4,512,512]{2,1,0:T(8,128)(2,1)} %copy-done), calls=%async_computation.2 | async-start | bytes 4194304 | tf_op jit(solution)/shard_map/all_to_all | solution.py:126
  80.5 15.9 %collective-permute-start.5 = (f32[24,512]{1,0:T(8,128)S(1)}, f32[24,512]{1,0:T(8,128)S(1)}, u32[]{:S(2)}, u32[]{:S(2)}) collective-permute-start(f32[24,512]{1,0:T(8,128)S(1)} %add.30), channel_id=1, source_target_pairs={{0,256},{128,384},{256,0},{384,128},{1,257},{129,385},{257,1},{385... | collective-permute-start | bytes 147464 | tf_op jit(solution)/shard_map/ppermute | solution.py:130
  99.8 3.0 %collective-permute-done.6 = f32[16,512]{1,0:T(8,128)S(1)} collective-permute-done((f32[16,512]{1,0:T(8,128)S(1)}, f32[16,512]{1,0:T(8,128)S(1)}, u32[]{:S(2)}, u32[]{:S(2)}) %collective-permute-start.6) | collective-permute-done | bytes 32800 | tf_op jit(solution)/shard_map/ppermute | solution.py:130
  102.9 2.6 %collective-permute-start.7 = (f32[32,512]{1,0:T(8,128)S(1)}, f32[32,512]{1,0:T(8,128)S(1)}, u32[]{:S(2)}, u32[]{:S(2)}) collective-permute-start(f32[32,512]{1,0:T(8,128)S(1)} %pad_maximum_fusion.4), channel_id=1, source_target_pairs={{0,16},{8,24},{16,0},{24,8},{1,17},{9,25},{17,1},{25,9},{2,18},{10... | collective-permute-start | bytes 196616 | tf_op jit(solution)/shard_map/ppermute | solution.py:130
  106.6 13.6 %all-to-all-start.3 = ((bf16[4,128,512]{2,1,0:T(8,128)(2,1)}), bf16[4,128,512]{2,1,0:T(8,128)(2,1)S(1)}, u32[]{:S(2)}, u32[]{:S(2)}) async-start(bf16[4,128,512]{2,1,0:T(8,128)(2,1)} %bitcast.9), calls=%async_computation.3 | async-start | bytes 1048576 | tf_op jit(solution)/shard_map/all_to_all | solution.py:126
  120.3 6.1 %collective-permute-start.8 = (f32[72,512]{1,0:T(8,128)S(1)}, f32[72,512]{1,0:T(8,128)S(1)}, u32[]{:S(2)}, u32[]{:S(2)}) collective-permute-start(f32[72,512]{1,0:T(8,128)S(1)} %pad_maximum_fusion.3), channel_id=1, source_target_pairs={{0,2},{2,0},{4,6},{6,4},{1,3},{3,1},{5,7},{7,5},{8,10},{10,8},{12,... | collective-permute-start | bytes 442376 | tf_op jit(solution)/shard_map/ppermute | solution.py:130
  126.4 2.8 %collective-permute-done.8 = f32[72,512]{1,0:T(8,128)S(1)} collective-permute-done((f32[72,512]{1,0:T(8,128)S(1)}, f32[72,512]{1,0:T(8,128)S(1)}, u32[]{:S(2)}, u32[]{:S(2)}) %collective-permute-start.8) | collective-permute-done | bytes 147488 | tf_op jit(solution)/shard_map/ppermute | solution.py:130
  129.3 2.9 %collective-permute-start.9 = (f32[72,512]{1,0:T(8,128)S(1)}, f32[72,512]{1,0:T(8,128)S(1)}, u32[]{:S(2)}, u32[]{:S(2)}) collective-permute-start(f32[72,512]{1,0:T(8,128)S(1)} %add.34), channel_id=1, source_target_pairs={{0,4},{2,6},{4,0},{6,2},{1,5},{3,7},{5,1},{7,3},{8,12},{10,14},{12... | collective-permute-start | bytes 442376 | tf_op jit(solution)/shard_map/ppermute | solution.py:130
  132.2 4.9 %collective-permute-done.9 = f32[72,512]{1,0:T(8,128)S(1)} collective-permute-done((f32[72,512]{1,0:T(8,128)S(1)}, f32[72,512]{1,0:T(8,128)S(1)}, u32[]{:S(2)}, u32[]{:S(2)}) %collective-permute-start.9) | collective-permute-done | bytes 147488 | tf_op jit(solution)/shard_map/ppermute | solution.py:130
  139.3 3.5 %collective-permute-done.10.refs_1_ = f32[64,512]{1,0:T(8,128)S(1)} collective-permute-done((f32[64,512]{1,0:T(8,128)S(1)}, f32[64,512]{1,0:T(8,128)S(1)}, u32[]{:S(2)}, u32[]{:S(2)}) %collective-permute-start.10) | collective-permute-done | bytes 131104 | tf_op jit(solution)/shard_map/ppermute | solution.py:130
  142.9 4.5 %collective-permute-start.11 = (f32[128,512]{1,0:T(8,128)S(1)}, f32[128,512]{1,0:T(8,128)S(1)}, u32[]{:S(2)}, u32[]{:S(2)}) collective-permute-start(f32[128,512]{1,0:T(8,128)S(1)} %pad_maximum_fusion.2), channel_id=1, source_target_pairs={{0,64},{32,96},{64,0},{96,32},{1,65},{33,97},{65,1},{97,33},{2,66}... | collective-permute-start | bytes 786440 | tf_op jit(solution)/shard_map/ppermute | solution.py:130
  147.4 4.1 %collective-permute-done.11.refs_2_ = f32[128,512]{1,0:T(8,128)S(1)} collective-permute-done((f32[128,512]{1,0:T(8,128)S(1)}, f32[128,512]{1,0:T(8,128)S(1)}, u32[]{:S(2)}, u32[]{:S(2)}) %collective-permute-start.11) | collective-permute-done | bytes 262176 | tf_op jit(solution)/shard_map/ppermute | solution.py:130
  151.5 7.0 %collective-permute-start.12 = (f32[256,512]{1,0:T(8,128)S(1)}, f32[256,512]{1,0:T(8,128)S(1)}, u32[]{:S(2)}, u32[]{:S(2)}) collective-permute-start(f32[256,512]{1,0:T(8,128)S(1)} %pad_maximum_fusion.1), channel_id=1, source_target_pairs={{0,1},{1,0},{2,3},{3,2},{4,5},{5,4},{6,7},{7,6},{8,9},{9,8},{10,11... | collective-permute-start | bytes 1572872 | tf_op jit(solution)/shard_map/ppermute | solution.py:130
  (54 shorter events, 21.4 us)
Async XLA Ops:
  26.4 34.6 %all-to-all-start.1 = ((bf16[4,512,512]{2,1,0:T(8,128)(2,1)}), bf16[4,512,512]{2,1,0:T(8,128)(2,1)S(1)}, u32[]{:S(2)}, u32[]{:S(2)}) async-start(bf16[4,512,512]{2,1,0:T(8,128)(2,1)} %broadcast_in_dim.10), calls=%async_computation.1 | async-start | bytes 4194304 | tf_op jit(solution)/shard_map/all_to_all | solution.py:126
  31.1 39.8 %copy-start.2 = (s32[1,1,85]{2,1,0:T(1,128)S(1)}, s32[1,1,85]{2,1,0:T(1,128)}, u32[]{:S(2)}) copy-start(s32[1,1,85]{2,1,0:T(1,128)} %param.13) | copy-start | bytes 1024
  32.2 5.0 %collective-permute-start = (f32[72,512]{1,0:T(8,128)S(1)}, f32[72,512]{1,0:T(8,128)S(1)}, u32[]{:S(2)}, u32[]{:S(2)}) collective-permute-start(f32[72,512]{1,0:T(8,128)S(1)} %get-tuple-element.10), channel_id=1, source_target_pairs={{0,1},{1,0},{2,3},{3,2},{4,5},{5,4},{6,7},{7,6},{8,9},{9,8},{10,11... | collective-permute-start | bytes 442376 | tf_op jit(solution)/shard_map/ppermute | solution.py:130
  37.2 7.1 %collective-permute-start.1 = (f32[40,512]{1,0:T(8,128)S(1)}, f32[40,512]{1,0:T(8,128)S(1)}, u32[]{:S(2)}, u32[]{:S(2)}) collective-permute-start(f32[40,512]{1,0:T(8,128)S(1)} %concatenate.45), channel_id=1, source_target_pairs={{0,64},{32,96},{64,0},{96,32},{1,65},{33,97},{65,1},{97,33},{2,66}... | collective-permute-start | bytes 245768 | tf_op jit(solution)/shard_map/ppermute | solution.py:130
  44.3 5.1 %collective-permute-start.2 = (f32[24,512]{1,0:T(8,128)S(1)}, f32[24,512]{1,0:T(8,128)S(1)}, u32[]{:S(2)}, u32[]{:S(2)}) collective-permute-start(f32[24,512]{1,0:T(8,128)S(1)} %concatenate.46), channel_id=1, source_target_pairs={{0,32},{32,0},{64,96},{96,64},{1,33},{33,1},{65,97},{97,65},{2,34}... | collective-permute-start | bytes 147464 | tf_op jit(solution)/shard_map/ppermute | solution.py:130
  49.4 11.5 %collective-permute-start.3 = (f32[24,512]{1,0:T(8,128)S(1)}, f32[24,512]{1,0:T(8,128)S(1)}, u32[]{:S(2)}, u32[]{:S(2)}) collective-permute-start(f32[24,512]{1,0:T(8,128)S(1)} %maximum_add_fusion.1), channel_id=1, source_target_pairs={{0,128},{128,0},{256,384},{384,256},{1,129},{129,1},{257,385},{385... | collective-permute-start | bytes 147464 | tf_op jit(solution)/shard_map/ppermute | solution.py:130
  61.0 8.6 %collective-permute-start.4 = (bf16[4,512,512]{2,1,0:T(8,128)(2,1)S(1)}, bf16[4,512,512]{2,1,0:T(8,128)(2,1)S(1)}, u32[]{:S(2)}, u32[]{:S(2)}) collective-permute-start(bf16[4,512,512]{2,1,0:T(8,128)(2,1)S(1)} %all-to-all-done.1.own_ref), channel_id=1, source_target_pairs={{0,1},{1,0},{2,3},{3,2},{4,5},{5,4},{6,7},{7,6},{8,9},{9,8},{10,11... | collective-permute-start | bytes 6291464 | tf_op jit(solution)/shard_map/ppermute | solution.py:160
  69.6 1.3 copy-start.3
  75.4 1.3 copy-start
  76.7 28.8 %all-to-all-start.2 = ((bf16[4,512,512]{2,1,0:T(8,128)(2,1)}), bf16[4,512,512]{2,1,0:T(8,128)(2,1)S(1)}, u32[]{:S(2)}, u32[]{:S(2)}) async-start(bf16[4,512,512]{2,1,0:T(8,128)(2,1)} %copy-done), calls=%async_computation.2 | async-start | bytes 4194304 | tf_op jit(solution)/shard_map/all_to_all | solution.py:126
  80.5 17.4 %collective-permute-start.5 = (f32[24,512]{1,0:T(8,128)S(1)}, f32[24,512]{1,0:T(8,128)S(1)}, u32[]{:S(2)}, u32[]{:S(2)}) collective-permute-start(f32[24,512]{1,0:T(8,128)S(1)} %add.30), channel_id=1, source_target_pairs={{0,256},{128,384},{256,0},{384,128},{1,257},{129,385},{257,1},{385... | collective-permute-start | bytes 147464 | tf_op jit(solution)/shard_map/ppermute | solution.py:130
  97.9 5.0 %collective-permute-start.6 = (f32[16,512]{1,0:T(8,128)S(1)}, f32[16,512]{1,0:T(8,128)S(1)}, u32[]{:S(2)}, u32[]{:S(2)}) collective-permute-start(f32[16,512]{1,0:T(8,128)S(1)} %slice.45), channel_id=1, source_target_pairs={{0,8},{8,0},{16,24},{24,16},{1,9},{9,1},{17,25},{25,17},{2,10},{10... | collective-permute-start | bytes 98312 | tf_op jit(solution)/shard_map/ppermute | solution.py:130
  102.9 17.4 %collective-permute-start.7 = (f32[32,512]{1,0:T(8,128)S(1)}, f32[32,512]{1,0:T(8,128)S(1)}, u32[]{:S(2)}, u32[]{:S(2)}) collective-permute-start(f32[32,512]{1,0:T(8,128)S(1)} %pad_maximum_fusion.4), channel_id=1, source_target_pairs={{0,16},{8,24},{16,0},{24,8},{1,17},{9,25},{17,1},{25,9},{2,18},{10... | collective-permute-start | bytes 196616 | tf_op jit(solution)/shard_map/ppermute | solution.py:130
  106.6 52.0 %copy-start.4 = (s32[32]{0:T(128)S(1)}, s32[32]{0:T(128)}, u32[]{:S(2)}) copy-start(s32[32]{0:T(128)} %constant.21.clone) | copy-start | bytes 388
  106.6 55.0 %all-to-all-start.3 = ((bf16[4,128,512]{2,1,0:T(8,128)(2,1)}), bf16[4,128,512]{2,1,0:T(8,128)(2,1)S(1)}, u32[]{:S(2)}, u32[]{:S(2)}) async-start(bf16[4,128,512]{2,1,0:T(8,128)(2,1)} %bitcast.9), calls=%async_computation.3 | async-start | bytes 1048576 | tf_op jit(solution)/shard_map/all_to_all | solution.py:126
  120.3 8.9 %collective-permute-start.8 = (f32[72,512]{1,0:T(8,128)S(1)}, f32[72,512]{1,0:T(8,128)S(1)}, u32[]{:S(2)}, u32[]{:S(2)}) collective-permute-start(f32[72,512]{1,0:T(8,128)S(1)} %pad_maximum_fusion.3), channel_id=1, source_target_pairs={{0,2},{2,0},{4,6},{6,4},{1,3},{3,1},{5,7},{7,5},{8,10},{10,8},{12,... | collective-permute-start | bytes 442376 | tf_op jit(solution)/shard_map/ppermute | solution.py:130
  129.2 32.4 %copy-start.1 = (bf16[512,512]{1,0:T(8,128)(2,1)S(1)}, bf16[512,512]{1,0:T(8,128)(2,1)}, u32[]{:S(2)}) copy-start(bf16[512,512]{1,0:T(8,128)(2,1)} %weight_ref.1) | copy-start | bytes 1572868
  129.3 7.8 %collective-permute-start.9 = (f32[72,512]{1,0:T(8,128)S(1)}, f32[72,512]{1,0:T(8,128)S(1)}, u32[]{:S(2)}, u32[]{:S(2)}) collective-permute-start(f32[72,512]{1,0:T(8,128)S(1)} %add.34), channel_id=1, source_target_pairs={{0,4},{2,6},{4,0},{6,2},{1,5},{3,7},{5,1},{7,3},{8,12},{10,14},{12... | collective-permute-start | bytes 442376 | tf_op jit(solution)/shard_map/ppermute | solution.py:130
  137.1 5.7 %collective-permute-start.10 = (f32[64,512]{1,0:T(8,128)S(1)}, f32[64,512]{1,0:T(8,128)S(1)}, u32[]{:S(2)}, u32[]{:S(2)}) collective-permute-start(f32[64,512]{1,0:T(8,128)S(1)} %slice.47.refs_0_), channel_id=1, source_target_pairs={{0,32},{32,0},{64,96},{96,64},{1,33},{33,1},{65,97},{97,65},{2,34}... | collective-permute-start | bytes 393224 | tf_op jit(solution)/shard_map/ppermute | solution.py:130
  142.9 8.6 %collective-permute-start.11 = (f32[128,512]{1,0:T(8,128)S(1)}, f32[128,512]{1,0:T(8,128)S(1)}, u32[]{:S(2)}, u32[]{:S(2)}) collective-permute-start(f32[128,512]{1,0:T(8,128)S(1)} %pad_maximum_fusion.2), channel_id=1, source_target_pairs={{0,64},{32,96},{64,0},{96,32},{1,65},{33,97},{65,1},{97,33},{2,66}... | collective-permute-start | bytes 786440 | tf_op jit(solution)/shard_map/ppermute | solution.py:130
  151.5 8.6 %collective-permute-start.12 = (f32[256,512]{1,0:T(8,128)S(1)}, f32[256,512]{1,0:T(8,128)S(1)}, u32[]{:S(2)}, u32[]{:S(2)}) collective-permute-start(f32[256,512]{1,0:T(8,128)S(1)} %pad_maximum_fusion.1), channel_id=1, source_target_pairs={{0,1},{1,0},{2,3},{3,2},{4,5},{5,4},{6,7},{7,6},{8,9},{9,8},{10,11... | collective-permute-start | bytes 1572872 | tf_op jit(solution)/shard_map/ppermute | solution.py:130

commit v6 on v5

--- a/solution.py
+++ b/solution.py
@@ -11,7 +11,7 @@
 F32 = jnp.float32
 BF16 = jnp.bfloat16
 MARK = jax.ShapeDtypeStruct((8, 128), F32)
-VMEM_LIMIT = 48 * 1024 * 1024
+VMEM_LIMIT = 24 * 1024 * 1024
 
 
 def tile_kernel(pos_ref, live_ref, core_ref, blocks_ref, own_ref, other_ref, out_ref, mark_ref, acc_ref, low_ref, sems, *, group, n_x):
@@ -90,7 +90,7 @@
     for ref in refs[:-1]:
         for k in range(ref.shape[0] // n_slice):
             first = pl.multiple_of((index_ref[0] ^ index_ref[1 + offset]) * n_slice, n_slice)
-            out_ref[pl.ds(first, n_slice), :] = ref[k * n_slice : (k + 1) * n_slice, :]
+            out_ref[pl.ds(first, n_slice), :] = ref[k * n_slice : (k + 1) * n_slice, :].astype(F32)
             offset += 1
 
 
@@ -158,6 +158,9 @@
     terms = terms + trade(terms, "zh", 1)
     own, terms = lax.optimization_barrier((own, terms))
     other = lax.ppermute(own, "core", [(0, 1), (1, 0)])
+    terms = terms + trade(terms, "x", 1)
+    later, terms = lax.optimization_barrier((core, terms))
+    terms = terms + trade(terms, "x", 2)
     slots = adj_blocks.shape[2]
     group = max(d for d in range(1, 9) if slots % d == 0)
     sent, mark = call(
@@ -172,24 +175,21 @@
         marked=True,
         n_scalar=3,
         n_in=3,
-    )(block_pos.reshape(-1), block_live.reshape(-1), core, adj_blocks[0, 0], own, other)
-    terms, _ = lax.optimization_barrier((terms, mark))
+    )(block_pos.reshape(-1), block_live.reshape(-1), later, adj_blocks[0, 0], own, other)
+    terms, sent = lax.optimization_barrier((terms, sent))
     terms = terms + trade(terms, "zh", 2)
     factor = 1.0 / math.sqrt(blk * n_zh * n_y * n_zl * n_x * n_core)
     terms = terms * factor
-    slices, bias = terms[:n_slice], terms[n_slice:]
+    slices = terms[:n_slice].astype(BF16)
     offsets = [0]
     for bit in (1, 2):
         slices = jnp.concatenate([slices, trade(slices, "zl", bit)], axis=0)
         offsets += [o ^ (bit * n_y * n_core) for o in offsets]
-    terms = jnp.concatenate([slices, bias], axis=0)
     got = swap(sent, "y")
     sent, mark = call(fold_kernel, jax.ShapeDtypeStruct((n_zh * blk, n_feat), BF16), marked=True)(got)
-    terms, _ = lax.optimization_barrier((terms, mark))
-    for bit in (1, 2):
-        terms = terms + trade(terms, "x", bit)
-    pieces = [terms[: n_zl * n_slice]]
-    for axis, bit, stride in (("y", 1, n_core), ("y", 2, n_core), ("core", 1, 1)):
+    slices, sent = lax.optimization_barrier((slices, sent))
+    pieces = [slices]
+    for axis, bit, stride in (("y", 2, n_core), ("y", 1, n_core), ("core", 1, 1)):
         pieces.append(trade(jnp.concatenate(pieces, axis=0), axis, bit))
         offsets += [o ^ (bit * stride) for o in offsets]
     mine = lax.axis_index(("zl", "y", "core")).astype(jnp.int32)
@@ -199,7 +199,7 @@
     )
     got = swap(sent.reshape(n_zh, blk, n_feat), "zh")
     out_rows = call(last_kernel, jax.ShapeDtypeStruct((blk, n_feat), BF16), n_in=2)(got, weight)
-    return out_rows[None], grad_weight, terms[n_zl * n_slice]
+    return out_rows[None], grad_weight, terms[n_slice]
 
 
 def solution(mesh):

time: 164 us -> 160 us (0.976)
  waiting for transfers between devices: 31.6 us -> 29.4 us
    all_to_all x3, waiting for transfers between devices: 0.01 us -> 6.11 us  [swap(): return lax.all_to_all(value, axis, split_axis=0, concat_axis=0, tiled=True)]
    ppermute x12, waiting for transfers between devices: 28.4 us -> 23.3 us  [trade(): lax.ppermute(value, axis, [(i, i ^ bit) for i in range(lax.axis_size(axis...]
    ppermute x1, waiting for transfers between devices: 3.12 us -> 0.01 us  [body(): other = lax.ppermute(own, 'core', [(0, 1), (1, 0)])]
    ppermute x12, starting transfers between devices: 64.1 us -> 62 us  [trade(): lax.ppermute(value, axis, [(i, i ^ bit) for i in range(lax.axis_size(axis...]
    all_to_all x3, starting transfers between devices: 22.2 us -> 23.9 us  [swap(): return lax.all_to_all(value, axis, split_axis=0, concat_axis=0, tiled=True)]
  transfers between devices with their start and end apart: 16 -> 16, of which waited for: 12 -> 13; matrix products, arithmetic and copies ran while one was open for 1% -> 1% of each run, Pallas kernels for 2% -> 2%
where the time goes in v6:
time: 160 us; the launch traced here: 159 us
  starting transfers between devices  90.7 us (57%)
  waiting for transfers between devices  29.4 us (18%)
  blocking collectives  22 us (14%)
  Pallas kernels  7.68 us (5%)
  local copies, waits for them, and re-layouts  6.34 us (4%)
  between operations  1.6 us (1%)
    ppermute x12, starting transfers between devices, trade(): lax.ppermute(value, axis, [(i, i ^ bit) for i in range(lax.axis_size(axis...  62 us
    all_to_all x3, starting transfers between devices, swap(): return lax.all_to_all(value, axis, split_axis=0, concat_axis=0, tiled=True)  23.9 us
    ppermute x12, waiting for transfers between devices, trade(): lax.ppermute(value, axis, [(i, i ^ bit) for i in range(lax.axis_size(axis...  23.3 us
    all_to_all x1, blocking collectives, swap(): return lax.all_to_all(value, axis, split_axis=0, concat_axis=0, tiled=True)  22 us
    all_to_all x3, waiting for transfers between devices, swap(): return lax.all_to_all(value, axis, split_axis=0, concat_axis=0, tiled=True)  6.11 us
    ppermute x1, starting transfers between devices, body(): other = lax.ppermute(own, 'core', [(0, 1), (1, 0)])  4.83 us
    unnamed x11, local copies, waits for them, and re-layouts  4.14 us
  transfers between devices with their start and end apart: 16, of which 13 were waited for; matrix products, arithmetic and copies ran while one was open for 1% of the time, Pallas kernels for 2%

profile of v6, /device:TPU:1, one launch (start us, length us, event | category | flops | bytes accessed | tf_op | source)
XLA Modules:
  0.0 159.1 jit_solution(9220595486730649655)
XLA Ops:
  2.8 22.0 %all_to_all.20.got_ref = bf16[4,160,512]{2,1,0:T(8,128)(2,1)S(1)} all-to-all(bf16[4,160,512]{2,1,0:T(8,128)(2,1)S(1)} %pad_maximum_fusion), channel_id=1, replica_groups=mesh['zh'=4,'y'=4,'zl'=4,'x'=4,'core'=2] {'zl'}, dimensions={0} | all-to-all | bytes 1310720 | tf_op jit(solution)/shard_map/all_to_all | solution.py:126
  26.4 4.7 %all-to-all-start.1 = ((bf16[4,512,512]{2,1,0:T(8,128)(2,1)}), bf16[4,512,512]{2,1,0:T(8,128)(2,1)S(1)}, u32[]{:S(2)}, u32[]{:S(2)}) async-start(bf16[4,512,512]{2,1,0:T(8,128)(2,1)} %broadcast_in_dim.10), calls=%async_computation.1 | async-start | bytes 4194304 | tf_op jit(solution)/shard_map/all_to_all | solution.py:126
  32.2 4.0 %collective-permute-start = (f32[72,512]{1,0:T(8,128)S(1)}, f32[72,512]{1,0:T(8,128)S(1)}, u32[]{:S(2)}, u32[]{:S(2)}) collective-permute-start(f32[72,512]{1,0:T(8,128)S(1)} %get-tuple-element.16), channel_id=1, source_target_pairs={{0,1},{1,0},{2,3},{3,2},{4,5},{5,4},{6,7},{7,6},{8,9},{9,8},{10,11... | collective-permute-start | bytes 442376 | tf_op jit(solution)/shard_map/ppermute | solution.py:130
  37.2 4.8 %collective-permute-start.1 = (f32[40,512]{1,0:T(8,128)S(1)}, f32[40,512]{1,0:T(8,128)S(1)}, u32[]{:S(2)}, u32[]{:S(2)}) collective-permute-start(f32[40,512]{1,0:T(8,128)S(1)} %concatenate.45), channel_id=1, source_target_pairs={{0,64},{32,96},{64,0},{96,32},{1,65},{33,97},{65,1},{97,33},{2,66}... | collective-permute-start | bytes 245768 | tf_op jit(solution)/shard_map/ppermute | solution.py:130
  42.1 2.2 %collective-permute-done.1 = f32[40,512]{1,0:T(8,128)S(1)} collective-permute-done((f32[40,512]{1,0:T(8,128)S(1)}, f32[40,512]{1,0:T(8,128)S(1)}, u32[]{:S(2)}, u32[]{:S(2)}) %collective-permute-start.1) | collective-permute-done | bytes 81952 | tf_op jit(solution)/shard_map/ppermute | solution.py:130
  44.3 3.2 %collective-permute-start.2 = (f32[24,512]{1,0:T(8,128)S(1)}, f32[24,512]{1,0:T(8,128)S(1)}, u32[]{:S(2)}, u32[]{:S(2)}) collective-permute-start(f32[24,512]{1,0:T(8,128)S(1)} %concatenate.46), channel_id=1, source_target_pairs={{0,32},{32,0},{64,96},{96,64},{1,33},{33,1},{65,97},{97,65},{2,34}... | collective-permute-start | bytes 147464 | tf_op jit(solution)/shard_map/ppermute | solution.py:130
  49.4 8.8 %collective-permute-start.3 = (f32[24,512]{1,0:T(8,128)S(1)}, f32[24,512]{1,0:T(8,128)S(1)}, u32[]{:S(2)}, u32[]{:S(2)}) collective-permute-start(f32[24,512]{1,0:T(8,128)S(1)} %maximum_add_fusion.1), channel_id=1, source_target_pairs={{0,128},{128,0},{256,384},{384,256},{1,129},{129,1},{257,385},{385... | collective-permute-start | bytes 147464 | tf_op jit(solution)/shard_map/ppermute | solution.py:130
  58.3 2.7 %collective-permute-done.3 = f32[24,512]{1,0:T(8,128)S(1)} collective-permute-done((f32[24,512]{1,0:T(8,128)S(1)}, f32[24,512]{1,0:T(8,128)S(1)}, u32[]{:S(2)}, u32[]{:S(2)}) %collective-permute-start.3) | collective-permute-done | bytes 49184 | tf_op jit(solution)/shard_map/ppermute | solution.py:130
  61.0 4.8 %collective-permute-start.6 = (bf16[4,512,512]{2,1,0:T(8,128)(2,1)S(1)}, bf16[4,512,512]{2,1,0:T(8,128)(2,1)S(1)}, u32[]{:S(2)}, u32[]{:S(2)}) collective-permute-start(bf16[4,512,512]{2,1,0:T(8,128)(2,1)S(1)} %all-to-all-done.1.own_ref), channel_id=1, source_target_pairs={{0,1},{1,0},{2,3},{3,2},{4,5},{5,4},{6,7},{7,6},{8,9},{9,8},{10,11... | collective-permute-start | bytes 6291464 | tf_op jit(solution)/shard_map/ppermute | solution.py:160
  65.8 3.7 %collective-permute-start.4 = (f32[24,512]{1,0:T(8,128)S(1)}, f32[24,512]{1,0:T(8,128)S(1)}, u32[]{:S(2)}, u32[]{:S(2)}) collective-permute-start(f32[24,512]{1,0:T(8,128)S(1)} %add.30), channel_id=1, source_target_pairs={{0,2},{2,0},{4,6},{6,4},{1,3},{3,1},{5,7},{7,5},{8,10},{10,8},{12,... | collective-permute-start | bytes 147464 | tf_op jit(solution)/shard_map/ppermute | solution.py:130
  69.5 2.1 %collective-permute-done.4 = f32[24,512]{1,0:T(8,128)S(1)} collective-permute-done((f32[24,512]{1,0:T(8,128)S(1)}, f32[24,512]{1,0:T(8,128)S(1)}, u32[]{:S(2)}, u32[]{:S(2)}) %collective-permute-start.4) | collective-permute-done | bytes 49184 | tf_op jit(solution)/shard_map/ppermute | solution.py:130
  71.6 4.7 %collective-permute-start.5 = (f32[24,512]{1,0:T(8,128)S(1)}, f32[24,512]{1,0:T(8,128)S(1)}, u32[]{:S(2)}, u32[]{:S(2)}) collective-permute-start(f32[24,512]{1,0:T(8,128)S(1)} %add.31), channel_id=1, source_target_pairs={{0,4},{2,6},{4,0},{6,2},{1,5},{3,7},{5,1},{7,3},{8,12},{10,14},{12... | collective-permute-start | bytes 147464 | tf_op jit(solution)/shard_map/ppermute | solution.py:130
  79.7 2.9 %shard_map.104 = (bf16[4,512,512]{2,1,0:T(8,128)(2,1)S(1)}, f32[8,128]{1,0:T(8,128)}) custom-call(s32[85]{0:T(128)S(1)} %bitcast.21, s32[1]{0:T(128)} %bitcast.19.live_ref, s32[1]{0:T(128)} %bitcast.core_ref, bf16[85,128,128]{2,1,0:T(8,128)(2,1)S(1)} %bitcast.20, bf16[4,512,512]{2,1,0:T(8,128)(2,1)S(1)} %all-to-all-done.1.own_ref, ...), custom_call_target="tpu_custom_call" | custom-call | tf_op jit(solution)/shard_map/pallas_call | solution.py:166
  84.0 6.5 %all-to-all-start.2 = ((bf16[4,512,512]{2,1,0:T(8,128)(2,1)}), bf16[4,512,512]{2,1,0:T(8,128)(2,1)S(1)}, u32[]{:S(2)}, u32[]{:S(2)}) async-start(bf16[4,512,512]{2,1,0:T(8,128)(2,1)} %copy-done.1), calls=%async_computation.2 | async-start | bytes 4194304 | tf_op jit(solution)/shard_map/all_to_all | solution.py:126
  90.5 12.7 %collective-permute-start.7 = (f32[24,512]{1,0:T(8,128)S(1)}, f32[24,512]{1,0:T(8,128)S(1)}, u32[]{:S(2)}, u32[]{:S(2)}) collective-permute-start(f32[24,512]{1,0:T(8,128)S(1)} %add.32), channel_id=1, source_target_pairs={{0,256},{128,384},{256,0},{384,128},{1,257},{129,385},{257,1},{385... | collective-permute-start | bytes 147464 | tf_op jit(solution)/shard_map/ppermute | solution.py:130
  106.8 2.8 %collective-permute-done.8 = bf16[16,512]{1,0:T(8,128)(2,1)S(1)} collective-permute-done((bf16[16,512]{1,0:T(8,128)(2,1)S(1)}, bf16[16,512]{1,0:T(8,128)(2,1)S(1)}, u32[]{:S(2)}, u32[]{:S(2)}) %collective-permute-start.8) | collective-permute-done | bytes 16416 | tf_op jit(solution)/shard_map/ppermute | solution.py:130
  109.7 2.7 %collective-permute-start.9 = (bf16[32,512]{1,0:T(8,128)(2,1)S(1)}, bf16[32,512]{1,0:T(8,128)(2,1)S(1)}, u32[]{:S(2)}, u32[]{:S(2)}) collective-permute-start(bf16[32,512]{1,0:T(8,128)(2,1)S(1)} %pad_maximum_fusion.4), channel_id=1, source_target_pairs={{0,16},{8,24},{16,0},{24,8},{1,17},{9,25},{17,1},{25,9},{2,18},{10... | collective-permute-start | bytes 98312 | tf_op jit(solution)/shard_map/ppermute | solution.py:130
  112.4 3.2 %collective-permute-done.9 = bf16[32,512]{1,0:T(8,128)(2,1)S(1)} collective-permute-done((bf16[32,512]{1,0:T(8,128)(2,1)S(1)}, bf16[32,512]{1,0:T(8,128)(2,1)S(1)}, u32[]{:S(2)}, u32[]{:S(2)}) %collective-permute-start.9) | collective-permute-done | bytes 32800 | tf_op jit(solution)/shard_map/ppermute | solution.py:130
  116.6 12.7 %all-to-all-start.3 = ((bf16[4,128,512]{2,1,0:T(8,128)(2,1)}), bf16[4,128,512]{2,1,0:T(8,128)(2,1)S(1)}, u32[]{:S(2)}, u32[]{:S(2)}) async-start(bf16[4,128,512]{2,1,0:T(8,128)(2,1)} %bitcast.9), calls=%async_computation.3 | async-start | bytes 1048576 | tf_op jit(solution)/shard_map/all_to_all | solution.py:126
  129.4 4.8 %collective-permute-start.10 = (bf16[64,512]{1,0:T(8,128)(2,1)S(1)}, bf16[64,512]{1,0:T(8,128)(2,1)S(1)}, u32[]{:S(2)}, u32[]{:S(2)}) collective-permute-start(bf16[64,512]{1,0:T(8,128)(2,1)S(1)} %pad_maximum_fusion.3.refs_0_), channel_id=1, source_target_pairs={{0,64},{32,96},{64,0},{96,32},{1,65},{33,97},{65,1},{97,33},{2,66}... | collective-permute-start | bytes 196616 | tf_op jit(solution)/shard_map/ppermute | solution.py:130
  135.9 3.5 %collective-permute-start.11 = (bf16[128,512]{1,0:T(8,128)(2,1)S(1)}, bf16[128,512]{1,0:T(8,128)(2,1)S(1)}, u32[]{:S(2)}, u32[]{:S(2)}) collective-permute-start(bf16[128,512]{1,0:T(8,128)(2,1)S(1)} %pad_maximum_fusion.2), channel_id=1, source_target_pairs={{0,32},{32,0},{64,96},{96,64},{1,33},{33,1},{65,97},{97,65},{2,34}... | collective-permute-start | bytes 393224 | tf_op jit(solution)/shard_map/ppermute | solution.py:130
  139.4 2.6 %collective-permute-done.11.refs_2_ = bf16[128,512]{1,0:T(8,128)(2,1)S(1)} collective-permute-done((bf16[128,512]{1,0:T(8,128)(2,1)S(1)}, bf16[128,512]{1,0:T(8,128)(2,1)S(1)}, u32[]{:S(2)}, u32[]{:S(2)}) %collective-permute-start.11) | collective-permute-done | bytes 131104 | tf_op jit(solution)/shard_map/ppermute | solution.py:130
  142.0 7.1 %collective-permute-start.12 = (bf16[256,512]{1,0:T(8,128)(2,1)S(1)}, bf16[256,512]{1,0:T(8,128)(2,1)S(1)}, u32[]{:S(2)}, u32[]{:S(2)}) collective-permute-start(bf16[256,512]{1,0:T(8,128)(2,1)S(1)} %pad_maximum_fusion.1), channel_id=1, source_target_pairs={{0,1},{1,0},{2,3},{3,2},{4,5},{5,4},{6,7},{7,6},{8,9},{9,8},{10,11... | collective-permute-start | bytes 786440 | tf_op jit(solution)/shard_map/ppermute | solution.py:130
  151.9 6.1 %all-to-all-done.3.in_ref = bf16[4,128,512]{2,1,0:T(8,128)(2,1)S(1)} async-done(((bf16[4,128,512]{2,1,0:T(8,128)(2,1)}), bf16[4,128,512]{2,1,0:T(8,128)(2,1)S(1)}, u32[]{:S(2)}, u32[]{:S(2)}) %all-to-all-start.3) | async-done | bytes 524320 | tf_op jit(solution)/shard_map/all_to_all | solution.py:126
  (52 shorter events, 22.1 us)
Async XLA Ops:
  26.4 34.6 %all-to-all-start.1 = ((bf16[4,512,512]{2,1,0:T(8,128)(2,1)}), bf16[4,512,512]{2,1,0:T(8,128)(2,1)S(1)}, u32[]{:S(2)}, u32[]{:S(2)}) async-start(bf16[4,512,512]{2,1,0:T(8,128)(2,1)} %broadcast_in_dim.10), calls=%async_computation.1 | async-start | bytes 4194304 | tf_op jit(solution)/shard_map/all_to_all | solution.py:126
  31.1 46.9 %copy-start.3 = (s32[1,1,85]{2,1,0:T(1,128)S(1)}, s32[1,1,85]{2,1,0:T(1,128)}, u32[]{:S(2)}) copy-start(s32[1,1,85]{2,1,0:T(1,128)} %param.13) | copy-start | bytes 1024
  32.2 5.0 %collective-permute-start = (f32[72,512]{1,0:T(8,128)S(1)}, f32[72,512]{1,0:T(8,128)S(1)}, u32[]{:S(2)}, u32[]{:S(2)}) collective-permute-start(f32[72,512]{1,0:T(8,128)S(1)} %get-tuple-element.16), channel_id=1, source_target_pairs={{0,1},{1,0},{2,3},{3,2},{4,5},{5,4},{6,7},{7,6},{8,9},{9,8},{10,11... | collective-permute-start | bytes 442376 | tf_op jit(solution)/shard_map/ppermute | solution.py:130
  37.2 7.1 %collective-permute-start.1 = (f32[40,512]{1,0:T(8,128)S(1)}, f32[40,512]{1,0:T(8,128)S(1)}, u32[]{:S(2)}, u32[]{:S(2)}) collective-permute-start(f32[40,512]{1,0:T(8,128)S(1)} %concatenate.45), channel_id=1, source_target_pairs={{0,64},{32,96},{64,0},{96,32},{1,65},{33,97},{65,1},{97,33},{2,66}... | collective-permute-start | bytes 245768 | tf_op jit(solution)/shard_map/ppermute | solution.py:130
  44.3 5.1 %collective-permute-start.2 = (f32[24,512]{1,0:T(8,128)S(1)}, f32[24,512]{1,0:T(8,128)S(1)}, u32[]{:S(2)}, u32[]{:S(2)}) collective-permute-start(f32[24,512]{1,0:T(8,128)S(1)} %concatenate.46), channel_id=1, source_target_pairs={{0,32},{32,0},{64,96},{96,64},{1,33},{33,1},{65,97},{97,65},{2,34}... | collective-permute-start | bytes 147464 | tf_op jit(solution)/shard_map/ppermute | solution.py:130
  49.4 11.5 %collective-permute-start.3 = (f32[24,512]{1,0:T(8,128)S(1)}, f32[24,512]{1,0:T(8,128)S(1)}, u32[]{:S(2)}, u32[]{:S(2)}) collective-permute-start(f32[24,512]{1,0:T(8,128)S(1)} %maximum_add_fusion.1), channel_id=1, source_target_pairs={{0,128},{128,0},{256,384},{384,256},{1,129},{129,1},{257,385},{385... | collective-permute-start | bytes 147464 | tf_op jit(solution)/shard_map/ppermute | solution.py:130
  61.0 16.9 %collective-permute-start.6 = (bf16[4,512,512]{2,1,0:T(8,128)(2,1)S(1)}, bf16[4,512,512]{2,1,0:T(8,128)(2,1)S(1)}, u32[]{:S(2)}, u32[]{:S(2)}) collective-permute-start(bf16[4,512,512]{2,1,0:T(8,128)(2,1)S(1)} %all-to-all-done.1.own_ref), channel_id=1, source_target_pairs={{0,1},{1,0},{2,3},{3,2},{4,5},{5,4},{6,7},{7,6},{8,9},{9,8},{10,11... | collective-permute-start | bytes 6291464 | tf_op jit(solution)/shard_map/ppermute | solution.py:160
  65.8 5.7 %collective-permute-start.4 = (f32[24,512]{1,0:T(8,128)S(1)}, f32[24,512]{1,0:T(8,128)S(1)}, u32[]{:S(2)}, u32[]{:S(2)}) collective-permute-start(f32[24,512]{1,0:T(8,128)S(1)} %add.30), channel_id=1, source_target_pairs={{0,2},{2,0},{4,6},{6,4},{1,3},{3,1},{5,7},{7,5},{8,10},{10,8},{12,... | collective-permute-start | bytes 147464 | tf_op jit(solution)/shard_map/ppermute | solution.py:130
  71.6 6.3 %collective-permute-start.5 = (f32[24,512]{1,0:T(8,128)S(1)}, f32[24,512]{1,0:T(8,128)S(1)}, u32[]{:S(2)}, u32[]{:S(2)}) collective-permute-start(f32[24,512]{1,0:T(8,128)S(1)} %add.31), channel_id=1, source_target_pairs={{0,4},{2,6},{4,0},{6,2},{1,5},{3,7},{5,1},{7,3},{8,12},{10,14},{12... | collective-permute-start | bytes 147464 | tf_op jit(solution)/shard_map/ppermute | solution.py:130
  77.9 1.8 %copy-start = (bf16[1,1,85,128,128]{4,3,2,1,0:T(8,128)(2,1)S(1)}, bf16[1,1,85,128,128]{4,3,2,1,0:T(8,128)(2,1)}, u32[]{:S(2)}) copy-start(bf16[1,1,85,128,128]{4,3,2,1,0:T(8,128)(2,1)} %param.12) | copy-start | bytes 8355844
  82.6 1.3 copy-start.1
  84.0 31.6 %all-to-all-start.2 = ((bf16[4,512,512]{2,1,0:T(8,128)(2,1)}), bf16[4,512,512]{2,1,0:T(8,128)(2,1)S(1)}, u32[]{:S(2)}, u32[]{:S(2)}) async-start(bf16[4,512,512]{2,1,0:T(8,128)(2,1)} %copy-done.1), calls=%async_computation.2 | async-start | bytes 4194304 | tf_op jit(solution)/shard_map/all_to_all | solution.py:126
  90.5 14.4 %collective-permute-start.7 = (f32[24,512]{1,0:T(8,128)S(1)}, f32[24,512]{1,0:T(8,128)S(1)}, u32[]{:S(2)}, u32[]{:S(2)}) collective-permute-start(f32[24,512]{1,0:T(8,128)S(1)} %add.32), channel_id=1, source_target_pairs={{0,256},{128,384},{256,0},{384,128},{1,257},{129,385},{257,1},{385... | collective-permute-start | bytes 147464 | tf_op jit(solution)/shard_map/ppermute | solution.py:130
  104.8 44.3 %copy-start.4 = (s32[32]{0:T(128)S(1)}, s32[32]{0:T(128)}, u32[]{:S(2)}) copy-start(s32[32]{0:T(128)} %constant.21.clone) | copy-start | bytes 388
  104.9 4.8 %collective-permute-start.8 = (bf16[16,512]{1,0:T(8,128)(2,1)S(1)}, bf16[16,512]{1,0:T(8,128)(2,1)S(1)}, u32[]{:S(2)}, u32[]{:S(2)}) collective-permute-start(bf16[16,512]{1,0:T(8,128)(2,1)S(1)} %slice.41), channel_id=1, source_target_pairs={{0,8},{8,0},{16,24},{24,16},{1,9},{9,1},{17,25},{25,17},{2,10},{10... | collective-permute-start | bytes 49160 | tf_op jit(solution)/shard_map/ppermute | solution.py:130
  109.7 5.9 %collective-permute-start.9 = (bf16[32,512]{1,0:T(8,128)(2,1)S(1)}, bf16[32,512]{1,0:T(8,128)(2,1)S(1)}, u32[]{:S(2)}, u32[]{:S(2)}) collective-permute-start(bf16[32,512]{1,0:T(8,128)(2,1)S(1)} %pad_maximum_fusion.4), channel_id=1, source_target_pairs={{0,16},{8,24},{16,0},{24,8},{1,17},{9,25},{17,1},{25,9},{2,18},{10... | collective-permute-start | bytes 98312 | tf_op jit(solution)/shard_map/ppermute | solution.py:130
  116.6 41.3 %copy-start.2 = (bf16[512,512]{1,0:T(8,128)(2,1)S(1)}, bf16[512,512]{1,0:T(8,128)(2,1)}, u32[]{:S(2)}) copy-start(bf16[512,512]{1,0:T(8,128)(2,1)} %weight_ref.1) | copy-start | bytes 1572868
  116.6 41.3 %all-to-all-start.3 = ((bf16[4,128,512]{2,1,0:T(8,128)(2,1)}), bf16[4,128,512]{2,1,0:T(8,128)(2,1)S(1)}, u32[]{:S(2)}, u32[]{:S(2)}) async-start(bf16[4,128,512]{2,1,0:T(8,128)(2,1)} %bitcast.9), calls=%async_computation.3 | async-start | bytes 1048576 | tf_op jit(solution)/shard_map/all_to_all | solution.py:126
  129.4 6.5 %collective-permute-start.10 = (bf16[64,512]{1,0:T(8,128)(2,1)S(1)}, bf16[64,512]{1,0:T(8,128)(2,1)S(1)}, u32[]{:S(2)}, u32[]{:S(2)}) collective-permute-start(bf16[64,512]{1,0:T(8,128)(2,1)S(1)} %pad_maximum_fusion.3.refs_0_), channel_id=1, source_target_pairs={{0,64},{32,96},{64,0},{96,32},{1,65},{33,97},{65,1},{97,33},{2,66}... | collective-permute-start | bytes 196616 | tf_op jit(solution)/shard_map/ppermute | solution.py:130
  135.9 6.1 %collective-permute-start.11 = (bf16[128,512]{1,0:T(8,128)(2,1)S(1)}, bf16[128,512]{1,0:T(8,128)(2,1)S(1)}, u32[]{:S(2)}, u32[]{:S(2)}) collective-permute-start(bf16[128,512]{1,0:T(8,128)(2,1)S(1)} %pad_maximum_fusion.2), channel_id=1, source_target_pairs={{0,32},{32,0},{64,96},{96,64},{1,33},{33,1},{65,97},{97,65},{2,34}... | collective-permute-start | bytes 393224 | tf_op jit(solution)/shard_map/ppermute | solution.py:130
  142.0 8.3 %collective-permute-start.12 = (bf16[256,512]{1,0:T(8,128)(2,1)S(1)}, bf16[256,512]{1,0:T(8,128)(2,1)S(1)}, u32[]{:S(2)}, u32[]{:S(2)}) collective-permute-start(bf16[256,512]{1,0:T(8,128)(2,1)S(1)} %pad_maximum_fusion.1), channel_id=1, source_target_pairs={{0,1},{1,0},{2,3},{3,2},{4,5},{5,4},{6,7},{7,6},{8,9},{9,8},{10,11... | collective-permute-start | bytes 786440 | tf_op jit(solution)/shard_map/ppermute | solution.py:130

commit v7 on v6

--- a/solution.py
+++ b/solution.py
@@ -106,7 +106,7 @@
     rows_ref[...] = product.astype(BF16)
 
 
-def call(kernel, out_shape, scratch=(), n_scalar=0, n_in=1, marked=False, out_space=pltpu.VMEM):
+def call(kernel, out_shape, scratch=(), n_scalar=0, n_in=1, marked=False, out_space=pltpu.VMEM, cost=None):
     smem = pl.BlockSpec(memory_space=pltpu.SMEM)
     vmem = pl.BlockSpec(memory_space=pltpu.VMEM)
     out_specs = jax.tree.map(lambda _: pl.BlockSpec(memory_space=out_space), out_shape)
@@ -118,6 +118,7 @@
         in_specs=[smem] * n_scalar + [vmem] * n_in,
         out_specs=out_specs,
         scratch_shapes=list(scratch),
+        cost_estimate=cost,
         compiler_params=pltpu.CompilerParams(vmem_limit_bytes=VMEM_LIMIT),
     )
 
@@ -155,12 +156,9 @@
     for bit, n in ((2, 2 * n_slice), (1, n_slice)):
         kept, away, bias = terms[:n], terms[n : 2 * n], terms[2 * n :]
         terms = jnp.concatenate([kept, bias], axis=0) + trade(jnp.concatenate([away, bias], axis=0), "y", bit)
-    terms = terms + trade(terms, "zh", 1)
     own, terms = lax.optimization_barrier((own, terms))
     other = lax.ppermute(own, "core", [(0, 1), (1, 0)])
-    terms = terms + trade(terms, "x", 1)
-    later, terms = lax.optimization_barrier((core, terms))
-    terms = terms + trade(terms, "x", 2)
+    terms = swap(jnp.broadcast_to(terms, (n_zh,) + terms.shape), "zh")
     slots = adj_blocks.shape[2]
     group = max(d for d in range(1, 9) if slots % d == 0)
     sent, mark = call(
@@ -173,11 +171,18 @@
         ],
         out_space=pltpu.HBM,
         marked=True,
+        cost=pl.CostEstimate(
+            flops=2 * slots * blk * blk * n_feat,
+            transcendentals=0,
+            bytes_accessed=8 * slots * blk * n_feat,
+        ),
         n_scalar=3,
         n_in=3,
-    )(block_pos.reshape(-1), block_live.reshape(-1), later, adj_blocks[0, 0], own, other)
+    )(block_pos.reshape(-1), block_live.reshape(-1), core, adj_blocks[0, 0], own, other)
     terms, sent = lax.optimization_barrier((terms, sent))
-    terms = terms + trade(terms, "zh", 2)
+    terms = terms.sum(axis=0)
+    for bit in (1, 2):
+        terms = terms + trade(terms, "x", bit)
     factor = 1.0 / math.sqrt(blk * n_zh * n_y * n_zl * n_x * n_core)
     terms = terms * factor
     slices = terms[:n_slice].astype(BF16)

time: 160 us -> 156 us (0.975)
  the two profiles are of different devices: /device:TPU:1 before, /device:TPU:33 now
where the time goes in v7:
time: 156 us; the launch traced here: 155 us
  starting transfers between devices  69.1 us (44%)
  waiting for transfers between devices  47.9 us (31%)
  blocking collectives  19.3 us (12%)
  Pallas kernels  9.11 us (6%)
  local copies, waits for them, and re-layouts  7.06 us (5%)
  between operations  1.58 us (1%)
    ppermute x10, starting transfers between devices, trade(): lax.ppermute(value, axis, [(i, i ^ bit) for i in range(lax.axis_size(axis...  33.5 us
    all_to_all x4, starting transfers between devices, swap(): return lax.all_to_all(value, axis, split_axis=0, concat_axis=0, tiled=True)  30.3 us
    ppermute x10, waiting for transfers between devices, trade(): lax.ppermute(value, axis, [(i, i ^ bit) for i in range(lax.axis_size(axis...  25.7 us
    all_to_all x4, waiting for transfers between devices, swap(): return lax.all_to_all(value, axis, split_axis=0, concat_axis=0, tiled=True)  22.3 us
    all_to_all x1, blocking collectives, swap(): return lax.all_to_all(value, axis, split_axis=0, concat_axis=0, tiled=True)  19.3 us
    ppermute x1, starting transfers between devices, body(): other = lax.ppermute(own, 'core', [(0, 1), (1, 0)])  5.26 us
    pallas_call x1, Pallas kernels, body(): call(functools.partial(tile_kernel, group=group, n_x=n_x), jax.ShapeDtype...  4.32 us
    unnamed x11, local copies, waits for them, and re-layouts  4.15 us
  transfers between devices with their start and end apart: 15, of which 14 were waited for; matrix products, arithmetic and copies ran while one was open for 1% of the time, Pallas kernels for 4%

profile of v7, /device:TPU:33, one launch (start us, length us, event | category | flops | bytes accessed | tf_op | source)
XLA Modules:
  0.0 155.5 jit_solution(11158986605600521826)
XLA Ops:
  2.8 19.3 %all_to_all.25.got_ref = bf16[4,160,512]{2,1,0:T(8,128)(2,1)S(1)} all-to-all(bf16[4,160,512]{2,1,0:T(8,128)(2,1)S(1)} %pad_maximum_fusion), channel_id=1, replica_groups=mesh['zh'=4,'y'=4,'zl'=4,'x'=4,'core'=2] {'zl'}, dimensions={0} | all-to-all | bytes 1310720 | tf_op jit(solution)/shard_map/all_to_all | solution.py:127
  23.7 4.5 %all-to-all-start.1 = ((bf16[4,512,512]{2,1,0:T(8,128)(2,1)}), bf16[4,512,512]{2,1,0:T(8,128)(2,1)S(1)}, u32[]{:S(2)}, u32[]{:S(2)}) async-start(bf16[4,512,512]{2,1,0:T(8,128)(2,1)} %broadcast_in_dim.13), calls=%async_computation.1 | async-start | bytes 4194304 | tf_op jit(solution)/shard_map/all_to_all | solution.py:127
  29.3 4.3 %collective-permute-start = (f32[72,512]{1,0:T(8,128)S(1)}, f32[72,512]{1,0:T(8,128)S(1)}, u32[]{:S(2)}, u32[]{:S(2)}) collective-permute-start(f32[72,512]{1,0:T(8,128)S(1)} %get-tuple-element.14), channel_id=1, source_target_pairs={{0,1},{1,0},{2,3},{3,2},{4,5},{5,4},{6,7},{7,6},{8,9},{9,8},{10,11... | collective-permute-start | bytes 442376 | tf_op jit(solution)/shard_map/ppermute | solution.py:131
  34.7 4.8 %collective-permute-start.1 = (f32[40,512]{1,0:T(8,128)S(1)}, f32[40,512]{1,0:T(8,128)S(1)}, u32[]{:S(2)}, u32[]{:S(2)}) collective-permute-start(f32[40,512]{1,0:T(8,128)S(1)} %concatenate.45), channel_id=1, source_target_pairs={{0,64},{32,96},{64,0},{96,32},{1,65},{33,97},{65,1},{97,33},{2,66}... | collective-permute-start | bytes 245768 | tf_op jit(solution)/shard_map/ppermute | solution.py:131
  39.5 2.2 %collective-permute-done.1 = f32[40,512]{1,0:T(8,128)S(1)} collective-permute-done((f32[40,512]{1,0:T(8,128)S(1)}, f32[40,512]{1,0:T(8,128)S(1)}, u32[]{:S(2)}, u32[]{:S(2)}) %collective-permute-start.1) | collective-permute-done | bytes 81952 | tf_op jit(solution)/shard_map/ppermute | solution.py:131
  41.8 3.2 %collective-permute-start.2 = (f32[24,512]{1,0:T(8,128)S(1)}, f32[24,512]{1,0:T(8,128)S(1)}, u32[]{:S(2)}, u32[]{:S(2)}) collective-permute-start(f32[24,512]{1,0:T(8,128)S(1)} %concatenate.46), channel_id=1, source_target_pairs={{0,32},{32,0},{64,96},{96,64},{1,33},{33,1},{65,97},{97,65},{2,34}... | collective-permute-start | bytes 147464 | tf_op jit(solution)/shard_map/ppermute | solution.py:131
  46.9 5.2 %all-to-all-done.1.own_ref = bf16[4,512,512]{2,1,0:T(8,128)(2,1)S(1)} async-done(((bf16[4,512,512]{2,1,0:T(8,128)(2,1)}), bf16[4,512,512]{2,1,0:T(8,128)(2,1)S(1)}, u32[]{:S(2)}, u32[]{:S(2)}) %all-to-all-start.1) | async-done | bytes 2097184 | tf_op jit(solution)/shard_map/all_to_all | solution.py:127
  52.1 5.3 %collective-permute-start.3 = (bf16[4,512,512]{2,1,0:T(8,128)(2,1)S(1)}, bf16[4,512,512]{2,1,0:T(8,128)(2,1)}, u32[]{:S(2)}, u32[]{:S(2)}) collective-permute-start(bf16[4,512,512]{2,1,0:T(8,128)(2,1)S(1)} %all-to-all-done.1.own_ref), channel_id=1, source_target_pairs={{0,1},{1,0},{2,3},{3,2},{4,5},{5,4},{6,7},{7,6},{8,9},{9,8},{10,11... | collective-permute-start | bytes 6291464 | tf_op jit(solution)/shard_map/ppermute | solution.py:160
  58.1 12.1 %all-to-all-start.2 = ((f32[4,24,512]{2,1,0:T(8,128)}), f32[4,24,512]{2,1,0:T(8,128)S(1)}, u32[]{:S(2)}, u32[]{:S(2)}) async-start(f32[4,24,512]{2,1,0:T(8,128)} %broadcast_in_dim.14), calls=%async_computation.2 | async-start | bytes 393216 | tf_op jit(solution)/shard_map/all_to_all | solution.py:127
  72.7 4.3 %shard_map.104 = (bf16[4,512,512]{2,1,0:T(8,128)(2,1)S(1)}, f32[8,128]{1,0:T(8,128)}) custom-call(s32[85]{0:T(128)S(1)} %bitcast.21, s32[1]{0:T(128)} %bitcast.19.live_ref, s32[1]{0:T(128)} %bitcast.4.core_ref, bf16[85,128,128]{2,1,0:T(8,128)(2,1)S(1)} %bitcast.20, bf16[4,512,512]{2,1,0:T(8,128)(2,1)S(1)} %all-to-all-done.1.own_ref, ...), custom_call_target="tpu_custom_call" | custom-call | flops 1426063360 | bytes 44564480 | tf_op jit(solution)/shard_map/pallas_call | solution.py:164
  78.3 8.1 %all-to-all-done.2 = f32[4,24,512]{2,1,0:T(8,128)S(1)} async-done(((f32[4,24,512]{2,1,0:T(8,128)}), f32[4,24,512]{2,1,0:T(8,128)S(1)}, u32[]{:S(2)}, u32[]{:S(2)}) %all-to-all-start.2) | async-done | bytes 196640 | tf_op jit(solution)/shard_map/all_to_all | solution.py:127
  86.4 4.2 %all-to-all-start.3 = ((bf16[4,512,512]{2,1,0:T(8,128)(2,1)}), bf16[4,512,512]{2,1,0:T(8,128)(2,1)S(1)}, u32[]{:S(2)}, u32[]{:S(2)}) async-start(bf16[4,512,512]{2,1,0:T(8,128)(2,1)} %copy-done.1), calls=%async_computation.3 | async-start | bytes 4194304 | tf_op jit(solution)/shard_map/all_to_all | solution.py:127
  92.8 2.6 %collective-permute-done.4 = f32[24,512]{1,0:T(8,128)S(1)} collective-permute-done((f32[24,512]{1,0:T(8,128)S(1)}, f32[24,512]{1,0:T(8,128)S(1)}, u32[]{:S(2)}, u32[]{:S(2)}) %collective-permute-start.4) | collective-permute-done | bytes 49184 | tf_op jit(solution)/shard_map/ppermute | solution.py:131
  95.5 2.5 %collective-permute-start.5 = (f32[24,512]{1,0:T(8,128)S(1)}, f32[24,512]{1,0:T(8,128)S(1)}, u32[]{:S(2)}, u32[]{:S(2)}) collective-permute-start(f32[24,512]{1,0:T(8,128)S(1)} %add.24), channel_id=1, source_target_pairs={{0,4},{2,6},{4,0},{6,2},{1,5},{3,7},{5,1},{7,3},{8,12},{10,14},{12... | collective-permute-start | bytes 147464 | tf_op jit(solution)/shard_map/ppermute | solution.py:131
  98.0 3.8 %collective-permute-done.5 = f32[24,512]{1,0:T(8,128)S(1)} collective-permute-done((f32[24,512]{1,0:T(8,128)S(1)}, f32[24,512]{1,0:T(8,128)S(1)}, u32[]{:S(2)}, u32[]{:S(2)}) %collective-permute-start.5) | collective-permute-done | bytes 49184 | tf_op jit(solution)/shard_map/ppermute | solution.py:131
  103.8 2.8 %collective-permute-done.6 = bf16[16,512]{1,0:T(8,128)(2,1)S(1)} collective-permute-done((bf16[16,512]{1,0:T(8,128)(2,1)S(1)}, bf16[16,512]{1,0:T(8,128)(2,1)S(1)}, u32[]{:S(2)}, u32[]{:S(2)}) %collective-permute-start.6) | collective-permute-done | bytes 16416 | tf_op jit(solution)/shard_map/ppermute | solution.py:131
  106.6 3.1 %collective-permute-start.7 = (bf16[32,512]{1,0:T(8,128)(2,1)S(1)}, bf16[32,512]{1,0:T(8,128)(2,1)S(1)}, u32[]{:S(2)}, u32[]{:S(2)}) collective-permute-start(bf16[32,512]{1,0:T(8,128)(2,1)S(1)} %pad_maximum_fusion.4), channel_id=1, source_target_pairs={{0,16},{8,24},{16,0},{24,8},{1,17},{9,25},{17,1},{25,9},{2,18},{10... | collective-permute-start | bytes 98312 | tf_op jit(solution)/shard_map/ppermute | solution.py:131
  109.7 2.8 %collective-permute-done.7 = bf16[32,512]{1,0:T(8,128)(2,1)S(1)} collective-permute-done((bf16[32,512]{1,0:T(8,128)(2,1)S(1)}, bf16[32,512]{1,0:T(8,128)(2,1)S(1)}, u32[]{:S(2)}, u32[]{:S(2)}) %collective-permute-start.7) | collective-permute-done | bytes 32800 | tf_op jit(solution)/shard_map/ppermute | solution.py:131
  114.1 9.5 %all-to-all-start.4 = ((bf16[4,128,512]{2,1,0:T(8,128)(2,1)}), bf16[4,128,512]{2,1,0:T(8,128)(2,1)S(1)}, u32[]{:S(2)}, u32[]{:S(2)}) async-start(bf16[4,128,512]{2,1,0:T(8,128)(2,1)} %bitcast.9), calls=%async_computation.4 | async-start | bytes 1048576 | tf_op jit(solution)/shard_map/all_to_all | solution.py:127
  123.6 2.2 %collective-permute-start.8 = (bf16[64,512]{1,0:T(8,128)(2,1)S(1)}, bf16[64,512]{1,0:T(8,128)(2,1)S(1)}, u32[]{:S(2)}, u32[]{:S(2)}) collective-permute-start(bf16[64,512]{1,0:T(8,128)(2,1)S(1)} %pad_maximum_fusion.3.refs_0_), channel_id=1, source_target_pairs={{0,64},{32,96},{64,0},{96,32},{1,65},{33,97},{65,1},{97,33},{2,66}... | collective-permute-start | bytes 196616 | tf_op jit(solution)/shard_map/ppermute | solution.py:131
  125.9 4.3 %collective-permute-done.8.refs_1_ = bf16[64,512]{1,0:T(8,128)(2,1)S(1)} collective-permute-done((bf16[64,512]{1,0:T(8,128)(2,1)S(1)}, bf16[64,512]{1,0:T(8,128)(2,1)S(1)}, u32[]{:S(2)}, u32[]{:S(2)}) %collective-permute-start.8) | collective-permute-done | bytes 65568 | tf_op jit(solution)/shard_map/ppermute | solution.py:131
  132.4 3.8 %collective-permute-done.9.refs_2_ = bf16[128,512]{1,0:T(8,128)(2,1)S(1)} collective-permute-done((bf16[128,512]{1,0:T(8,128)(2,1)S(1)}, bf16[128,512]{1,0:T(8,128)(2,1)S(1)}, u32[]{:S(2)}, u32[]{:S(2)}) %collective-permute-start.9) | collective-permute-done | bytes 131104 | tf_op jit(solution)/shard_map/ppermute | solution.py:131
  136.2 7.0 %collective-permute-start.10 = (bf16[256,512]{1,0:T(8,128)(2,1)S(1)}, bf16[256,512]{1,0:T(8,128)(2,1)S(1)}, u32[]{:S(2)}, u32[]{:S(2)}) collective-permute-start(bf16[256,512]{1,0:T(8,128)(2,1)S(1)} %pad_maximum_fusion.1), channel_id=1, source_target_pairs={{0,1},{1,0},{2,3},{3,2},{4,5},{5,4},{6,7},{7,6},{8,9},{9,8},{10,11... | collective-permute-start | bytes 786440 | tf_op jit(solution)/shard_map/ppermute | solution.py:131
  146.0 8.4 %all-to-all-done.4.in_ref = bf16[4,128,512]{2,1,0:T(8,128)(2,1)S(1)} async-done(((bf16[4,128,512]{2,1,0:T(8,128)(2,1)}), bf16[4,128,512]{2,1,0:T(8,128)(2,1)S(1)}, u32[]{:S(2)}, u32[]{:S(2)}) %all-to-all-start.4) | async-done | bytes 524320 | tf_op jit(solution)/shard_map/all_to_all | solution.py:127
  (50 shorter events, 23.4 us)
Async XLA Ops:
  23.7 28.4 %all-to-all-start.1 = ((bf16[4,512,512]{2,1,0:T(8,128)(2,1)}), bf16[4,512,512]{2,1,0:T(8,128)(2,1)S(1)}, u32[]{:S(2)}, u32[]{:S(2)}) async-start(bf16[4,512,512]{2,1,0:T(8,128)(2,1)} %broadcast_in_dim.13), calls=%async_computation.1 | async-start | bytes 4194304 | tf_op jit(solution)/shard_map/all_to_all | solution.py:127
  28.2 42.7 %copy-start.3 = (s32[1,1,85]{2,1,0:T(1,128)S(1)}, s32[1,1,85]{2,1,0:T(1,128)}, u32[]{:S(2)}) copy-start(s32[1,1,85]{2,1,0:T(1,128)} %param.13) | copy-start | bytes 1024
  29.3 5.3 %collective-permute-start = (f32[72,512]{1,0:T(8,128)S(1)}, f32[72,512]{1,0:T(8,128)S(1)}, u32[]{:S(2)}, u32[]{:S(2)}) collective-permute-start(f32[72,512]{1,0:T(8,128)S(1)} %get-tuple-element.14), channel_id=1, source_target_pairs={{0,1},{1,0},{2,3},{3,2},{4,5},{5,4},{6,7},{7,6},{8,9},{9,8},{10,11... | collective-permute-start | bytes 442376 | tf_op jit(solution)/shard_map/ppermute | solution.py:131
  34.7 7.1 %collective-permute-start.1 = (f32[40,512]{1,0:T(8,128)S(1)}, f32[40,512]{1,0:T(8,128)S(1)}, u32[]{:S(2)}, u32[]{:S(2)}) collective-permute-start(f32[40,512]{1,0:T(8,128)S(1)} %concatenate.45), channel_id=1, source_target_pairs={{0,64},{32,96},{64,0},{96,32},{1,65},{33,97},{65,1},{97,33},{2,66}... | collective-permute-start | bytes 245768 | tf_op jit(solution)/shard_map/ppermute | solution.py:131
  41.8 5.1 %collective-permute-start.2 = (f32[24,512]{1,0:T(8,128)S(1)}, f32[24,512]{1,0:T(8,128)S(1)}, u32[]{:S(2)}, u32[]{:S(2)}) collective-permute-start(f32[24,512]{1,0:T(8,128)S(1)} %concatenate.46), channel_id=1, source_target_pairs={{0,32},{32,0},{64,96},{96,64},{1,33},{33,1},{65,97},{97,65},{2,34}... | collective-permute-start | bytes 147464 | tf_op jit(solution)/shard_map/ppermute | solution.py:131
  52.1 18.7 %collective-permute-start.3 = (bf16[4,512,512]{2,1,0:T(8,128)(2,1)S(1)}, bf16[4,512,512]{2,1,0:T(8,128)(2,1)}, u32[]{:S(2)}, u32[]{:S(2)}) collective-permute-start(bf16[4,512,512]{2,1,0:T(8,128)(2,1)S(1)} %all-to-all-done.1.own_ref), channel_id=1, source_target_pairs={{0,1},{1,0},{2,3},{3,2},{4,5},{5,4},{6,7},{7,6},{8,9},{9,8},{10,11... | collective-permute-start | bytes 6291464 | tf_op jit(solution)/shard_map/ppermute | solution.py:160
  58.1 28.3 %all-to-all-start.2 = ((f32[4,24,512]{2,1,0:T(8,128)}), f32[4,24,512]{2,1,0:T(8,128)S(1)}, u32[]{:S(2)}, u32[]{:S(2)}) async-start(f32[4,24,512]{2,1,0:T(8,128)} %broadcast_in_dim.14), calls=%async_computation.2 | async-start | bytes 393216 | tf_op jit(solution)/shard_map/all_to_all | solution.py:127
  70.9 1.8 %copy-start = (bf16[1,1,85,128,128]{4,3,2,1,0:T(8,128)(2,1)S(1)}, bf16[1,1,85,128,128]{4,3,2,1,0:T(8,128)(2,1)}, u32[]{:S(2)}) copy-start(bf16[1,1,85,128,128]{4,3,2,1,0:T(8,128)(2,1)} %param.12) | copy-start | bytes 8355844
  77.0 1.3 copy-start.1
  86.4 26.6 %all-to-all-start.3 = ((bf16[4,512,512]{2,1,0:T(8,128)(2,1)}), bf16[4,512,512]{2,1,0:T(8,128)(2,1)S(1)}, u32[]{:S(2)}, u32[]{:S(2)}) async-start(bf16[4,512,512]{2,1,0:T(8,128)(2,1)} %copy-done.1), calls=%async_computation.3 | async-start | bytes 4194304 | tf_op jit(solution)/shard_map/all_to_all | solution.py:127
  90.6 4.8 %collective-permute-start.4 = (f32[24,512]{1,0:T(8,128)S(1)}, f32[24,512]{1,0:T(8,128)S(1)}, u32[]{:S(2)}, u32[]{:S(2)}) collective-permute-start(f32[24,512]{1,0:T(8,128)S(1)} %reduce_sum.9), channel_id=1, source_target_pairs={{0,2},{2,0},{4,6},{6,4},{1,3},{3,1},{5,7},{7,5},{8,10},{10,8},{12,... | collective-permute-start | bytes 147464 | tf_op jit(solution)/shard_map/ppermute | solution.py:131
  95.5 6.3 %collective-permute-start.5 = (f32[24,512]{1,0:T(8,128)S(1)}, f32[24,512]{1,0:T(8,128)S(1)}, u32[]{:S(2)}, u32[]{:S(2)}) collective-permute-start(f32[24,512]{1,0:T(8,128)S(1)} %add.24), channel_id=1, source_target_pairs={{0,4},{2,6},{4,0},{6,2},{1,5},{3,7},{5,1},{7,3},{8,12},{10,14},{12... | collective-permute-start | bytes 147464 | tf_op jit(solution)/shard_map/ppermute | solution.py:131
  101.8 41.4 %copy-start.4 = (s32[32]{0:T(128)S(1)}, s32[32]{0:T(128)}, u32[]{:S(2)}) copy-start(s32[32]{0:T(128)} %constant.23.clone) | copy-start | bytes 388
  101.8 4.8 %collective-permute-start.6 = (bf16[16,512]{1,0:T(8,128)(2,1)S(1)}, bf16[16,512]{1,0:T(8,128)(2,1)S(1)}, u32[]{:S(2)}, u32[]{:S(2)}) collective-permute-start(bf16[16,512]{1,0:T(8,128)(2,1)S(1)} %slice.41), channel_id=1, source_target_pairs={{0,8},{8,0},{16,24},{24,16},{1,9},{9,1},{17,25},{25,17},{2,10},{10... | collective-permute-start | bytes 49160 | tf_op jit(solution)/shard_map/ppermute | solution.py:131
  106.6 5.8 %collective-permute-start.7 = (bf16[32,512]{1,0:T(8,128)(2,1)S(1)}, bf16[32,512]{1,0:T(8,128)(2,1)S(1)}, u32[]{:S(2)}, u32[]{:S(2)}) collective-permute-start(bf16[32,512]{1,0:T(8,128)(2,1)S(1)} %pad_maximum_fusion.4), channel_id=1, source_target_pairs={{0,16},{8,24},{16,0},{24,8},{1,17},{9,25},{17,1},{25,9},{2,18},{10... | collective-permute-start | bytes 98312 | tf_op jit(solution)/shard_map/ppermute | solution.py:131
  114.1 40.3 %copy-start.2 = (bf16[512,512]{1,0:T(8,128)(2,1)S(1)}, bf16[512,512]{1,0:T(8,128)(2,1)}, u32[]{:S(2)}) copy-start(bf16[512,512]{1,0:T(8,128)(2,1)} %weight_ref.1) | copy-start | bytes 1572868
  114.1 40.3 %all-to-all-start.4 = ((bf16[4,128,512]{2,1,0:T(8,128)(2,1)}), bf16[4,128,512]{2,1,0:T(8,128)(2,1)S(1)}, u32[]{:S(2)}, u32[]{:S(2)}) async-start(bf16[4,128,512]{2,1,0:T(8,128)(2,1)} %bitcast.9), calls=%async_computation.4 | async-start | bytes 1048576 | tf_op jit(solution)/shard_map/all_to_all | solution.py:127
  123.6 6.5 %collective-permute-start.8 = (bf16[64,512]{1,0:T(8,128)(2,1)S(1)}, bf16[64,512]{1,0:T(8,128)(2,1)S(1)}, u32[]{:S(2)}, u32[]{:S(2)}) collective-permute-start(bf16[64,512]{1,0:T(8,128)(2,1)S(1)} %pad_maximum_fusion.3.refs_0_), channel_id=1, source_target_pairs={{0,64},{32,96},{64,0},{96,32},{1,65},{33,97},{65,1},{97,33},{2,66}... | collective-permute-start | bytes 196616 | tf_op jit(solution)/shard_map/ppermute | solution.py:131
  130.2 6.0 %collective-permute-start.9 = (bf16[128,512]{1,0:T(8,128)(2,1)S(1)}, bf16[128,512]{1,0:T(8,128)(2,1)S(1)}, u32[]{:S(2)}, u32[]{:S(2)}) collective-permute-start(bf16[128,512]{1,0:T(8,128)(2,1)S(1)} %pad_maximum_fusion.2), channel_id=1, source_target_pairs={{0,32},{32,0},{64,96},{96,64},{1,33},{33,1},{65,97},{97,65},{2,34}... | collective-permute-start | bytes 393224 | tf_op jit(solution)/shard_map/ppermute | solution.py:131
  136.2 8.2 %collective-permute-start.10 = (bf16[256,512]{1,0:T(8,128)(2,1)S(1)}, bf16[256,512]{1,0:T(8,128)(2,1)S(1)}, u32[]{:S(2)}, u32[]{:S(2)}) collective-permute-start(bf16[256,512]{1,0:T(8,128)(2,1)S(1)} %pad_maximum_fusion.1), channel_id=1, source_target_pairs={{0,1},{1,0},{2,3},{3,2},{4,5},{5,4},{6,7},{7,6},{8,9},{9,8},{10,11... | collective-permute-start | bytes 786440 | tf_op jit(solution)/shard_map/ppermute | solution.py:131

commit v8 on v7

--- a/solution.py
+++ b/solution.py
@@ -12,17 +12,26 @@
 BF16 = jnp.bfloat16
 MARK = jax.ShapeDtypeStruct((8, 128), F32)
 VMEM_LIMIT = 24 * 1024 * 1024
-
-
-def tile_kernel(pos_ref, live_ref, core_ref, blocks_ref, own_ref, other_ref, out_ref, mark_ref, acc_ref, low_ref, sems, *, group, n_x):
+TILE_LIMIT = 54 * 1024 * 1024
+
+
+def tile_kernel(pos_ref, live_ref, core_ref, blocks_ref, own_ref, other_ref, out_ref, mark_ref, acc_ref, low_ref, near_ref, sems, near_sems, *, group, n_x):
     n_y, width, _ = out_ref.shape
     blk = blocks_ref.shape[-1]
     tile_cols = acc_ref.shape[0]
-    acc_ref[...] = jnp.zeros_like(acc_ref)
     my_core = core_ref[0]
     live = live_ref[0]
+    turns = (live + group - 1) // group
+
+    def fetch(turn):
+        part = pl.ds(turn * group, group)
+        return pltpu.make_async_copy(blocks_ref.at[part], near_ref.at[part], near_sems.at[turn])
+
+    lax.fori_loop(0, turns, lambda turn, carry: (fetch(turn).start(), carry)[1], 0)
+    acc_ref[...] = jnp.zeros_like(acc_ref)
 
     def add_group(turn, carry):
+        fetch(turn).wait()
         found = []
         for k in range(group):
             slot = turn * group + k
@@ -33,7 +42,7 @@
             rows = jnp.where(
                 source % 2 == my_core, own_ref[x_part, pl.ds(first, blk), :], other_ref[x_part, pl.ds(first, blk), :]
             )
-            block = blocks_ref[slot]
+            block = near_ref[slot]
             block = jnp.where(slot < live, block, jnp.zeros_like(block))
             product = lax.dot_general(block, rows, (((0,), (0,)), ((), ())), preferred_element_type=F32)
             found.append((position % tile_cols, product))
@@ -41,7 +50,7 @@
             acc_ref[column] += product
         return carry
 
-    lax.fori_loop(0, (live + group - 1) // group, add_group, 0)
+    lax.fori_loop(0, turns, add_group, 0)
     copies = []
     for y in range(n_y):
         for z in range(width // blk):
@@ -54,20 +63,21 @@
 
 
 def terms_kernel(place_ref, got_ref, keep_ref, send_ref, sum_ref, *, blk):
-    n_src, width, n_feat = got_ref.shape
-    n_y = n_feat // blk
-    n_pair = width - blk
+    n_src, _, n_feat = got_ref.shape
+    n_y, n_pair, _ = sum_ref.shape
     n_slice = n_pair // 2
+    n_mine = n_y * n_pair
     ones = jnp.ones((8, blk), BF16)
     bias_terms = jnp.zeros((8, n_feat), F32)
+    total = jnp.zeros((n_mine, n_feat), F32)
     for s in range(n_src):
-        bias_terms += jnp.dot(ones, got_ref[s, :blk, :], preferred_element_type=F32)
+        rows = got_ref[s, :blk, :]
+        features = [got_ref[s, blk:, k * n_mine : (k + 1) * n_mine] for k in range(n_feat // n_mine)]
+        features = jnp.concatenate(features, axis=0)
+        total += lax.dot_general(features, rows, (((0,), (0,)), ((), ())), preferred_element_type=F32)
+        bias_terms += jnp.dot(ones, rows, preferred_element_type=F32)
     for y in range(n_y):
-        total = jnp.zeros((n_pair, n_feat), F32)
-        for s in range(n_src):
-            features = got_ref[s, blk:, y * blk : (y + 1) * blk]
-            total += jnp.dot(features, got_ref[s, :blk, :], preferred_element_type=F32)
-        sum_ref[y] = total
+        sum_ref[y] = total[y * n_pair : (y + 1) * n_pair]
     mine, my_y = place_ref[0], place_ref[1]
     for ref, core in ((keep_ref, mine), (send_ref, 1 - mine)):
         first = pl.multiple_of(core * n_slice, n_slice)
@@ -106,7 +116,7 @@
     rows_ref[...] = product.astype(BF16)
 
 
-def call(kernel, out_shape, scratch=(), n_scalar=0, n_in=1, marked=False, out_space=pltpu.VMEM, cost=None):
+def call(kernel, out_shape, scratch=(), n_scalar=0, n_far=0, n_in=1, marked=False, limit=VMEM_LIMIT, out_space=pltpu.VMEM, cost=None):
     smem = pl.BlockSpec(memory_space=pltpu.SMEM)
     vmem = pl.BlockSpec(memory_space=pltpu.VMEM)
     out_specs = jax.tree.map(lambda _: pl.BlockSpec(memory_space=out_space), out_shape)
@@ -115,11 +125,11 @@
     return pl.pallas_call(
         kernel,
         out_shape=out_shape,
-        in_specs=[smem] * n_scalar + [vmem] * n_in,
+        in_specs=[smem] * n_scalar + [pl.BlockSpec(memory_space=pltpu.HBM)] * n_far + [vmem] * n_in,
         out_specs=out_specs,
         scratch_shapes=list(scratch),
         cost_estimate=cost,
-        compiler_params=pltpu.CompilerParams(vmem_limit_bytes=VMEM_LIMIT),
+        compiler_params=pltpu.CompilerParams(vmem_limit_bytes=limit),
     )
 
 
@@ -138,8 +148,9 @@
     n_pair = n_feat // (n_zl * n_y)
     n_slice = n_pair // n_core
     grad_pre = grad_out * relu_mask.astype(BF16)
-    columns = aggregated.T.reshape(n_zl, n_y, n_pair, blk).transpose(0, 2, 1, 3)
-    columns = columns.reshape(n_zl, n_pair, n_y * blk)
+    n_mine = n_feat // n_zl
+    columns = aggregated.reshape(n_feat // n_mine, blk * n_mine // n_feat, n_zl, n_mine).transpose(2, 1, 0, 3)
+    columns = columns.reshape(n_zl, blk * n_mine // n_feat, n_feat)
     sent = jnp.concatenate([jnp.broadcast_to(grad_pre, (n_zl, blk, n_feat)), columns], axis=1)
     got = swap(sent, "zl")
     core, y_index = (lax.axis_index(a).astype(jnp.int32).reshape(1) for a in ("core", "y"))
@@ -156,9 +167,10 @@
     for bit, n in ((2, 2 * n_slice), (1, n_slice)):
         kept, away, bias = terms[:n], terms[n : 2 * n], terms[2 * n :]
         terms = jnp.concatenate([kept, bias], axis=0) + trade(jnp.concatenate([away, bias], axis=0), "y", bit)
+    terms = terms + trade(terms, "zh", 1)
     own, terms = lax.optimization_barrier((own, terms))
     other = lax.ppermute(own, "core", [(0, 1), (1, 0)])
-    terms = swap(jnp.broadcast_to(terms, (n_zh,) + terms.shape), "zh")
+    terms = swap(jnp.broadcast_to(terms, (n_x,) + terms.shape), "x")
     slots = adj_blocks.shape[2]
     group = max(d for d in range(1, 9) if slots % d == 0)
     sent, mark = call(
@@ -167,8 +179,12 @@
         scratch=[
             pltpu.VMEM((n_zh * n_y, blk, n_feat), F32),
             pltpu.VMEM((n_y, n_zh * blk, n_feat), BF16),
+            pltpu.VMEM((slots, blk, blk), BF16),
             pltpu.SemaphoreType.DMA((n_y,)),
+            pltpu.SemaphoreType.DMA((slots // group,)),
         ],
+        n_far=1,
+        limit=TILE_LIMIT,
         out_space=pltpu.HBM,
         marked=True,
         cost=pl.CostEstimate(
@@ -177,12 +193,11 @@
             bytes_accessed=8 * slots * blk * n_feat,
         ),
         n_scalar=3,
-        n_in=3,
+        n_in=2,
     )(block_pos.reshape(-1), block_live.reshape(-1), core, adj_blocks[0, 0], own, other)
     terms, sent = lax.optimization_barrier((terms, sent))
     terms = terms.sum(axis=0)
-    for bit in (1, 2):
-        terms = terms + trade(terms, "x", bit)
+    terms = terms + trade(terms, "zh", 2)
     factor = 1.0 / math.sqrt(blk * n_zh * n_y * n_zl * n_x * n_core)
     terms = terms * factor
     slices = terms[:n_slice].astype(BF16)

time: 156 us -> 155 us (level)
  the two profiles are of different devices: /device:TPU:33 before, /device:TPU:1 now
where the time goes in v8:
time: 155 us; the launch traced here: 154 us
  starting transfers between devices  82.5 us (53%)
  waiting for transfers between devices  30.3 us (20%)
  blocking collectives  22 us (14%)
  Pallas kernels  12.6 us (8%)
  local copies, waits for them, and re-layouts  3.99 us (3%)
  between operations  1.6 us (1%)
    ppermute x10, starting transfers between devices, trade(): lax.ppermute(value, axis, [(i, i ^ bit) for i in range(lax.axis_size(axis...  51.2 us
    all_to_all x4, starting transfers between devices, swap(): return lax.all_to_all(value, axis, split_axis=0, concat_axis=0, tiled=True)  26.5 us
    ppermute x10, waiting for transfers between devices, trade(): lax.ppermute(value, axis, [(i, i ^ bit) for i in range(lax.axis_size(axis...  23 us
    all_to_all x1, blocking collectives, swap(): return lax.all_to_all(value, axis, split_axis=0, concat_axis=0, tiled=True)  22 us
    pallas_call x1, Pallas kernels, body(): call(functools.partial(tile_kernel, group=group, n_x=n_x), jax.ShapeDtype...  7.9 us
    all_to_all x4, waiting for transfers between devices, swap(): return lax.all_to_all(value, axis, split_axis=0, concat_axis=0, tiled=True)  7.33 us
    ppermute x1, starting transfers between devices, body(): other = lax.ppermute(own, 'core', [(0, 1), (1, 0)])  4.83 us
  transfers between devices with their start and end apart: 15, of which 11 were waited for; matrix products, arithmetic and copies ran while one was open for 1% of the time, Pallas kernels for 7%

profile of v8, /device:TPU:1, one launch (start us, length us, event | category | flops | bytes accessed | tf_op | source)
XLA Modules:
  0.0 154.4 jit_solution(10195415208333521759)
XLA Ops:
  2.9 22.0 %all_to_all.25.got_ref = bf16[4,160,512]{2,1,0:T(8,128)(2,1)S(1)} all-to-all(bf16[4,160,512]{2,1,0:T(8,128)(2,1)S(1)} %pad_maximum_fusion), channel_id=1, replica_groups=mesh['zh'=4,'y'=4,'zl'=4,'x'=4,'core'=2] {'zl'}, dimensions={0} | all-to-all | bytes 1310720 | tf_op jit(solution)/shard_map/all_to_all | solution.py:137
  26.4 4.7 %all-to-all-start.1 = ((bf16[4,512,512]{2,1,0:T(8,128)(2,1)}), bf16[4,512,512]{2,1,0:T(8,128)(2,1)S(1)}, u32[]{:S(2)}, u32[]{:S(2)}) async-start(bf16[4,512,512]{2,1,0:T(8,128)(2,1)} %broadcast_in_dim.13), calls=%async_computation.1 | async-start | bytes 4194304 | tf_op jit(solution)/shard_map/all_to_all | solution.py:137
  32.2 4.0 %collective-permute-start = (f32[72,512]{1,0:T(8,128)S(1)}, f32[72,512]{1,0:T(8,128)S(1)}, u32[]{:S(2)}, u32[]{:S(2)}) collective-permute-start(f32[72,512]{1,0:T(8,128)S(1)} %get-tuple-element.14), channel_id=1, source_target_pairs={{0,1},{1,0},{2,3},{3,2},{4,5},{5,4},{6,7},{7,6},{8,9},{9,8},{10,11... | collective-permute-start | bytes 442376 | tf_op jit(solution)/shard_map/ppermute | solution.py:141
  37.2 4.8 %collective-permute-start.1 = (f32[40,512]{1,0:T(8,128)S(1)}, f32[40,512]{1,0:T(8,128)S(1)}, u32[]{:S(2)}, u32[]{:S(2)}) collective-permute-start(f32[40,512]{1,0:T(8,128)S(1)} %concatenate.45), channel_id=1, source_target_pairs={{0,64},{32,96},{64,0},{96,32},{1,65},{33,97},{65,1},{97,33},{2,66}... | collective-permute-start | bytes 245768 | tf_op jit(solution)/shard_map/ppermute | solution.py:141
  42.1 2.2 %collective-permute-done.1 = f32[40,512]{1,0:T(8,128)S(1)} collective-permute-done((f32[40,512]{1,0:T(8,128)S(1)}, f32[40,512]{1,0:T(8,128)S(1)}, u32[]{:S(2)}, u32[]{:S(2)}) %collective-permute-start.1) | collective-permute-done | bytes 81952 | tf_op jit(solution)/shard_map/ppermute | solution.py:141
  44.3 3.2 %collective-permute-start.2 = (f32[24,512]{1,0:T(8,128)S(1)}, f32[24,512]{1,0:T(8,128)S(1)}, u32[]{:S(2)}, u32[]{:S(2)}) collective-permute-start(f32[24,512]{1,0:T(8,128)S(1)} %concatenate.46), channel_id=1, source_target_pairs={{0,32},{32,0},{64,96},{96,64},{1,33},{33,1},{65,97},{97,65},{2,34}... | collective-permute-start | bytes 147464 | tf_op jit(solution)/shard_map/ppermute | solution.py:141
  49.4 8.8 %collective-permute-start.3 = (f32[24,512]{1,0:T(8,128)S(1)}, f32[24,512]{1,0:T(8,128)S(1)}, u32[]{:S(2)}, u32[]{:S(2)}) collective-permute-start(f32[24,512]{1,0:T(8,128)S(1)} %maximum_add_fusion.1), channel_id=1, source_target_pairs={{0,128},{128,0},{256,384},{384,256},{1,129},{129,1},{257,385},{385... | collective-permute-start | bytes 147464 | tf_op jit(solution)/shard_map/ppermute | solution.py:141
  58.3 2.7 %collective-permute-done.3 = f32[24,512]{1,0:T(8,128)S(1)} collective-permute-done((f32[24,512]{1,0:T(8,128)S(1)}, f32[24,512]{1,0:T(8,128)S(1)}, u32[]{:S(2)}, u32[]{:S(2)}) %collective-permute-start.3) | collective-permute-done | bytes 49184 | tf_op jit(solution)/shard_map/ppermute | solution.py:141
  61.0 4.8 %collective-permute-start.4 = (bf16[4,512,512]{2,1,0:T(8,128)(2,1)S(1)}, bf16[4,512,512]{2,1,0:T(8,128)(2,1)}, u32[]{:S(2)}, u32[]{:S(2)}) collective-permute-start(bf16[4,512,512]{2,1,0:T(8,128)(2,1)S(1)} %all-to-all-done.1.own_ref), channel_id=1, source_target_pairs={{0,1},{1,0},{2,3},{3,2},{4,5},{5,4},{6,7},{7,6},{8,9},{9,8},{10,11... | collective-permute-start | bytes 6291464 | tf_op jit(solution)/shard_map/ppermute | solution.py:172
  66.5 4.5 %all-to-all-start.2 = ((f32[4,24,512]{2,1,0:T(8,128)}), f32[4,24,512]{2,1,0:T(8,128)S(1)}, u32[]{:S(2)}, u32[]{:S(2)}) async-start(f32[4,24,512]{2,1,0:T(8,128)} %broadcast_in_dim.14), calls=%async_computation.2 | async-start | bytes 393216 | tf_op jit(solution)/shard_map/all_to_all | solution.py:137
  71.7 7.9 %shard_map.104 = (bf16[4,512,512]{2,1,0:T(8,128)(2,1)}, f32[8,128]{1,0:T(8,128)}) custom-call(s32[85]{0:T(128)} %bitcast.19, s32[1]{0:T(128)} %bitcast.13.live_ref, s32[1]{0:T(128)} %bitcast.2.core_ref, bf16[85,128,128]{2,1,0:T(8,128)(2,1)} %bitcast.14, bf16[4,512,512]{2,1,0:T(8,128)(2,1)} %copy-done.1, bf16[4,512,512]{2,1,0:T(8,128)(2,1)} %collective-permute-done.4.other_ref), custom_call_target="tpu_custom_call" | custom-call | flops 1426063360 | bytes 44564480 | tf_op jit(solution)/shard_map/pallas_call | solution.py:176
  79.6 3.6 %all-to-all-start.3 = ((bf16[4,512,512]{2,1,0:T(8,128)(2,1)}), bf16[4,512,512]{2,1,0:T(8,128)(2,1)S(1)}, u32[]{:S(2)}, u32[]{:S(2)}) async-start(bf16[4,512,512]{2,1,0:T(8,128)(2,1)} %get-tuple-element.19), calls=%async_computation.3 | async-start | bytes 4194304 | tf_op jit(solution)/shard_map/all_to_all | solution.py:137
  83.3 14.4 %collective-permute-start.5 = (f32[24,512]{1,0:T(8,128)S(1)}, f32[24,512]{1,0:T(8,128)S(1)}, u32[]{:S(2)}, u32[]{:S(2)}) collective-permute-start(f32[24,512]{1,0:T(8,128)S(1)} %reduce_sum.9), channel_id=1, source_target_pairs={{0,256},{128,384},{256,0},{384,128},{1,257},{129,385},{257,1},{385... | collective-permute-start | bytes 147464 | tf_op jit(solution)/shard_map/ppermute | solution.py:141
  97.7 2.0 %collective-permute-done.5 = f32[24,512]{1,0:T(8,128)S(1)} collective-permute-done((f32[24,512]{1,0:T(8,128)S(1)}, f32[24,512]{1,0:T(8,128)S(1)}, u32[]{:S(2)}, u32[]{:S(2)}) %collective-permute-start.5) | collective-permute-done | bytes 49184 | tf_op jit(solution)/shard_map/ppermute | solution.py:141
  99.7 1.9 %collective-permute-start.6 = (bf16[16,512]{1,0:T(8,128)(2,1)S(1)}, bf16[16,512]{1,0:T(8,128)(2,1)S(1)}, u32[]{:S(2)}, u32[]{:S(2)}) collective-permute-start(bf16[16,512]{1,0:T(8,128)(2,1)S(1)} %slice.41), channel_id=1, source_target_pairs={{0,8},{8,0},{16,24},{24,16},{1,9},{9,1},{17,25},{25,17},{2,10},{10... | collective-permute-start | bytes 49160 | tf_op jit(solution)/shard_map/ppermute | solution.py:141
  101.6 2.8 %collective-permute-done.6 = bf16[16,512]{1,0:T(8,128)(2,1)S(1)} collective-permute-done((bf16[16,512]{1,0:T(8,128)(2,1)S(1)}, bf16[16,512]{1,0:T(8,128)(2,1)S(1)}, u32[]{:S(2)}, u32[]{:S(2)}) %collective-permute-start.6) | collective-permute-done | bytes 16416 | tf_op jit(solution)/shard_map/ppermute | solution.py:141
  106.4 3.7 %collective-permute-done.7 = bf16[32,512]{1,0:T(8,128)(2,1)S(1)} collective-permute-done((bf16[32,512]{1,0:T(8,128)(2,1)S(1)}, bf16[32,512]{1,0:T(8,128)(2,1)S(1)}, u32[]{:S(2)}, u32[]{:S(2)}) %collective-permute-start.7) | collective-permute-done | bytes 32800 | tf_op jit(solution)/shard_map/ppermute | solution.py:141
  111.2 13.6 %all-to-all-start.4 = ((bf16[4,128,512]{2,1,0:T(8,128)(2,1)}), bf16[4,128,512]{2,1,0:T(8,128)(2,1)S(1)}, u32[]{:S(2)}, u32[]{:S(2)}) async-start(bf16[4,128,512]{2,1,0:T(8,128)(2,1)} %bitcast.7), calls=%async_computation.4 | async-start | bytes 1048576 | tf_op jit(solution)/shard_map/all_to_all | solution.py:137
  124.8 3.8 %collective-permute-start.8 = (bf16[64,512]{1,0:T(8,128)(2,1)S(1)}, bf16[64,512]{1,0:T(8,128)(2,1)S(1)}, u32[]{:S(2)}, u32[]{:S(2)}) collective-permute-start(bf16[64,512]{1,0:T(8,128)(2,1)S(1)} %pad_maximum_fusion.3.refs_0_), channel_id=1, source_target_pairs={{0,64},{32,96},{64,0},{96,32},{1,65},{33,97},{65,1},{97,33},{2,66}... | collective-permute-start | bytes 196616 | tf_op jit(solution)/shard_map/ppermute | solution.py:141
  128.6 2.7 %collective-permute-done.8.refs_1_ = bf16[64,512]{1,0:T(8,128)(2,1)S(1)} collective-permute-done((bf16[64,512]{1,0:T(8,128)(2,1)S(1)}, bf16[64,512]{1,0:T(8,128)(2,1)S(1)}, u32[]{:S(2)}, u32[]{:S(2)}) %collective-permute-start.8) | collective-permute-done | bytes 65568 | tf_op jit(solution)/shard_map/ppermute | solution.py:141
  131.3 2.5 %collective-permute-start.9 = (bf16[128,512]{1,0:T(8,128)(2,1)S(1)}, bf16[128,512]{1,0:T(8,128)(2,1)S(1)}, u32[]{:S(2)}, u32[]{:S(2)}) collective-permute-start(bf16[128,512]{1,0:T(8,128)(2,1)S(1)} %pad_maximum_fusion.2), channel_id=1, source_target_pairs={{0,32},{32,0},{64,96},{96,64},{1,33},{33,1},{65,97},{97,65},{2,34}... | collective-permute-start | bytes 393224 | tf_op jit(solution)/shard_map/ppermute | solution.py:141
  133.9 3.5 %collective-permute-done.9.refs_2_ = bf16[128,512]{1,0:T(8,128)(2,1)S(1)} collective-permute-done((bf16[128,512]{1,0:T(8,128)(2,1)S(1)}, bf16[128,512]{1,0:T(8,128)(2,1)S(1)}, u32[]{:S(2)}, u32[]{:S(2)}) %collective-permute-start.9) | collective-permute-done | bytes 131104 | tf_op jit(solution)/shard_map/ppermute | solution.py:141
  137.4 5.8 %collective-permute-start.10 = (bf16[256,512]{1,0:T(8,128)(2,1)S(1)}, bf16[256,512]{1,0:T(8,128)(2,1)S(1)}, u32[]{:S(2)}, u32[]{:S(2)}) collective-permute-start(bf16[256,512]{1,0:T(8,128)(2,1)S(1)} %pad_maximum_fusion.1), channel_id=1, source_target_pairs={{0,1},{1,0},{2,3},{3,2},{4,5},{5,4},{6,7},{7,6},{8,9},{9,8},{10,11... | collective-permute-start | bytes 786440 | tf_op jit(solution)/shard_map/ppermute | solution.py:141
  145.9 7.3 %all-to-all-done.4.in_ref = bf16[4,128,512]{2,1,0:T(8,128)(2,1)S(1)} async-done(((bf16[4,128,512]{2,1,0:T(8,128)(2,1)}), bf16[4,128,512]{2,1,0:T(8,128)(2,1)S(1)}, u32[]{:S(2)}, u32[]{:S(2)}) %all-to-all-start.4) | async-done | bytes 524320 | tf_op jit(solution)/shard_map/all_to_all | solution.py:137
  (47 shorter events, 15.4 us)
Async XLA Ops:
  26.4 34.5 %all-to-all-start.1 = ((bf16[4,512,512]{2,1,0:T(8,128)(2,1)}), bf16[4,512,512]{2,1,0:T(8,128)(2,1)S(1)}, u32[]{:S(2)}, u32[]{:S(2)}) async-start(bf16[4,512,512]{2,1,0:T(8,128)(2,1)} %broadcast_in_dim.13), calls=%async_computation.1 | async-start | bytes 4194304 | tf_op jit(solution)/shard_map/all_to_all | solution.py:137
  32.2 5.0 %collective-permute-start = (f32[72,512]{1,0:T(8,128)S(1)}, f32[72,512]{1,0:T(8,128)S(1)}, u32[]{:S(2)}, u32[]{:S(2)}) collective-permute-start(f32[72,512]{1,0:T(8,128)S(1)} %get-tuple-element.14), channel_id=1, source_target_pairs={{0,1},{1,0},{2,3},{3,2},{4,5},{5,4},{6,7},{7,6},{8,9},{9,8},{10,11... | collective-permute-start | bytes 442376 | tf_op jit(solution)/shard_map/ppermute | solution.py:141
  37.2 7.1 %collective-permute-start.1 = (f32[40,512]{1,0:T(8,128)S(1)}, f32[40,512]{1,0:T(8,128)S(1)}, u32[]{:S(2)}, u32[]{:S(2)}) collective-permute-start(f32[40,512]{1,0:T(8,128)S(1)} %concatenate.45), channel_id=1, source_target_pairs={{0,64},{32,96},{64,0},{96,32},{1,65},{33,97},{65,1},{97,33},{2,66}... | collective-permute-start | bytes 245768 | tf_op jit(solution)/shard_map/ppermute | solution.py:141
  44.3 5.1 %collective-permute-start.2 = (f32[24,512]{1,0:T(8,128)S(1)}, f32[24,512]{1,0:T(8,128)S(1)}, u32[]{:S(2)}, u32[]{:S(2)}) collective-permute-start(f32[24,512]{1,0:T(8,128)S(1)} %concatenate.46), channel_id=1, source_target_pairs={{0,32},{32,0},{64,96},{96,64},{1,33},{33,1},{65,97},{97,65},{2,34}... | collective-permute-start | bytes 147464 | tf_op jit(solution)/shard_map/ppermute | solution.py:141
  49.4 11.5 %collective-permute-start.3 = (f32[24,512]{1,0:T(8,128)S(1)}, f32[24,512]{1,0:T(8,128)S(1)}, u32[]{:S(2)}, u32[]{:S(2)}) collective-permute-start(f32[24,512]{1,0:T(8,128)S(1)} %maximum_add_fusion.1), channel_id=1, source_target_pairs={{0,128},{128,0},{256,384},{384,256},{1,129},{129,1},{257,385},{385... | collective-permute-start | bytes 147464 | tf_op jit(solution)/shard_map/ppermute | solution.py:141
  61.0 10.7 %copy-start.1 = (bf16[4,512,512]{2,1,0:T(8,128)(2,1)}, bf16[4,512,512]{2,1,0:T(8,128)(2,1)S(1)}, u32[]{:S(2)}) copy-start(bf16[4,512,512]{2,1,0:T(8,128)(2,1)S(1)} %all-to-all-done.1.own_ref) | copy-start | bytes 6291460
  61.0 10.7 %collective-permute-start.4 = (bf16[4,512,512]{2,1,0:T(8,128)(2,1)S(1)}, bf16[4,512,512]{2,1,0:T(8,128)(2,1)}, u32[]{:S(2)}, u32[]{:S(2)}) collective-permute-start(bf16[4,512,512]{2,1,0:T(8,128)(2,1)S(1)} %all-to-all-done.1.own_ref), channel_id=1, source_target_pairs={{0,1},{1,0},{2,3},{3,2},{4,5},{5,4},{6,7},{7,6},{8,9},{9,8},{10,11... | collective-permute-start | bytes 6291464 | tf_op jit(solution)/shard_map/ppermute | solution.py:172
  66.5 13.1 %all-to-all-start.2 = ((f32[4,24,512]{2,1,0:T(8,128)}), f32[4,24,512]{2,1,0:T(8,128)S(1)}, u32[]{:S(2)}, u32[]{:S(2)}) async-start(f32[4,24,512]{2,1,0:T(8,128)} %broadcast_in_dim.14), calls=%async_computation.2 | async-start | bytes 393216 | tf_op jit(solution)/shard_map/all_to_all | solution.py:137
  79.6 30.5 %all-to-all-start.3 = ((bf16[4,512,512]{2,1,0:T(8,128)(2,1)}), bf16[4,512,512]{2,1,0:T(8,128)(2,1)S(1)}, u32[]{:S(2)}, u32[]{:S(2)}) async-start(bf16[4,512,512]{2,1,0:T(8,128)(2,1)} %get-tuple-element.19), calls=%async_computation.3 | async-start | bytes 4194304 | tf_op jit(solution)/shard_map/all_to_all | solution.py:137
  83.3 16.4 %collective-permute-start.5 = (f32[24,512]{1,0:T(8,128)S(1)}, f32[24,512]{1,0:T(8,128)S(1)}, u32[]{:S(2)}, u32[]{:S(2)}) collective-permute-start(f32[24,512]{1,0:T(8,128)S(1)} %reduce_sum.9), channel_id=1, source_target_pairs={{0,256},{128,384},{256,0},{384,128},{1,257},{129,385},{257,1},{385... | collective-permute-start | bytes 147464 | tf_op jit(solution)/shard_map/ppermute | solution.py:141
  99.7 43.5 %copy-start.2 = (s32[32]{0:T(128)S(1)}, s32[32]{0:T(128)}, u32[]{:S(2)}) copy-start(s32[32]{0:T(128)} %constant.23.clone) | copy-start | bytes 388
  99.7 4.8 %collective-permute-start.6 = (bf16[16,512]{1,0:T(8,128)(2,1)S(1)}, bf16[16,512]{1,0:T(8,128)(2,1)S(1)}, u32[]{:S(2)}, u32[]{:S(2)}) collective-permute-start(bf16[16,512]{1,0:T(8,128)(2,1)S(1)} %slice.41), channel_id=1, source_target_pairs={{0,8},{8,0},{16,24},{24,16},{1,9},{9,1},{17,25},{25,17},{2,10},{10... | collective-permute-start | bytes 49160 | tf_op jit(solution)/shard_map/ppermute | solution.py:141
  104.5 5.6 %collective-permute-start.7 = (bf16[32,512]{1,0:T(8,128)(2,1)S(1)}, bf16[32,512]{1,0:T(8,128)(2,1)S(1)}, u32[]{:S(2)}, u32[]{:S(2)}) collective-permute-start(bf16[32,512]{1,0:T(8,128)(2,1)S(1)} %pad_maximum_fusion.4), channel_id=1, source_target_pairs={{0,16},{8,24},{16,0},{24,8},{1,17},{9,25},{17,1},{25,9},{2,18},{10... | collective-permute-start | bytes 98312 | tf_op jit(solution)/shard_map/ppermute | solution.py:141
  111.2 42.0 %copy-start = (bf16[512,512]{1,0:T(8,128)(2,1)S(1)}, bf16[512,512]{1,0:T(8,128)(2,1)}, u32[]{:S(2)}) copy-start(bf16[512,512]{1,0:T(8,128)(2,1)} %weight_ref.1) | copy-start | bytes 1572868
  111.2 42.0 %all-to-all-start.4 = ((bf16[4,128,512]{2,1,0:T(8,128)(2,1)}), bf16[4,128,512]{2,1,0:T(8,128)(2,1)S(1)}, u32[]{:S(2)}, u32[]{:S(2)}) async-start(bf16[4,128,512]{2,1,0:T(8,128)(2,1)} %bitcast.7), calls=%async_computation.4 | async-start | bytes 1048576 | tf_op jit(solution)/shard_map/all_to_all | solution.py:137
  124.8 6.5 %collective-permute-start.8 = (bf16[64,512]{1,0:T(8,128)(2,1)S(1)}, bf16[64,512]{1,0:T(8,128)(2,1)S(1)}, u32[]{:S(2)}, u32[]{:S(2)}) collective-permute-start(bf16[64,512]{1,0:T(8,128)(2,1)S(1)} %pad_maximum_fusion.3.refs_0_), channel_id=1, source_target_pairs={{0,64},{32,96},{64,0},{96,32},{1,65},{33,97},{65,1},{97,33},{2,66}... | collective-permute-start | bytes 196616 | tf_op jit(solution)/shard_map/ppermute | solution.py:141
  131.3 6.0 %collective-permute-start.9 = (bf16[128,512]{1,0:T(8,128)(2,1)S(1)}, bf16[128,512]{1,0:T(8,128)(2,1)S(1)}, u32[]{:S(2)}, u32[]{:S(2)}) collective-permute-start(bf16[128,512]{1,0:T(8,128)(2,1)S(1)} %pad_maximum_fusion.2), channel_id=1, source_target_pairs={{0,32},{32,0},{64,96},{96,64},{1,33},{33,1},{65,97},{97,65},{2,34}... | collective-permute-start | bytes 393224 | tf_op jit(solution)/shard_map/ppermute | solution.py:141
  137.4 7.0 %collective-permute-start.10 = (bf16[256,512]{1,0:T(8,128)(2,1)S(1)}, bf16[256,512]{1,0:T(8,128)(2,1)S(1)}, u32[]{:S(2)}, u32[]{:S(2)}) collective-permute-start(bf16[256,512]{1,0:T(8,128)(2,1)S(1)} %pad_maximum_fusion.1), channel_id=1, source_target_pairs={{0,1},{1,0},{2,3},{3,2},{4,5},{5,4},{6,7},{7,6},{8,9},{9,8},{10,11... | collective-permute-start | bytes 786440 | tf_op jit(solution)/shard_map/ppermute | solution.py:141

commit v9 on v8

--- a/solution.py
+++ b/solution.py
@@ -15,7 +15,7 @@
 TILE_LIMIT = 54 * 1024 * 1024
 
 
-def tile_kernel(pos_ref, live_ref, core_ref, blocks_ref, own_ref, other_ref, out_ref, mark_ref, acc_ref, low_ref, near_ref, sems, near_sems, *, group, n_x):
+def tile_kernel(pos_ref, live_ref, core_ref, blocks_ref, own_ref, other_ref, out_ref, mark_ref, acc_ref, low_ref, near_ref, rows_ref, sems, near_sems, rows_sems, *, group, n_x):
     n_y, width, _ = out_ref.shape
     blk = blocks_ref.shape[-1]
     tile_cols = acc_ref.shape[0]
@@ -27,8 +27,14 @@
         part = pl.ds(turn * group, group)
         return pltpu.make_async_copy(blocks_ref.at[part], near_ref.at[part], near_sems.at[turn])
 
-    lax.fori_loop(0, turns, lambda turn, carry: (fetch(turn).start(), carry)[1], 0)
+    fetch(0).start()
+    halves = [pltpu.make_async_copy(r, rows_ref.at[k], rows_sems.at[k]) for k, r in enumerate((own_ref, other_ref))]
+    for half in halves:
+        half.start()
+    lax.fori_loop(1, turns, lambda turn, carry: (fetch(turn).start(), carry)[1], 0)
     acc_ref[...] = jnp.zeros_like(acc_ref)
+    for half in halves:
+        half.wait()
 
     def add_group(turn, carry):
         fetch(turn).wait()
@@ -39,9 +45,7 @@
             source = position // tile_cols
             first = pl.multiple_of(source // (2 * n_x) * blk, blk)
             x_part = (source // 2) % n_x
-            rows = jnp.where(
-                source % 2 == my_core, own_ref[x_part, pl.ds(first, blk), :], other_ref[x_part, pl.ds(first, blk), :]
-            )
+            rows = rows_ref[(source % 2) ^ my_core, x_part, pl.ds(first, blk), :]
             block = near_ref[slot]
             block = jnp.where(slot < live, block, jnp.zeros_like(block))
             product = lax.dot_general(block, rows, (((0,), (0,)), ((), ())), preferred_element_type=F32)
@@ -60,6 +64,18 @@
     mark_ref[...] = jnp.zeros_like(mark_ref)
     for copy in copies:
         copy.wait()
+
+
+def pack_kernel(grad_ref, mask_ref, features_ref, out_ref):
+    n_dst, width, n_feat = out_ref.shape
+    blk = grad_ref.shape[0]
+    n_mine = n_feat // n_dst
+    grad_pre = grad_ref[...] * mask_ref[...].astype(BF16)
+    for z in range(n_dst):
+        out_ref[z, :blk, :] = grad_pre
+        for k in range(n_feat // n_mine):
+            rows = slice(k * (width - blk), (k + 1) * (width - blk))
+            out_ref[z, blk:, k * n_mine : (k + 1) * n_mine] = features_ref[rows, z * n_mine : (z + 1) * n_mine]
 
 
 def terms_kernel(place_ref, got_ref, keep_ref, send_ref, sum_ref, *, blk):
@@ -147,11 +163,12 @@
     n_rows = n_zl * blk
     n_pair = n_feat // (n_zl * n_y)
     n_slice = n_pair // n_core
-    grad_pre = grad_out * relu_mask.astype(BF16)
     n_mine = n_feat // n_zl
-    columns = aggregated.reshape(n_feat // n_mine, blk * n_mine // n_feat, n_zl, n_mine).transpose(2, 1, 0, 3)
-    columns = columns.reshape(n_zl, blk * n_mine // n_feat, n_feat)
-    sent = jnp.concatenate([jnp.broadcast_to(grad_pre, (n_zl, blk, n_feat)), columns], axis=1)
+    sent = call(
+        pack_kernel,
+        jax.ShapeDtypeStruct((n_zl, blk + blk * n_mine // n_feat, n_feat), BF16),
+        n_in=3,
+    )(grad_out, relu_mask, aggregated)
     got = swap(sent, "zl")
     core, y_index = (lax.axis_index(a).astype(jnp.int32).reshape(1) for a in ("core", "y"))
     half = jax.ShapeDtypeStruct((n_y * n_slice + 8, n_feat), F32)
@@ -180,10 +197,12 @@
             pltpu.VMEM((n_zh * n_y, blk, n_feat), F32),
             pltpu.VMEM((n_y, n_zh * blk, n_feat), BF16),
             pltpu.VMEM((slots, blk, blk), BF16),
+            pltpu.VMEM((n_core, n_x, n_rows, n_feat), BF16),
             pltpu.SemaphoreType.DMA((n_y,)),
             pltpu.SemaphoreType.DMA((slots // group,)),
+            pltpu.SemaphoreType.DMA((n_core,)),
         ],
-        n_far=1,
+        n_far=3,
         limit=TILE_LIMIT,
         out_space=pltpu.HBM,
         marked=True,
@@ -193,7 +212,7 @@
             bytes_accessed=8 * slots * blk * n_feat,
         ),
         n_scalar=3,
-        n_in=2,
+        n_in=0,
     )(block_pos.reshape(-1), block_live.reshape(-1), core, adj_blocks[0, 0], own, other)
     terms, sent = lax.optimization_barrier((terms, sent))
     terms = terms.sum(axis=0)

time: 155 us -> 156 us (level); the launches traced: 154 us -> 153 us
  Pallas kernels: 12.6 us -> 10.3 us
  local copies, waits for them, and re-layouts: 3.99 us -> 5.61 us
    unnamed x6 -> x12, local copies, waits for them, and re-layouts: 0.01 us -> 2.77 us
    all_to_all x4, starting transfers between devices: 26.5 us -> 29.2 us  [swap(): return lax.all_to_all(value, axis, split_axis=0, concat_axis=0, tiled=True)]
    pallas_call x1, Pallas kernels: 7.9 us -> 5.5 us  [body(): call(functools.partial(tile_kernel, group=group, n_x=n_x), jax.ShapeDtype...]
    ppermute x10, starting transfers between devices: 51.2 us -> 49.6 us  [trade(): lax.ppermute(value, axis, [(i, i ^ bit) for i in range(lax.axis_size(axis...]
  transfers between devices with their start and end apart: 15 -> 15, of which waited for: 11 -> 11; matrix products, arithmetic and copies ran while one was open for 1% -> 1% of each run, Pallas kernels for 7% -> 5%
where the time goes in v9:
time: 156 us; the launch traced here: 153 us
  starting transfers between devices  83.6 us (54%)
  waiting for transfers between devices  29.9 us (19%)
  blocking collectives  22 us (14%)
  Pallas kernels  10.3 us (7%)
  local copies, waits for them, and re-layouts  5.61 us (4%)
  between operations  1.57 us (1%)
    ppermute x10, starting transfers between devices, trade(): lax.ppermute(value, axis, [(i, i ^ bit) for i in range(lax.axis_size(axis...  49.6 us
    all_to_all x4, starting transfers between devices, swap(): return lax.all_to_all(value, axis, split_axis=0, concat_axis=0, tiled=True)  29.2 us
    ppermute x10, waiting for transfers between devices, trade(): lax.ppermute(value, axis, [(i, i ^ bit) for i in range(lax.axis_size(axis...  23 us
    all_to_all x1, blocking collectives, swap(): return lax.all_to_all(value, axis, split_axis=0, concat_axis=0, tiled=True)  22 us
    all_to_all x4, waiting for transfers between devices, swap(): return lax.all_to_all(value, axis, split_axis=0, concat_axis=0, tiled=True)  6.9 us
    pallas_call x1, Pallas kernels, body(): call(functools.partial(tile_kernel, group=group, n_x=n_x), jax.ShapeDtype...  5.5 us
    ppermute x1, starting transfers between devices, body(): other = lax.ppermute(own, 'core', [(0, 1), (1, 0)])  4.83 us
  transfers between devices with their start and end apart: 15, of which 11 were waited for; matrix products, arithmetic and copies ran while one was open for 1% of the time, Pallas kernels for 5%

profile of v9, /device:TPU:1, one launch (start us, length us, event | category | flops | bytes accessed | tf_op | source)
XLA Modules:
  0.0 153.2 jit_solution(5509452703457686135)
XLA Ops:
  3.4 22.0 %all_to_all.25.got_ref = bf16[4,160,512]{2,1,0:T(8,128)(2,1)S(1)} all-to-all(bf16[4,160,512]{2,1,0:T(8,128)(2,1)S(1)} %shard_map.103), channel_id=1, replica_groups=mesh['zh'=4,'y'=4,'zl'=4,'x'=4,'core'=2] {'zl'}, dimensions={0} | all-to-all | bytes 1310720 | tf_op jit(solution)/shard_map/all_to_all | solution.py:153
  27.0 4.7 %all-to-all-start.1 = ((bf16[4,512,512]{2,1,0:T(8,128)(2,1)}), bf16[4,512,512]{2,1,0:T(8,128)(2,1)S(1)}, u32[]{:S(2)}, u32[]{:S(2)}) async-start(bf16[4,512,512]{2,1,0:T(8,128)(2,1)} %broadcast_in_dim.9), calls=%async_computation.1 | async-start | bytes 4194304 | tf_op jit(solution)/shard_map/all_to_all | solution.py:153
  32.7 4.0 %collective-permute-start = (f32[72,512]{1,0:T(8,128)S(1)}, f32[72,512]{1,0:T(8,128)S(1)}, u32[]{:S(2)}, u32[]{:S(2)}) collective-permute-start(f32[72,512]{1,0:T(8,128)S(1)} %get-tuple-element.14), channel_id=1, source_target_pairs={{0,1},{1,0},{2,3},{3,2},{4,5},{5,4},{6,7},{7,6},{8,9},{9,8},{10,11... | collective-permute-start | bytes 442376 | tf_op jit(solution)/shard_map/ppermute | solution.py:157
  37.8 4.8 %collective-permute-start.1 = (f32[40,512]{1,0:T(8,128)S(1)}, f32[40,512]{1,0:T(8,128)S(1)}, u32[]{:S(2)}, u32[]{:S(2)}) collective-permute-start(f32[40,512]{1,0:T(8,128)S(1)} %concatenate.41), channel_id=1, source_target_pairs={{0,64},{32,96},{64,0},{96,32},{1,65},{33,97},{65,1},{97,33},{2,66}... | collective-permute-start | bytes 245768 | tf_op jit(solution)/shard_map/ppermute | solution.py:157
  42.6 2.2 %collective-permute-done.1 = f32[40,512]{1,0:T(8,128)S(1)} collective-permute-done((f32[40,512]{1,0:T(8,128)S(1)}, f32[40,512]{1,0:T(8,128)S(1)}, u32[]{:S(2)}, u32[]{:S(2)}) %collective-permute-start.1) | collective-permute-done | bytes 81952 | tf_op jit(solution)/shard_map/ppermute | solution.py:157
  44.9 3.2 %collective-permute-start.2 = (f32[24,512]{1,0:T(8,128)S(1)}, f32[24,512]{1,0:T(8,128)S(1)}, u32[]{:S(2)}, u32[]{:S(2)}) collective-permute-start(f32[24,512]{1,0:T(8,128)S(1)} %concatenate.42), channel_id=1, source_target_pairs={{0,32},{32,0},{64,96},{96,64},{1,33},{33,1},{65,97},{97,65},{2,34}... | collective-permute-start | bytes 147464 | tf_op jit(solution)/shard_map/ppermute | solution.py:157
  50.0 8.8 %collective-permute-start.3 = (f32[24,512]{1,0:T(8,128)S(1)}, f32[24,512]{1,0:T(8,128)S(1)}, u32[]{:S(2)}, u32[]{:S(2)}) collective-permute-start(f32[24,512]{1,0:T(8,128)S(1)} %maximum_add_fusion.1), channel_id=1, source_target_pairs={{0,128},{128,0},{256,384},{384,256},{1,129},{129,1},{257,385},{385... | collective-permute-start | bytes 147464 | tf_op jit(solution)/shard_map/ppermute | solution.py:157
  58.8 2.7 %collective-permute-done.3 = f32[24,512]{1,0:T(8,128)S(1)} collective-permute-done((f32[24,512]{1,0:T(8,128)S(1)}, f32[24,512]{1,0:T(8,128)S(1)}, u32[]{:S(2)}, u32[]{:S(2)}) %collective-permute-start.3) | collective-permute-done | bytes 49184 | tf_op jit(solution)/shard_map/ppermute | solution.py:157
  61.5 4.8 %collective-permute-start.4 = (bf16[4,512,512]{2,1,0:T(8,128)(2,1)S(1)}, bf16[4,512,512]{2,1,0:T(8,128)(2,1)}, u32[]{:S(2)}, u32[]{:S(2)}) collective-permute-start(bf16[4,512,512]{2,1,0:T(8,128)(2,1)S(1)} %all-to-all-done.1.own_ref), channel_id=1, source_target_pairs={{0,1},{1,0},{2,3},{3,2},{4,5},{5,4},{6,7},{7,6},{8,9},{9,8},{10,11... | collective-permute-start | bytes 6291464 | tf_op jit(solution)/shard_map/ppermute | solution.py:189
  67.1 4.5 %all-to-all-start.2 = ((f32[4,24,512]{2,1,0:T(8,128)}), f32[4,24,512]{2,1,0:T(8,128)S(1)}, u32[]{:S(2)}, u32[]{:S(2)}) async-start(f32[4,24,512]{2,1,0:T(8,128)} %broadcast_in_dim.10), calls=%async_computation.2 | async-start | bytes 393216 | tf_op jit(solution)/shard_map/all_to_all | solution.py:153
  72.3 5.5 %shard_map.105 = (bf16[4,512,512]{2,1,0:T(8,128)(2,1)}, f32[8,128]{1,0:T(8,128)}) custom-call(s32[85]{0:T(128)} %bitcast.15, s32[1]{0:T(128)} %bitcast.10.live_ref, s32[1]{0:T(128)} %bitcast.1.core_ref, bf16[85,128,128]{2,1,0:T(8,128)(2,1)} %bitcast.11, bf16[4,512,512]{2,1,0:T(8,128)(2,1)} %copy-done.4, bf16[4,512,512]{2,1,0:T(8,128)(2,1)} %collective-permute-done.4.other_ref), custom_call_target="tpu_custom_call" | custom-call | flops 1426063360 | bytes 44564480 | tf_op jit(solution)/shard_map/pallas_call | solution.py:193
  77.8 10.0 %all-to-all-start.3 = ((bf16[4,512,512]{2,1,0:T(8,128)(2,1)}), bf16[4,512,512]{2,1,0:T(8,128)(2,1)S(1)}, u32[]{:S(2)}, u32[]{:S(2)}) async-start(bf16[4,512,512]{2,1,0:T(8,128)(2,1)} %get-tuple-element.19), calls=%async_computation.3 | async-start | bytes 4194304 | tf_op jit(solution)/shard_map/all_to_all | solution.py:153
  87.8 10.6 %collective-permute-start.5 = (f32[24,512]{1,0:T(8,128)S(1)}, f32[24,512]{1,0:T(8,128)S(1)}, u32[]{:S(2)}, u32[]{:S(2)}) collective-permute-start(f32[24,512]{1,0:T(8,128)S(1)} %reduce_sum.9), channel_id=1, source_target_pairs={{0,256},{128,384},{256,0},{384,128},{1,257},{129,385},{257,1},{385... | collective-permute-start | bytes 147464 | tf_op jit(solution)/shard_map/ppermute | solution.py:157
  98.4 3.0 %collective-permute-done.5 = f32[24,512]{1,0:T(8,128)S(1)} collective-permute-done((f32[24,512]{1,0:T(8,128)S(1)}, f32[24,512]{1,0:T(8,128)S(1)}, u32[]{:S(2)}, u32[]{:S(2)}) %collective-permute-start.5) | collective-permute-done | bytes 49184 | tf_op jit(solution)/shard_map/ppermute | solution.py:157
  101.4 1.9 %collective-permute-start.6 = (bf16[16,512]{1,0:T(8,128)(2,1)S(1)}, bf16[16,512]{1,0:T(8,128)(2,1)S(1)}, u32[]{:S(2)}, u32[]{:S(2)}) collective-permute-start(bf16[16,512]{1,0:T(8,128)(2,1)S(1)} %slice.41), channel_id=1, source_target_pairs={{0,8},{8,0},{16,24},{24,16},{1,9},{9,1},{17,25},{25,17},{2,10},{10... | collective-permute-start | bytes 49160 | tf_op jit(solution)/shard_map/ppermute | solution.py:157
  103.3 2.6 %collective-permute-done.6 = bf16[16,512]{1,0:T(8,128)(2,1)S(1)} collective-permute-done((bf16[16,512]{1,0:T(8,128)(2,1)S(1)}, bf16[16,512]{1,0:T(8,128)(2,1)S(1)}, u32[]{:S(2)}, u32[]{:S(2)}) %collective-permute-start.6) | collective-permute-done | bytes 16416 | tf_op jit(solution)/shard_map/ppermute | solution.py:157
  105.9 1.9 %collective-permute-start.7 = (bf16[32,512]{1,0:T(8,128)(2,1)S(1)}, bf16[32,512]{1,0:T(8,128)(2,1)S(1)}, u32[]{:S(2)}, u32[]{:S(2)}) collective-permute-start(bf16[32,512]{1,0:T(8,128)(2,1)S(1)} %pad_maximum_fusion.3), channel_id=1, source_target_pairs={{0,16},{8,24},{16,0},{24,8},{1,17},{9,25},{17,1},{25,9},{2,18},{10... | collective-permute-start | bytes 98312 | tf_op jit(solution)/shard_map/ppermute | solution.py:157
  107.8 4.8 %collective-permute-done.7 = bf16[32,512]{1,0:T(8,128)(2,1)S(1)} collective-permute-done((bf16[32,512]{1,0:T(8,128)(2,1)S(1)}, bf16[32,512]{1,0:T(8,128)(2,1)S(1)}, u32[]{:S(2)}, u32[]{:S(2)}) %collective-permute-start.7) | collective-permute-done | bytes 32800 | tf_op jit(solution)/shard_map/ppermute | solution.py:157
  113.7 10.0 %all-to-all-start.4 = ((bf16[4,128,512]{2,1,0:T(8,128)(2,1)}), bf16[4,128,512]{2,1,0:T(8,128)(2,1)S(1)}, u32[]{:S(2)}, u32[]{:S(2)}) async-start(bf16[4,128,512]{2,1,0:T(8,128)(2,1)} %bitcast.6), calls=%async_computation.4 | async-start | bytes 1048576 | tf_op jit(solution)/shard_map/all_to_all | solution.py:153
  123.7 4.8 %collective-permute-start.8 = (bf16[64,512]{1,0:T(8,128)(2,1)S(1)}, bf16[64,512]{1,0:T(8,128)(2,1)S(1)}, u32[]{:S(2)}, u32[]{:S(2)}) collective-permute-start(bf16[64,512]{1,0:T(8,128)(2,1)S(1)} %pad_maximum_fusion.2.refs_0_), channel_id=1, source_target_pairs={{0,64},{32,96},{64,0},{96,32},{1,65},{33,97},{65,1},{97,33},{2,66}... | collective-permute-start | bytes 196616 | tf_op jit(solution)/shard_map/ppermute | solution.py:157
  130.2 3.3 %collective-permute-start.9 = (bf16[128,512]{1,0:T(8,128)(2,1)S(1)}, bf16[128,512]{1,0:T(8,128)(2,1)S(1)}, u32[]{:S(2)}, u32[]{:S(2)}) collective-permute-start(bf16[128,512]{1,0:T(8,128)(2,1)S(1)} %pad_maximum_fusion.1), channel_id=1, source_target_pairs={{0,32},{32,0},{64,96},{96,64},{1,33},{33,1},{65,97},{97,65},{2,34}... | collective-permute-start | bytes 393224 | tf_op jit(solution)/shard_map/ppermute | solution.py:157
  133.5 2.7 %collective-permute-done.9.refs_2_ = bf16[128,512]{1,0:T(8,128)(2,1)S(1)} collective-permute-done((bf16[128,512]{1,0:T(8,128)(2,1)S(1)}, bf16[128,512]{1,0:T(8,128)(2,1)S(1)}, u32[]{:S(2)}, u32[]{:S(2)}) %collective-permute-start.9) | collective-permute-done | bytes 131104 | tf_op jit(solution)/shard_map/ppermute | solution.py:157
  136.2 6.3 %collective-permute-start.10 = (bf16[256,512]{1,0:T(8,128)(2,1)S(1)}, bf16[256,512]{1,0:T(8,128)(2,1)S(1)}, u32[]{:S(2)}, u32[]{:S(2)}) collective-permute-start(bf16[256,512]{1,0:T(8,128)(2,1)S(1)} %pad_maximum_fusion), channel_id=1, source_target_pairs={{0,1},{1,0},{2,3},{3,2},{4,5},{5,4},{6,7},{7,6},{8,9},{9,8},{10,11... | collective-permute-start | bytes 786440 | tf_op jit(solution)/shard_map/ppermute | solution.py:157
  145.2 6.9 %all-to-all-done.4.in_ref = bf16[4,128,512]{2,1,0:T(8,128)(2,1)S(1)} async-done(((bf16[4,128,512]{2,1,0:T(8,128)(2,1)}), bf16[4,128,512]{2,1,0:T(8,128)(2,1)S(1)}, u32[]{:S(2)}, u32[]{:S(2)}) %all-to-all-start.4) | async-done | bytes 524320 | tf_op jit(solution)/shard_map/all_to_all | solution.py:153
  (48 shorter events, 15.7 us)
Async XLA Ops:
  0.6 1.0 copy-start.1
  1.6 0.9 copy-start.2
  2.5 0.9 copy-start.3
  27.0 34.5 %all-to-all-start.1 = ((bf16[4,512,512]{2,1,0:T(8,128)(2,1)}), bf16[4,512,512]{2,1,0:T(8,128)(2,1)S(1)}, u32[]{:S(2)}, u32[]{:S(2)}) async-start(bf16[4,512,512]{2,1,0:T(8,128)(2,1)} %broadcast_in_dim.9), calls=%async_computation.1 | async-start | bytes 4194304 | tf_op jit(solution)/shard_map/all_to_all | solution.py:153
  32.7 5.0 %collective-permute-start = (f32[72,512]{1,0:T(8,128)S(1)}, f32[72,512]{1,0:T(8,128)S(1)}, u32[]{:S(2)}, u32[]{:S(2)}) collective-permute-start(f32[72,512]{1,0:T(8,128)S(1)} %get-tuple-element.14), channel_id=1, source_target_pairs={{0,1},{1,0},{2,3},{3,2},{4,5},{5,4},{6,7},{7,6},{8,9},{9,8},{10,11... | collective-permute-start | bytes 442376 | tf_op jit(solution)/shard_map/ppermute | solution.py:157
  37.8 7.1 %collective-permute-start.1 = (f32[40,512]{1,0:T(8,128)S(1)}, f32[40,512]{1,0:T(8,128)S(1)}, u32[]{:S(2)}, u32[]{:S(2)}) collective-permute-start(f32[40,512]{1,0:T(8,128)S(1)} %concatenate.41), channel_id=1, source_target_pairs={{0,64},{32,96},{64,0},{96,32},{1,65},{33,97},{65,1},{97,33},{2,66}... | collective-permute-start | bytes 245768 | tf_op jit(solution)/shard_map/ppermute | solution.py:157
  44.9 5.1 %collective-permute-start.2 = (f32[24,512]{1,0:T(8,128)S(1)}, f32[24,512]{1,0:T(8,128)S(1)}, u32[]{:S(2)}, u32[]{:S(2)}) collective-permute-start(f32[24,512]{1,0:T(8,128)S(1)} %concatenate.42), channel_id=1, source_target_pairs={{0,32},{32,0},{64,96},{96,64},{1,33},{33,1},{65,97},{97,65},{2,34}... | collective-permute-start | bytes 147464 | tf_op jit(solution)/shard_map/ppermute | solution.py:157
  50.0 11.5 %collective-permute-start.3 = (f32[24,512]{1,0:T(8,128)S(1)}, f32[24,512]{1,0:T(8,128)S(1)}, u32[]{:S(2)}, u32[]{:S(2)}) collective-permute-start(f32[24,512]{1,0:T(8,128)S(1)} %maximum_add_fusion.1), channel_id=1, source_target_pairs={{0,128},{128,0},{256,384},{384,256},{1,129},{129,1},{257,385},{385... | collective-permute-start | bytes 147464 | tf_op jit(solution)/shard_map/ppermute | solution.py:157
  61.5 10.7 %copy-start.4 = (bf16[4,512,512]{2,1,0:T(8,128)(2,1)}, bf16[4,512,512]{2,1,0:T(8,128)(2,1)S(1)}, u32[]{:S(2)}) copy-start(bf16[4,512,512]{2,1,0:T(8,128)(2,1)S(1)} %all-to-all-done.1.own_ref) | copy-start | bytes 6291460
  61.5 10.7 %collective-permute-start.4 = (bf16[4,512,512]{2,1,0:T(8,128)(2,1)S(1)}, bf16[4,512,512]{2,1,0:T(8,128)(2,1)}, u32[]{:S(2)}, u32[]{:S(2)}) collective-permute-start(bf16[4,512,512]{2,1,0:T(8,128)(2,1)S(1)} %all-to-all-done.1.own_ref), channel_id=1, source_target_pairs={{0,1},{1,0},{2,3},{3,2},{4,5},{5,4},{6,7},{7,6},{8,9},{9,8},{10,11... | collective-permute-start | bytes 6291464 | tf_op jit(solution)/shard_map/ppermute | solution.py:189
  67.1 10.7 %all-to-all-start.2 = ((f32[4,24,512]{2,1,0:T(8,128)}), f32[4,24,512]{2,1,0:T(8,128)S(1)}, u32[]{:S(2)}, u32[]{:S(2)}) async-start(f32[4,24,512]{2,1,0:T(8,128)} %broadcast_in_dim.10), calls=%async_computation.2 | async-start | bytes 393216 | tf_op jit(solution)/shard_map/all_to_all | solution.py:153
  77.8 34.8 %all-to-all-start.3 = ((bf16[4,512,512]{2,1,0:T(8,128)(2,1)}), bf16[4,512,512]{2,1,0:T(8,128)(2,1)S(1)}, u32[]{:S(2)}, u32[]{:S(2)}) async-start(bf16[4,512,512]{2,1,0:T(8,128)(2,1)} %get-tuple-element.19), calls=%async_computation.3 | async-start | bytes 4194304 | tf_op jit(solution)/shard_map/all_to_all | solution.py:153
  87.8 13.5 %collective-permute-start.5 = (f32[24,512]{1,0:T(8,128)S(1)}, f32[24,512]{1,0:T(8,128)S(1)}, u32[]{:S(2)}, u32[]{:S(2)}) collective-permute-start(f32[24,512]{1,0:T(8,128)S(1)} %reduce_sum.9), channel_id=1, source_target_pairs={{0,256},{128,384},{256,0},{384,128},{1,257},{129,385},{257,1},{385... | collective-permute-start | bytes 147464 | tf_op jit(solution)/shard_map/ppermute | solution.py:157
  101.4 41.2 %copy-start.5 = (s32[32]{0:T(128)S(1)}, s32[32]{0:T(128)}, u32[]{:S(2)}) copy-start(s32[32]{0:T(128)} %constant.23.clone) | copy-start | bytes 388
  101.4 4.5 %collective-permute-start.6 = (bf16[16,512]{1,0:T(8,128)(2,1)S(1)}, bf16[16,512]{1,0:T(8,128)(2,1)S(1)}, u32[]{:S(2)}, u32[]{:S(2)}) collective-permute-start(bf16[16,512]{1,0:T(8,128)(2,1)S(1)} %slice.41), channel_id=1, source_target_pairs={{0,8},{8,0},{16,24},{24,16},{1,9},{9,1},{17,25},{25,17},{2,10},{10... | collective-permute-start | bytes 49160 | tf_op jit(solution)/shard_map/ppermute | solution.py:157
  105.9 6.7 %collective-permute-start.7 = (bf16[32,512]{1,0:T(8,128)(2,1)S(1)}, bf16[32,512]{1,0:T(8,128)(2,1)S(1)}, u32[]{:S(2)}, u32[]{:S(2)}) collective-permute-start(bf16[32,512]{1,0:T(8,128)(2,1)S(1)} %pad_maximum_fusion.3), channel_id=1, source_target_pairs={{0,16},{8,24},{16,0},{24,8},{1,17},{9,25},{17,1},{25,9},{2,18},{10... | collective-permute-start | bytes 98312 | tf_op jit(solution)/shard_map/ppermute | solution.py:157
  113.7 38.4 %copy-start = (bf16[512,512]{1,0:T(8,128)(2,1)S(1)}, bf16[512,512]{1,0:T(8,128)(2,1)}, u32[]{:S(2)}) copy-start(bf16[512,512]{1,0:T(8,128)(2,1)} %weight_ref.1) | copy-start | bytes 1572868
  113.7 38.4 %all-to-all-start.4 = ((bf16[4,128,512]{2,1,0:T(8,128)(2,1)}), bf16[4,128,512]{2,1,0:T(8,128)(2,1)S(1)}, u32[]{:S(2)}, u32[]{:S(2)}) async-start(bf16[4,128,512]{2,1,0:T(8,128)(2,1)} %bitcast.6), calls=%async_computation.4 | async-start | bytes 1048576 | tf_op jit(solution)/shard_map/all_to_all | solution.py:153
  123.7 6.5 %collective-permute-start.8 = (bf16[64,512]{1,0:T(8,128)(2,1)S(1)}, bf16[64,512]{1,0:T(8,128)(2,1)S(1)}, u32[]{:S(2)}, u32[]{:S(2)}) collective-permute-start(bf16[64,512]{1,0:T(8,128)(2,1)S(1)} %pad_maximum_fusion.2.refs_0_), channel_id=1, source_target_pairs={{0,64},{32,96},{64,0},{96,32},{1,65},{33,97},{65,1},{97,33},{2,66}... | collective-permute-start | bytes 196616 | tf_op jit(solution)/shard_map/ppermute | solution.py:157
  130.2 6.0 %collective-permute-start.9 = (bf16[128,512]{1,0:T(8,128)(2,1)S(1)}, bf16[128,512]{1,0:T(8,128)(2,1)S(1)}, u32[]{:S(2)}, u32[]{:S(2)}) collective-permute-start(bf16[128,512]{1,0:T(8,128)(2,1)S(1)} %pad_maximum_fusion.1), channel_id=1, source_target_pairs={{0,32},{32,0},{64,96},{96,64},{1,33},{33,1},{65,97},{97,65},{2,34}... | collective-permute-start | bytes 393224 | tf_op jit(solution)/shard_map/ppermute | solution.py:157
  136.2 7.4 %collective-permute-start.10 = (bf16[256,512]{1,0:T(8,128)(2,1)S(1)}, bf16[256,512]{1,0:T(8,128)(2,1)S(1)}, u32[]{:S(2)}, u32[]{:S(2)}) collective-permute-start(bf16[256,512]{1,0:T(8,128)(2,1)S(1)} %pad_maximum_fusion), channel_id=1, source_target_pairs={{0,1},{1,0},{2,3},{3,2},{4,5},{5,4},{6,7},{7,6},{8,9},{9,8},{10,11... | collective-permute-start | bytes 786440 | tf_op jit(solution)/shard_map/ppermute | solution.py:157

commit v10 on v9

--- a/solution.py
+++ b/solution.py
@@ -64,18 +64,6 @@
     mark_ref[...] = jnp.zeros_like(mark_ref)
     for copy in copies:
         copy.wait()
-
-
-def pack_kernel(grad_ref, mask_ref, features_ref, out_ref):
-    n_dst, width, n_feat = out_ref.shape
-    blk = grad_ref.shape[0]
-    n_mine = n_feat // n_dst
-    grad_pre = grad_ref[...] * mask_ref[...].astype(BF16)
-    for z in range(n_dst):
-        out_ref[z, :blk, :] = grad_pre
-        for k in range(n_feat // n_mine):
-            rows = slice(k * (width - blk), (k + 1) * (width - blk))
-            out_ref[z, blk:, k * n_mine : (k + 1) * n_mine] = features_ref[rows, z * n_mine : (z + 1) * n_mine]
 
 
 def terms_kernel(place_ref, got_ref, keep_ref, send_ref, sum_ref, *, blk):
@@ -164,11 +152,10 @@
     n_pair = n_feat // (n_zl * n_y)
     n_slice = n_pair // n_core
     n_mine = n_feat // n_zl
-    sent = call(
-        pack_kernel,
-        jax.ShapeDtypeStruct((n_zl, blk + blk * n_mine // n_feat, n_feat), BF16),
-        n_in=3,
-    )(grad_out, relu_mask, aggregated)
+    columns = aggregated.reshape(n_feat // n_mine, blk * n_mine // n_feat, n_zl, n_mine).transpose(2, 1, 0, 3)
+    columns = columns.reshape(n_zl, blk * n_mine // n_feat, n_feat)
+    grad_pre = grad_out * relu_mask.astype(BF16)
+    sent = jnp.concatenate([jnp.broadcast_to(grad_pre, (n_zl, blk, n_feat)), columns], axis=1)
     got = swap(sent, "zl")
     core, y_index = (lax.axis_index(a).astype(jnp.int32).reshape(1) for a in ("core", "y"))
     half = jax.ShapeDtypeStruct((n_y * n_slice + 8, n_feat), F32)
@@ -220,10 +207,8 @@
     factor = 1.0 / math.sqrt(blk * n_zh * n_y * n_zl * n_x * n_core)
     terms = terms * factor
     slices = terms[:n_slice].astype(BF16)
-    offsets = [0]
-    for bit in (1, 2):
-        slices = jnp.concatenate([slices, trade(slices, "zl", bit)], axis=0)
-        offsets += [o ^ (bit * n_y * n_core) for o in offsets]
+    slices = jnp.concatenate([slices] + [trade(slices, "zl", k) for k in range(1, n_zl)], axis=0)
+    offsets = [k * n_y * n_core for k in range(n_zl)]
     got = swap(sent, "y")
     sent, mark = call(fold_kernel, jax.ShapeDtypeStruct((n_zh * blk, n_feat), BF16), marked=True)(got)
     slices, sent = lax.optimization_barrier((slices, sent))

time: 156 us -> 156 us (level)
  the two profiles are of different devices: /device:TPU:1 before, /device:TPU:6 now
where the time goes in v10:
time: 156 us; the launch traced here: 155 us
  starting transfers between devices  80.7 us (52%)
  waiting for transfers between devices  32.3 us (21%)
  blocking collectives  23 us (15%)
  Pallas kernels  12.4 us (8%)
  local copies, waits for them, and re-layouts  3.99 us (3%)
  between operations  1.61 us (1%)
    ppermute x11, starting transfers between devices, trade(): lax.ppermute(value, axis, [(i, i ^ bit) for i in range(lax.axis_size(axis...  52.6 us
    all_to_all x4, starting transfers between devices, swap(): return lax.all_to_all(value, axis, split_axis=0, concat_axis=0, tiled=True)  26.1 us
    ppermute x11, waiting for transfers between devices, trade(): lax.ppermute(value, axis, [(i, i ^ bit) for i in range(lax.axis_size(axis...  23.2 us
    all_to_all x1, blocking collectives, swap(): return lax.all_to_all(value, axis, split_axis=0, concat_axis=0, tiled=True)  23 us
    all_to_all x4, waiting for transfers between devices, swap(): return lax.all_to_all(value, axis, split_axis=0, concat_axis=0, tiled=True)  9.13 us
    pallas_call x1, Pallas kernels, body(): call(functools.partial(tile_kernel, group=group, n_x=n_x), jax.ShapeDtype...  7.66 us
  transfers between devices with their start and end apart: 16, of which 10 were waited for; matrix products, arithmetic and copies ran while one was open for 1% of the time, Pallas kernels for 7%

profile of v10, /device:TPU:6, one launch (start us, length us, event | category | flops | bytes accessed | tf_op | source)
XLA Modules:
  0.0 155.3 jit_solution(16366036309278357600)
XLA Ops:
  2.9 23.0 %all_to_all.25.got_ref = bf16[4,160,512]{2,1,0:T(8,128)(2,1)S(1)} all-to-all(bf16[4,160,512]{2,1,0:T(8,128)(2,1)S(1)} %pad_maximum_fusion), channel_id=1, replica_groups=mesh['zh'=4,'y'=4,'zl'=4,'x'=4,'core'=2] {'zl'}, dimensions={0} | all-to-all | bytes 1310720 | tf_op jit(solution)/shard_map/all_to_all | solution.py:141
  27.4 4.8 %all-to-all-start.1 = ((bf16[4,512,512]{2,1,0:T(8,128)(2,1)}), bf16[4,512,512]{2,1,0:T(8,128)(2,1)S(1)}, u32[]{:S(2)}, u32[]{:S(2)}) async-start(bf16[4,512,512]{2,1,0:T(8,128)(2,1)} %broadcast_in_dim.13), calls=%async_computation.1 | async-start | bytes 4194304 | tf_op jit(solution)/shard_map/all_to_all | solution.py:141
  36.5 5.1 %collective-permute-start.1 = (f32[40,512]{1,0:T(8,128)S(1)}, f32[40,512]{1,0:T(8,128)S(1)}, u32[]{:S(2)}, u32[]{:S(2)}) collective-permute-start(f32[40,512]{1,0:T(8,128)S(1)} %concatenate.40), channel_id=1, source_target_pairs={{0,64},{32,96},{64,0},{96,32},{1,65},{33,97},{65,1},{97,33},{2,66}... | collective-permute-start | bytes 245768 | tf_op jit(solution)/shard_map/ppermute | solution.py:145
  41.7 2.8 %collective-permute-done.1 = f32[40,512]{1,0:T(8,128)S(1)} collective-permute-done((f32[40,512]{1,0:T(8,128)S(1)}, f32[40,512]{1,0:T(8,128)S(1)}, u32[]{:S(2)}, u32[]{:S(2)}) %collective-permute-start.1) | collective-permute-done | bytes 81952 | tf_op jit(solution)/shard_map/ppermute | solution.py:145
  44.5 3.5 %collective-permute-start.2 = (f32[24,512]{1,0:T(8,128)S(1)}, f32[24,512]{1,0:T(8,128)S(1)}, u32[]{:S(2)}, u32[]{:S(2)}) collective-permute-start(f32[24,512]{1,0:T(8,128)S(1)} %concatenate.41), channel_id=1, source_target_pairs={{0,32},{32,0},{64,96},{96,64},{1,33},{33,1},{65,97},{97,65},{2,34}... | collective-permute-start | bytes 147464 | tf_op jit(solution)/shard_map/ppermute | solution.py:145
  48.0 2.5 %collective-permute-done.2 = f32[24,512]{1,0:T(8,128)S(1)} collective-permute-done((f32[24,512]{1,0:T(8,128)S(1)}, f32[24,512]{1,0:T(8,128)S(1)}, u32[]{:S(2)}, u32[]{:S(2)}) %collective-permute-start.2) | collective-permute-done | bytes 49184 | tf_op jit(solution)/shard_map/ppermute | solution.py:145
  50.5 9.1 %collective-permute-start.3 = (f32[24,512]{1,0:T(8,128)S(1)}, f32[24,512]{1,0:T(8,128)S(1)}, u32[]{:S(2)}, u32[]{:S(2)}) collective-permute-start(f32[24,512]{1,0:T(8,128)S(1)} %maximum_add_fusion.1), channel_id=1, source_target_pairs={{0,128},{128,0},{256,384},{384,256},{1,129},{129,1},{257,385},{385... | collective-permute-start | bytes 147464 | tf_op jit(solution)/shard_map/ppermute | solution.py:145
  59.6 3.3 %collective-permute-done.3 = f32[24,512]{1,0:T(8,128)S(1)} collective-permute-done((f32[24,512]{1,0:T(8,128)S(1)}, f32[24,512]{1,0:T(8,128)S(1)}, u32[]{:S(2)}, u32[]{:S(2)}) %collective-permute-start.3) | collective-permute-done | bytes 49184 | tf_op jit(solution)/shard_map/ppermute | solution.py:145
  62.9 1.9 %collective-permute-start.4 = (bf16[4,512,512]{2,1,0:T(8,128)(2,1)S(1)}, bf16[4,512,512]{2,1,0:T(8,128)(2,1)}, u32[]{:S(2)}, u32[]{:S(2)}) collective-permute-start(bf16[4,512,512]{2,1,0:T(8,128)(2,1)S(1)} %all-to-all-done.1.own_ref), channel_id=1, source_target_pairs={{0,1},{1,0},{2,3},{3,2},{4,5},{5,4},{6,7},{7,6},{8,9},{9,8},{10,11... | collective-permute-start | bytes 6291464 | tf_op jit(solution)/shard_map/ppermute | solution.py:176
  65.5 4.8 %all-to-all-start.2 = ((f32[4,24,512]{2,1,0:T(8,128)}), f32[4,24,512]{2,1,0:T(8,128)S(1)}, u32[]{:S(2)}, u32[]{:S(2)}) async-start(f32[4,24,512]{2,1,0:T(8,128)} %broadcast_in_dim.14), calls=%async_computation.2 | async-start | bytes 393216 | tf_op jit(solution)/shard_map/all_to_all | solution.py:141
  71.0 7.7 %shard_map.104 = (bf16[4,512,512]{2,1,0:T(8,128)(2,1)}, f32[8,128]{1,0:T(8,128)}) custom-call(s32[85]{0:T(128)} %bitcast.19, s32[1]{0:T(128)} %bitcast.13.live_ref, s32[1]{0:T(128)} %bitcast.2.core_ref, bf16[85,128,128]{2,1,0:T(8,128)(2,1)} %bitcast.14, bf16[4,512,512]{2,1,0:T(8,128)(2,1)} %copy-done.1, bf16[4,512,512]{2,1,0:T(8,128)(2,1)} %collective-permute-done.4.other_ref), custom_call_target="tpu_custom_call" | custom-call | flops 1426063360 | bytes 44564480 | tf_op jit(solution)/shard_map/pallas_call | solution.py:180
  78.6 5.4 %all-to-all-start.3 = ((bf16[4,512,512]{2,1,0:T(8,128)(2,1)}), bf16[4,512,512]{2,1,0:T(8,128)(2,1)S(1)}, u32[]{:S(2)}, u32[]{:S(2)}) async-start(bf16[4,512,512]{2,1,0:T(8,128)(2,1)} %get-tuple-element.19), calls=%async_computation.3 | async-start | bytes 4194304 | tf_op jit(solution)/shard_map/all_to_all | solution.py:141
  84.1 11.9 %collective-permute-start.5 = (f32[24,512]{1,0:T(8,128)S(1)}, f32[24,512]{1,0:T(8,128)S(1)}, u32[]{:S(2)}, u32[]{:S(2)}) collective-permute-start(f32[24,512]{1,0:T(8,128)S(1)} %reduce_sum.9), channel_id=1, source_target_pairs={{0,256},{128,384},{256,0},{384,128},{1,257},{129,385},{257,1},{385... | collective-permute-start | bytes 147464 | tf_op jit(solution)/shard_map/ppermute | solution.py:145
  96.0 3.0 %collective-permute-done.5 = f32[24,512]{1,0:T(8,128)S(1)} collective-permute-done((f32[24,512]{1,0:T(8,128)S(1)}, f32[24,512]{1,0:T(8,128)S(1)}, u32[]{:S(2)}, u32[]{:S(2)}) %collective-permute-start.5) | collective-permute-done | bytes 49184 | tf_op jit(solution)/shard_map/ppermute | solution.py:145
  99.0 2.7 %collective-permute-start.6 = (bf16[16,512]{1,0:T(8,128)(2,1)S(1)}, bf16[16,512]{1,0:T(8,128)(2,1)S(1)}, u32[]{:S(2)}, u32[]{:S(2)}) collective-permute-start(bf16[16,512]{1,0:T(8,128)(2,1)S(1)} %slice.41), channel_id=1, source_target_pairs={{0,8},{8,0},{16,24},{24,16},{1,9},{9,1},{17,25},{25,17},{2,10},{10... | collective-permute-start | bytes 49160 | tf_op jit(solution)/shard_map/ppermute | solution.py:145
  101.7 4.1 %collective-permute-start.7 = (bf16[16,512]{1,0:T(8,128)(2,1)S(1)}, bf16[16,512]{1,0:T(8,128)(2,1)S(1)}, u32[]{:S(2)}, u32[]{:S(2)}) collective-permute-start(bf16[16,512]{1,0:T(8,128)(2,1)S(1)} %slice.41), channel_id=1, source_target_pairs={{0,16},{8,24},{16,0},{24,8},{1,17},{9,25},{17,1},{25,9},{2,18},{10... | collective-permute-start | bytes 49160 | tf_op jit(solution)/shard_map/ppermute | solution.py:145
  105.8 3.3 %collective-permute-start.8 = (bf16[16,512]{1,0:T(8,128)(2,1)S(1)}, bf16[16,512]{1,0:T(8,128)(2,1)S(1)}, u32[]{:S(2)}, u32[]{:S(2)}) collective-permute-start(bf16[16,512]{1,0:T(8,128)(2,1)S(1)} %slice.41), channel_id=1, source_target_pairs={{0,24},{8,16},{16,8},{24,0},{1,25},{9,17},{17,9},{25,1},{2,26},{10... | collective-permute-start | bytes 49160 | tf_op jit(solution)/shard_map/ppermute | solution.py:145
  109.2 4.1 %collective-permute-done.8 = bf16[16,512]{1,0:T(8,128)(2,1)S(1)} collective-permute-done((bf16[16,512]{1,0:T(8,128)(2,1)S(1)}, bf16[16,512]{1,0:T(8,128)(2,1)S(1)}, u32[]{:S(2)}, u32[]{:S(2)}) %collective-permute-start.8) | collective-permute-done | bytes 16416 | tf_op jit(solution)/shard_map/ppermute | solution.py:145
  114.3 11.2 %all-to-all-start.4 = ((bf16[4,128,512]{2,1,0:T(8,128)(2,1)}), bf16[4,128,512]{2,1,0:T(8,128)(2,1)S(1)}, u32[]{:S(2)}, u32[]{:S(2)}) async-start(bf16[4,128,512]{2,1,0:T(8,128)(2,1)} %bitcast.7), calls=%async_computation.4 | async-start | bytes 1048576 | tf_op jit(solution)/shard_map/all_to_all | solution.py:141
  125.5 5.3 %collective-permute-start.9 = (bf16[64,512]{1,0:T(8,128)(2,1)S(1)}, bf16[64,512]{1,0:T(8,128)(2,1)S(1)}, u32[]{:S(2)}, u32[]{:S(2)}) collective-permute-start(bf16[64,512]{1,0:T(8,128)(2,1)S(1)} %pad_maximum_fusion.3.refs_0_), channel_id=1, source_target_pairs={{0,64},{32,96},{64,0},{96,32},{1,65},{33,97},{65,1},{97,33},{2,66}... | collective-permute-start | bytes 196616 | tf_op jit(solution)/shard_map/ppermute | solution.py:145
  130.8 2.4 %collective-permute-done.9.refs_1_ = bf16[64,512]{1,0:T(8,128)(2,1)S(1)} collective-permute-done((bf16[64,512]{1,0:T(8,128)(2,1)S(1)}, bf16[64,512]{1,0:T(8,128)(2,1)S(1)}, u32[]{:S(2)}, u32[]{:S(2)}) %collective-permute-start.9) | collective-permute-done | bytes 65568 | tf_op jit(solution)/shard_map/ppermute | solution.py:145
  133.2 3.8 %collective-permute-start.10 = (bf16[128,512]{1,0:T(8,128)(2,1)S(1)}, bf16[128,512]{1,0:T(8,128)(2,1)S(1)}, u32[]{:S(2)}, u32[]{:S(2)}) collective-permute-start(bf16[128,512]{1,0:T(8,128)(2,1)S(1)} %pad_maximum_fusion.2), channel_id=1, source_target_pairs={{0,32},{32,0},{64,96},{96,64},{1,33},{33,1},{65,97},{97,65},{2,34}... | collective-permute-start | bytes 393224 | tf_op jit(solution)/shard_map/ppermute | solution.py:145
  137.0 3.1 %collective-permute-done.10.refs_2_ = bf16[128,512]{1,0:T(8,128)(2,1)S(1)} collective-permute-done((bf16[128,512]{1,0:T(8,128)(2,1)S(1)}, bf16[128,512]{1,0:T(8,128)(2,1)S(1)}, u32[]{:S(2)}, u32[]{:S(2)}) %collective-permute-start.10) | collective-permute-done | bytes 131104 | tf_op jit(solution)/shard_map/ppermute | solution.py:145
  145.1 9.1 %all-to-all-done.4.in_ref = bf16[4,128,512]{2,1,0:T(8,128)(2,1)S(1)} async-done(((bf16[4,128,512]{2,1,0:T(8,128)(2,1)}), bf16[4,128,512]{2,1,0:T(8,128)(2,1)S(1)}, u32[]{:S(2)}, u32[]{:S(2)}) %all-to-all-start.4) | async-done | bytes 524320 | tf_op jit(solution)/shard_map/all_to_all | solution.py:141
  (48 shorter events, 16.1 us)
Async XLA Ops:
  27.4 35.4 %all-to-all-start.1 = ((bf16[4,512,512]{2,1,0:T(8,128)(2,1)}), bf16[4,512,512]{2,1,0:T(8,128)(2,1)S(1)}, u32[]{:S(2)}, u32[]{:S(2)}) async-start(bf16[4,512,512]{2,1,0:T(8,128)(2,1)} %broadcast_in_dim.13), calls=%async_computation.1 | async-start | bytes 4194304 | tf_op jit(solution)/shard_map/all_to_all | solution.py:141
  33.2 3.3 %collective-permute-start = (f32[72,512]{1,0:T(8,128)S(1)}, f32[72,512]{1,0:T(8,128)S(1)}, u32[]{:S(2)}, u32[]{:S(2)}) collective-permute-start(f32[72,512]{1,0:T(8,128)S(1)} %get-tuple-element.14), channel_id=1, source_target_pairs={{0,1},{1,0},{2,3},{3,2},{4,5},{5,4},{6,7},{7,6},{8,9},{9,8},{10,11... | collective-permute-start | bytes 442376 | tf_op jit(solution)/shard_map/ppermute | solution.py:145
  36.5 7.9 %collective-permute-start.1 = (f32[40,512]{1,0:T(8,128)S(1)}, f32[40,512]{1,0:T(8,128)S(1)}, u32[]{:S(2)}, u32[]{:S(2)}) collective-permute-start(f32[40,512]{1,0:T(8,128)S(1)} %concatenate.40), channel_id=1, source_target_pairs={{0,64},{32,96},{64,0},{96,32},{1,65},{33,97},{65,1},{97,33},{2,66}... | collective-permute-start | bytes 245768 | tf_op jit(solution)/shard_map/ppermute | solution.py:145
  44.5 6.0 %collective-permute-start.2 = (f32[24,512]{1,0:T(8,128)S(1)}, f32[24,512]{1,0:T(8,128)S(1)}, u32[]{:S(2)}, u32[]{:S(2)}) collective-permute-start(f32[24,512]{1,0:T(8,128)S(1)} %concatenate.41), channel_id=1, source_target_pairs={{0,32},{32,0},{64,96},{96,64},{1,33},{33,1},{65,97},{97,65},{2,34}... | collective-permute-start | bytes 147464 | tf_op jit(solution)/shard_map/ppermute | solution.py:145
  50.5 12.4 %collective-permute-start.3 = (f32[24,512]{1,0:T(8,128)S(1)}, f32[24,512]{1,0:T(8,128)S(1)}, u32[]{:S(2)}, u32[]{:S(2)}) collective-permute-start(f32[24,512]{1,0:T(8,128)S(1)} %maximum_add_fusion.1), channel_id=1, source_target_pairs={{0,128},{128,0},{256,384},{384,256},{1,129},{129,1},{257,385},{385... | collective-permute-start | bytes 147464 | tf_op jit(solution)/shard_map/ppermute | solution.py:145
  62.9 8.1 %copy-start.1 = (bf16[4,512,512]{2,1,0:T(8,128)(2,1)}, bf16[4,512,512]{2,1,0:T(8,128)(2,1)S(1)}, u32[]{:S(2)}) copy-start(bf16[4,512,512]{2,1,0:T(8,128)(2,1)S(1)} %all-to-all-done.1.own_ref) | copy-start | bytes 6291460
  62.9 8.1 %collective-permute-start.4 = (bf16[4,512,512]{2,1,0:T(8,128)(2,1)S(1)}, bf16[4,512,512]{2,1,0:T(8,128)(2,1)}, u32[]{:S(2)}, u32[]{:S(2)}) collective-permute-start(bf16[4,512,512]{2,1,0:T(8,128)(2,1)S(1)} %all-to-all-done.1.own_ref), channel_id=1, source_target_pairs={{0,1},{1,0},{2,3},{3,2},{4,5},{5,4},{6,7},{7,6},{8,9},{9,8},{10,11... | collective-permute-start | bytes 6291464 | tf_op jit(solution)/shard_map/ppermute | solution.py:176
  65.5 13.1 %all-to-all-start.2 = ((f32[4,24,512]{2,1,0:T(8,128)}), f32[4,24,512]{2,1,0:T(8,128)S(1)}, u32[]{:S(2)}, u32[]{:S(2)}) async-start(f32[4,24,512]{2,1,0:T(8,128)} %broadcast_in_dim.14), calls=%async_computation.2 | async-start | bytes 393216 | tf_op jit(solution)/shard_map/all_to_all | solution.py:141
  78.6 34.6 %all-to-all-start.3 = ((bf16[4,512,512]{2,1,0:T(8,128)(2,1)}), bf16[4,512,512]{2,1,0:T(8,128)(2,1)S(1)}, u32[]{:S(2)}, u32[]{:S(2)}) async-start(bf16[4,512,512]{2,1,0:T(8,128)(2,1)} %get-tuple-element.19), calls=%async_computation.3 | async-start | bytes 4194304 | tf_op jit(solution)/shard_map/all_to_all | solution.py:141
  84.1 57.9 %copy-start.2 = (s32[32]{0:T(128)S(1)}, s32[32]{0:T(128)}, u32[]{:S(2)}) copy-start(s32[32]{0:T(128)} %constant.23.clone) | copy-start | bytes 388
  84.1 14.9 %collective-permute-start.5 = (f32[24,512]{1,0:T(8,128)S(1)}, f32[24,512]{1,0:T(8,128)S(1)}, u32[]{:S(2)}, u32[]{:S(2)}) collective-permute-start(f32[24,512]{1,0:T(8,128)S(1)} %reduce_sum.9), channel_id=1, source_target_pairs={{0,256},{128,384},{256,0},{384,128},{1,257},{129,385},{257,1},{385... | collective-permute-start | bytes 147464 | tf_op jit(solution)/shard_map/ppermute | solution.py:145
  99.0 10.1 %collective-permute-start.6 = (bf16[16,512]{1,0:T(8,128)(2,1)S(1)}, bf16[16,512]{1,0:T(8,128)(2,1)S(1)}, u32[]{:S(2)}, u32[]{:S(2)}) collective-permute-start(bf16[16,512]{1,0:T(8,128)(2,1)S(1)} %slice.41), channel_id=1, source_target_pairs={{0,8},{8,0},{16,24},{24,16},{1,9},{9,1},{17,25},{25,17},{2,10},{10... | collective-permute-start | bytes 49160 | tf_op jit(solution)/shard_map/ppermute | solution.py:145
  101.7 7.4 %collective-permute-start.7 = (bf16[16,512]{1,0:T(8,128)(2,1)S(1)}, bf16[16,512]{1,0:T(8,128)(2,1)S(1)}, u32[]{:S(2)}, u32[]{:S(2)}) collective-permute-start(bf16[16,512]{1,0:T(8,128)(2,1)S(1)} %slice.41), channel_id=1, source_target_pairs={{0,16},{8,24},{16,0},{24,8},{1,17},{9,25},{17,1},{25,9},{2,18},{10... | collective-permute-start | bytes 49160 | tf_op jit(solution)/shard_map/ppermute | solution.py:145
  105.8 7.4 %collective-permute-start.8 = (bf16[16,512]{1,0:T(8,128)(2,1)S(1)}, bf16[16,512]{1,0:T(8,128)(2,1)S(1)}, u32[]{:S(2)}, u32[]{:S(2)}) collective-permute-start(bf16[16,512]{1,0:T(8,128)(2,1)S(1)} %slice.41), channel_id=1, source_target_pairs={{0,24},{8,16},{16,8},{24,0},{1,25},{9,17},{17,9},{25,1},{2,26},{10... | collective-permute-start | bytes 49160 | tf_op jit(solution)/shard_map/ppermute | solution.py:145
  114.3 39.9 %copy-start = (bf16[512,512]{1,0:T(8,128)(2,1)S(1)}, bf16[512,512]{1,0:T(8,128)(2,1)}, u32[]{:S(2)}) copy-start(bf16[512,512]{1,0:T(8,128)(2,1)} %weight_ref.1) | copy-start | bytes 1572868
  114.3 39.9 %all-to-all-start.4 = ((bf16[4,128,512]{2,1,0:T(8,128)(2,1)}), bf16[4,128,512]{2,1,0:T(8,128)(2,1)S(1)}, u32[]{:S(2)}, u32[]{:S(2)}) async-start(bf16[4,128,512]{2,1,0:T(8,128)(2,1)} %bitcast.7), calls=%async_computation.4 | async-start | bytes 1048576 | tf_op jit(solution)/shard_map/all_to_all | solution.py:141
  125.5 7.7 %collective-permute-start.9 = (bf16[64,512]{1,0:T(8,128)(2,1)S(1)}, bf16[64,512]{1,0:T(8,128)(2,1)S(1)}, u32[]{:S(2)}, u32[]{:S(2)}) collective-permute-start(bf16[64,512]{1,0:T(8,128)(2,1)S(1)} %pad_maximum_fusion.3.refs_0_), channel_id=1, source_target_pairs={{0,64},{32,96},{64,0},{96,32},{1,65},{33,97},{65,1},{97,33},{2,66}... | collective-permute-start | bytes 196616 | tf_op jit(solution)/shard_map/ppermute | solution.py:145
  133.2 6.9 %collective-permute-start.10 = (bf16[128,512]{1,0:T(8,128)(2,1)S(1)}, bf16[128,512]{1,0:T(8,128)(2,1)S(1)}, u32[]{:S(2)}, u32[]{:S(2)}) collective-permute-start(bf16[128,512]{1,0:T(8,128)(2,1)S(1)} %pad_maximum_fusion.2), channel_id=1, source_target_pairs={{0,32},{32,0},{64,96},{96,64},{1,33},{33,1},{65,97},{97,65},{2,34}... | collective-permute-start | bytes 393224 | tf_op jit(solution)/shard_map/ppermute | solution.py:145
  140.1 3.4 %collective-permute-start.11 = (bf16[256,512]{1,0:T(8,128)(2,1)S(1)}, bf16[256,512]{1,0:T(8,128)(2,1)S(1)}, u32[]{:S(2)}, u32[]{:S(2)}) collective-permute-start(bf16[256,512]{1,0:T(8,128)(2,1)S(1)} %pad_maximum_fusion.1), channel_id=1, source_target_pairs={{0,1},{1,0},{2,3},{3,2},{4,5},{5,4},{6,7},{7,6},{8,9},{9,8},{10,11... | collective-permute-start | bytes 786440 | tf_op jit(solution)/shard_map/ppermute | solution.py:145

commit v11 on v10

--- a/solution.py
+++ b/solution.py
@@ -171,10 +171,9 @@
     for bit, n in ((2, 2 * n_slice), (1, n_slice)):
         kept, away, bias = terms[:n], terms[n : 2 * n], terms[2 * n :]
         terms = jnp.concatenate([kept, bias], axis=0) + trade(jnp.concatenate([away, bias], axis=0), "y", bit)
-    terms = terms + trade(terms, "zh", 1)
     own, terms = lax.optimization_barrier((own, terms))
     other = lax.ppermute(own, "core", [(0, 1), (1, 0)])
-    terms = swap(jnp.broadcast_to(terms, (n_x,) + terms.shape), "x")
+    terms = swap(jnp.broadcast_to(terms, (n_zh,) + terms.shape), "zh")
     slots = adj_blocks.shape[2]
     group = max(d for d in range(1, 9) if slots % d == 0)
     sent, mark = call(
@@ -203,12 +202,15 @@
     )(block_pos.reshape(-1), block_live.reshape(-1), core, adj_blocks[0, 0], own, other)
     terms, sent = lax.optimization_barrier((terms, sent))
     terms = terms.sum(axis=0)
-    terms = terms + trade(terms, "zh", 2)
+    for bit in (1, 2):
+        terms = terms + trade(terms, "x", bit)
     factor = 1.0 / math.sqrt(blk * n_zh * n_y * n_zl * n_x * n_core)
     terms = terms * factor
     slices = terms[:n_slice].astype(BF16)
-    slices = jnp.concatenate([slices] + [trade(slices, "zl", k) for k in range(1, n_zl)], axis=0)
-    offsets = [k * n_y * n_core for k in range(n_zl)]
+    offsets = [0]
+    for bit in (1, 2):
+        slices = jnp.concatenate([slices, trade(slices, "zl", bit)], axis=0)
+        offsets += [o ^ (bit * n_y * n_core) for o in offsets]
     got = swap(sent, "y")
     sent, mark = call(fold_kernel, jax.ShapeDtypeStruct((n_zh * blk, n_feat), BF16), marked=True)(got)
     slices, sent = lax.optimization_barrier((slices, sent))

time: 156 us -> 156 us (level)
  the two profiles are of different devices: /device:TPU:6 before, /device:TPU:24 now
where the time goes in v11:
time: 156 us
  starting transfers between devices  57.5 us (37%)
  waiting for transfers between devices  53.9 us (35%)
  blocking collectives  23 us (15%)
  Pallas kernels  14.2 us (9%)
  local copies, waits for them, and re-layouts  3.99 us (3%)
  between operations  1.56 us (1%)
    ppermute x10, waiting for transfers between devices, trade(): lax.ppermute(value, axis, [(i, i ^ bit) for i in range(lax.axis_size(axis...  31.7 us
    ppermute x10, starting transfers between devices, trade(): lax.ppermute(value, axis, [(i, i ^ bit) for i in range(lax.axis_size(axis...  29.5 us
    all_to_all x4, starting transfers between devices, swap(): return lax.all_to_all(value, axis, split_axis=0, concat_axis=0, tiled=True)  26.2 us
    all_to_all x1, blocking collectives, swap(): return lax.all_to_all(value, axis, split_axis=0, concat_axis=0, tiled=True)  23 us
    all_to_all x4, waiting for transfers between devices, swap(): return lax.all_to_all(value, axis, split_axis=0, concat_axis=0, tiled=True)  22.2 us
    pallas_call x1, Pallas kernels, body(): call(functools.partial(tile_kernel, group=group, n_x=n_x), jax.ShapeDtype...  9.48 us
  transfers between devices with their start and end apart: 15, of which 13 were waited for; matrix products, arithmetic and copies ran while one was open for 1% of the time, Pallas kernels for 8%

profile of v11, /device:TPU:24, one launch (start us, length us, event | category | flops | bytes accessed | tf_op | source)
XLA Modules:
  0.0 155.6 jit_solution(10777990301502514717)
XLA Ops:
  2.9 23.0 %all_to_all.25.got_ref = bf16[4,160,512]{2,1,0:T(8,128)(2,1)S(1)} all-to-all(bf16[4,160,512]{2,1,0:T(8,128)(2,1)S(1)} %pad_maximum_fusion), channel_id=1, replica_groups=mesh['zh'=4,'y'=4,'zl'=4,'x'=4,'core'=2] {'zl'}, dimensions={0} | all-to-all | bytes 1310720 | tf_op jit(solution)/shard_map/all_to_all | solution.py:141
  27.4 4.3 %all-to-all-start.1 = ((bf16[4,512,512]{2,1,0:T(8,128)(2,1)}), bf16[4,512,512]{2,1,0:T(8,128)(2,1)S(1)}, u32[]{:S(2)}, u32[]{:S(2)}) async-start(bf16[4,512,512]{2,1,0:T(8,128)(2,1)} %broadcast_in_dim.13), calls=%async_computation.1 | async-start | bytes 4194304 | tf_op jit(solution)/shard_map/all_to_all | solution.py:141
  36.1 3.1 %collective-permute-start.1 = (f32[40,512]{1,0:T(8,128)S(1)}, f32[40,512]{1,0:T(8,128)S(1)}, u32[]{:S(2)}, u32[]{:S(2)}) collective-permute-start(f32[40,512]{1,0:T(8,128)S(1)} %concatenate.45), channel_id=1, source_target_pairs={{0,64},{32,96},{64,0},{96,32},{1,65},{33,97},{65,1},{97,33},{2,66}... | collective-permute-start | bytes 245768 | tf_op jit(solution)/shard_map/ppermute | solution.py:145
  39.2 4.7 %collective-permute-done.1 = f32[40,512]{1,0:T(8,128)S(1)} collective-permute-done((f32[40,512]{1,0:T(8,128)S(1)}, f32[40,512]{1,0:T(8,128)S(1)}, u32[]{:S(2)}, u32[]{:S(2)}) %collective-permute-start.1) | collective-permute-done | bytes 81952 | tf_op jit(solution)/shard_map/ppermute | solution.py:145
  44.0 2.7 %collective-permute-start.2 = (f32[24,512]{1,0:T(8,128)S(1)}, f32[24,512]{1,0:T(8,128)S(1)}, u32[]{:S(2)}, u32[]{:S(2)}) collective-permute-start(f32[24,512]{1,0:T(8,128)S(1)} %concatenate.46), channel_id=1, source_target_pairs={{0,32},{32,0},{64,96},{96,64},{1,33},{33,1},{65,97},{97,65},{2,34}... | collective-permute-start | bytes 147464 | tf_op jit(solution)/shard_map/ppermute | solution.py:145
  46.7 3.3 %collective-permute-done.2 = f32[24,512]{1,0:T(8,128)S(1)} collective-permute-done((f32[24,512]{1,0:T(8,128)S(1)}, f32[24,512]{1,0:T(8,128)S(1)}, u32[]{:S(2)}, u32[]{:S(2)}) %collective-permute-start.2) | collective-permute-done | bytes 49184 | tf_op jit(solution)/shard_map/ppermute | solution.py:145
  50.0 6.9 %all-to-all-done.1.own_ref = bf16[4,512,512]{2,1,0:T(8,128)(2,1)S(1)} async-done(((bf16[4,512,512]{2,1,0:T(8,128)(2,1)}), bf16[4,512,512]{2,1,0:T(8,128)(2,1)S(1)}, u32[]{:S(2)}, u32[]{:S(2)}) %all-to-all-start.1) | async-done | bytes 2097184 | tf_op jit(solution)/shard_map/all_to_all | solution.py:141
  59.5 12.4 %all-to-all-start.2 = ((f32[4,24,512]{2,1,0:T(8,128)}), f32[4,24,512]{2,1,0:T(8,128)S(1)}, u32[]{:S(2)}, u32[]{:S(2)}) async-start(f32[4,24,512]{2,1,0:T(8,128)} %broadcast_in_dim.14), calls=%async_computation.2 | async-start | bytes 393216 | tf_op jit(solution)/shard_map/all_to_all | solution.py:141
  72.6 9.5 %shard_map.104 = (bf16[4,512,512]{2,1,0:T(8,128)(2,1)}, f32[8,128]{1,0:T(8,128)}) custom-call(s32[85]{0:T(128)} %bitcast.19, s32[1]{0:T(128)} %bitcast.13.live_ref, s32[1]{0:T(128)} %bitcast.2.core_ref, bf16[85,128,128]{2,1,0:T(8,128)(2,1)} %bitcast.14, bf16[4,512,512]{2,1,0:T(8,128)(2,1)} %copy-done.1, bf16[4,512,512]{2,1,0:T(8,128)(2,1)} %collective-permute-done.3.other_ref), custom_call_target="tpu_custom_call" | custom-call | flops 1426063360 | bytes 44564480 | tf_op jit(solution)/shard_map/pallas_call | solution.py:179
  82.1 6.6 %all-to-all-done.2 = f32[4,24,512]{2,1,0:T(8,128)S(1)} async-done(((f32[4,24,512]{2,1,0:T(8,128)}), f32[4,24,512]{2,1,0:T(8,128)S(1)}, u32[]{:S(2)}, u32[]{:S(2)}) %all-to-all-start.2) | async-done | bytes 196640 | tf_op jit(solution)/shard_map/all_to_all | solution.py:141
  88.6 4.7 %all-to-all-start.3 = ((bf16[4,512,512]{2,1,0:T(8,128)(2,1)}), bf16[4,512,512]{2,1,0:T(8,128)(2,1)S(1)}, u32[]{:S(2)}, u32[]{:S(2)}) async-start(bf16[4,512,512]{2,1,0:T(8,128)(2,1)} %get-tuple-element.19), calls=%async_computation.3 | async-start | bytes 4194304 | tf_op jit(solution)/shard_map/all_to_all | solution.py:141
  93.3 2.5 %collective-permute-start.4 = (f32[24,512]{1,0:T(8,128)S(1)}, f32[24,512]{1,0:T(8,128)S(1)}, u32[]{:S(2)}, u32[]{:S(2)}) collective-permute-start(f32[24,512]{1,0:T(8,128)S(1)} %reduce_sum.9), channel_id=1, source_target_pairs={{0,2},{2,0},{4,6},{6,4},{1,3},{3,1},{5,7},{7,5},{8,10},{10,8},{12,... | collective-permute-start | bytes 147464 | tf_op jit(solution)/shard_map/ppermute | solution.py:145
  95.8 4.0 %collective-permute-done.4 = f32[24,512]{1,0:T(8,128)S(1)} collective-permute-done((f32[24,512]{1,0:T(8,128)S(1)}, f32[24,512]{1,0:T(8,128)S(1)}, u32[]{:S(2)}, u32[]{:S(2)}) %collective-permute-start.4) | collective-permute-done | bytes 49184 | tf_op jit(solution)/shard_map/ppermute | solution.py:145
  99.8 2.0 %collective-permute-start.5 = (f32[24,512]{1,0:T(8,128)S(1)}, f32[24,512]{1,0:T(8,128)S(1)}, u32[]{:S(2)}, u32[]{:S(2)}) collective-permute-start(f32[24,512]{1,0:T(8,128)S(1)} %add.24), channel_id=1, source_target_pairs={{0,4},{2,6},{4,0},{6,2},{1,5},{3,7},{5,1},{7,3},{8,12},{10,14},{12... | collective-permute-start | bytes 147464 | tf_op jit(solution)/shard_map/ppermute | solution.py:145
  101.9 5.4 %collective-permute-done.5 = f32[24,512]{1,0:T(8,128)S(1)} collective-permute-done((f32[24,512]{1,0:T(8,128)S(1)}, f32[24,512]{1,0:T(8,128)S(1)}, u32[]{:S(2)}, u32[]{:S(2)}) %collective-permute-start.5) | collective-permute-done | bytes 49184 | tf_op jit(solution)/shard_map/ppermute | solution.py:145
  107.4 4.5 %collective-permute-start.6 = (bf16[16,512]{1,0:T(8,128)(2,1)S(1)}, bf16[16,512]{1,0:T(8,128)(2,1)S(1)}, u32[]{:S(2)}, u32[]{:S(2)}) collective-permute-start(bf16[16,512]{1,0:T(8,128)(2,1)S(1)} %slice.41), channel_id=1, source_target_pairs={{0,8},{8,0},{16,24},{24,16},{1,9},{9,1},{17,25},{25,17},{2,10},{10... | collective-permute-start | bytes 49160 | tf_op jit(solution)/shard_map/ppermute | solution.py:145
  113.6 4.0 %collective-permute-start.7 = (bf16[32,512]{1,0:T(8,128)(2,1)S(1)}, bf16[32,512]{1,0:T(8,128)(2,1)S(1)}, u32[]{:S(2)}, u32[]{:S(2)}) collective-permute-start(bf16[32,512]{1,0:T(8,128)(2,1)S(1)} %pad_maximum_fusion.4), channel_id=1, source_target_pairs={{0,16},{8,24},{16,0},{24,8},{1,17},{9,25},{17,1},{25,9},{2,18},{10... | collective-permute-start | bytes 98312 | tf_op jit(solution)/shard_map/ppermute | solution.py:145
  117.6 2.7 %collective-permute-done.7 = bf16[32,512]{1,0:T(8,128)(2,1)S(1)} collective-permute-done((bf16[32,512]{1,0:T(8,128)(2,1)S(1)}, bf16[32,512]{1,0:T(8,128)(2,1)S(1)}, u32[]{:S(2)}, u32[]{:S(2)}) %collective-permute-start.7) | collective-permute-done | bytes 32800 | tf_op jit(solution)/shard_map/ppermute | solution.py:145
  121.4 4.8 %all-to-all-start.4 = ((bf16[4,128,512]{2,1,0:T(8,128)(2,1)}), bf16[4,128,512]{2,1,0:T(8,128)(2,1)S(1)}, u32[]{:S(2)}, u32[]{:S(2)}) async-start(bf16[4,128,512]{2,1,0:T(8,128)(2,1)} %bitcast.7), calls=%async_computation.4 | async-start | bytes 1048576 | tf_op jit(solution)/shard_map/all_to_all | solution.py:141
  126.2 3.4 %collective-permute-start.8 = (bf16[64,512]{1,0:T(8,128)(2,1)S(1)}, bf16[64,512]{1,0:T(8,128)(2,1)S(1)}, u32[]{:S(2)}, u32[]{:S(2)}) collective-permute-start(bf16[64,512]{1,0:T(8,128)(2,1)S(1)} %pad_maximum_fusion.3.refs_0_), channel_id=1, source_target_pairs={{0,64},{32,96},{64,0},{96,32},{1,65},{33,97},{65,1},{97,33},{2,66}... | collective-permute-start | bytes 196616 | tf_op jit(solution)/shard_map/ppermute | solution.py:145
  129.5 4.3 %collective-permute-done.8.refs_1_ = bf16[64,512]{1,0:T(8,128)(2,1)S(1)} collective-permute-done((bf16[64,512]{1,0:T(8,128)(2,1)S(1)}, bf16[64,512]{1,0:T(8,128)(2,1)S(1)}, u32[]{:S(2)}, u32[]{:S(2)}) %collective-permute-start.8) | collective-permute-done | bytes 65568 | tf_op jit(solution)/shard_map/ppermute | solution.py:145
  133.8 3.4 %collective-permute-start.9 = (bf16[128,512]{1,0:T(8,128)(2,1)S(1)}, bf16[128,512]{1,0:T(8,128)(2,1)S(1)}, u32[]{:S(2)}, u32[]{:S(2)}) collective-permute-start(bf16[128,512]{1,0:T(8,128)(2,1)S(1)} %pad_maximum_fusion.2), channel_id=1, source_target_pairs={{0,32},{32,0},{64,96},{96,64},{1,33},{33,1},{65,97},{97,65},{2,34}... | collective-permute-start | bytes 393224 | tf_op jit(solution)/shard_map/ppermute | solution.py:145
  137.3 3.4 %collective-permute-done.9.refs_2_ = bf16[128,512]{1,0:T(8,128)(2,1)S(1)} collective-permute-done((bf16[128,512]{1,0:T(8,128)(2,1)S(1)}, bf16[128,512]{1,0:T(8,128)(2,1)S(1)}, u32[]{:S(2)}, u32[]{:S(2)}) %collective-permute-start.9) | collective-permute-done | bytes 131104 | tf_op jit(solution)/shard_map/ppermute | solution.py:145
  145.7 8.7 %all-to-all-done.4.in_ref = bf16[4,128,512]{2,1,0:T(8,128)(2,1)S(1)} async-done(((bf16[4,128,512]{2,1,0:T(8,128)(2,1)}), bf16[4,128,512]{2,1,0:T(8,128)(2,1)S(1)}, u32[]{:S(2)}, u32[]{:S(2)}) %all-to-all-start.4) | async-done | bytes 524320 | tf_op jit(solution)/shard_map/all_to_all | solution.py:141
  (47 shorter events, 19.7 us)
Async XLA Ops:
  27.4 29.5 %all-to-all-start.1 = ((bf16[4,512,512]{2,1,0:T(8,128)(2,1)}), bf16[4,512,512]{2,1,0:T(8,128)(2,1)S(1)}, u32[]{:S(2)}, u32[]{:S(2)}) async-start(bf16[4,512,512]{2,1,0:T(8,128)(2,1)} %broadcast_in_dim.13), calls=%async_computation.1 | async-start | bytes 4194304 | tf_op jit(solution)/shard_map/all_to_all | solution.py:141
  32.7 3.3 %collective-permute-start = (f32[72,512]{1,0:T(8,128)S(1)}, f32[72,512]{1,0:T(8,128)S(1)}, u32[]{:S(2)}, u32[]{:S(2)}) collective-permute-start(f32[72,512]{1,0:T(8,128)S(1)} %get-tuple-element.14), channel_id=1, source_target_pairs={{0,1},{1,0},{2,3},{3,2},{4,5},{5,4},{6,7},{7,6},{8,9},{9,8},{10,11... | collective-permute-start | bytes 442376 | tf_op jit(solution)/shard_map/ppermute | solution.py:145
  36.1 7.9 %collective-permute-start.1 = (f32[40,512]{1,0:T(8,128)S(1)}, f32[40,512]{1,0:T(8,128)S(1)}, u32[]{:S(2)}, u32[]{:S(2)}) collective-permute-start(f32[40,512]{1,0:T(8,128)S(1)} %concatenate.45), channel_id=1, source_target_pairs={{0,64},{32,96},{64,0},{96,32},{1,65},{33,97},{65,1},{97,33},{2,66}... | collective-permute-start | bytes 245768 | tf_op jit(solution)/shard_map/ppermute | solution.py:145
  44.0 6.0 %collective-permute-start.2 = (f32[24,512]{1,0:T(8,128)S(1)}, f32[24,512]{1,0:T(8,128)S(1)}, u32[]{:S(2)}, u32[]{:S(2)}) collective-permute-start(f32[24,512]{1,0:T(8,128)S(1)} %concatenate.46), channel_id=1, source_target_pairs={{0,32},{32,0},{64,96},{96,64},{1,33},{33,1},{65,97},{97,65},{2,34}... | collective-permute-start | bytes 147464 | tf_op jit(solution)/shard_map/ppermute | solution.py:145
  56.9 15.7 %copy-start.1 = (bf16[4,512,512]{2,1,0:T(8,128)(2,1)}, bf16[4,512,512]{2,1,0:T(8,128)(2,1)S(1)}, u32[]{:S(2)}) copy-start(bf16[4,512,512]{2,1,0:T(8,128)(2,1)S(1)} %all-to-all-done.1.own_ref) | copy-start | bytes 6291460
  56.9 15.7 %collective-permute-start.3 = (bf16[4,512,512]{2,1,0:T(8,128)(2,1)S(1)}, bf16[4,512,512]{2,1,0:T(8,128)(2,1)}, u32[]{:S(2)}, u32[]{:S(2)}) collective-permute-start(bf16[4,512,512]{2,1,0:T(8,128)(2,1)S(1)} %all-to-all-done.1.own_ref), channel_id=1, source_target_pairs={{0,1},{1,0},{2,3},{3,2},{4,5},{5,4},{6,7},{7,6},{8,9},{9,8},{10,11... | collective-permute-start | bytes 6291464 | tf_op jit(solution)/shard_map/ppermute | solution.py:175
  59.5 29.1 %all-to-all-start.2 = ((f32[4,24,512]{2,1,0:T(8,128)}), f32[4,24,512]{2,1,0:T(8,128)S(1)}, u32[]{:S(2)}, u32[]{:S(2)}) async-start(f32[4,24,512]{2,1,0:T(8,128)} %broadcast_in_dim.14), calls=%async_computation.2 | async-start | bytes 393216 | tf_op jit(solution)/shard_map/all_to_all | solution.py:141
  88.6 31.7 %all-to-all-start.3 = ((bf16[4,512,512]{2,1,0:T(8,128)(2,1)}), bf16[4,512,512]{2,1,0:T(8,128)(2,1)S(1)}, u32[]{:S(2)}, u32[]{:S(2)}) async-start(bf16[4,512,512]{2,1,0:T(8,128)(2,1)} %get-tuple-element.19), calls=%async_computation.3 | async-start | bytes 4194304 | tf_op jit(solution)/shard_map/all_to_all | solution.py:141
  93.3 6.5 %collective-permute-start.4 = (f32[24,512]{1,0:T(8,128)S(1)}, f32[24,512]{1,0:T(8,128)S(1)}, u32[]{:S(2)}, u32[]{:S(2)}) collective-permute-start(f32[24,512]{1,0:T(8,128)S(1)} %reduce_sum.9), channel_id=1, source_target_pairs={{0,2},{2,0},{4,6},{6,4},{1,3},{3,1},{5,7},{7,5},{8,10},{10,8},{12,... | collective-permute-start | bytes 147464 | tf_op jit(solution)/shard_map/ppermute | solution.py:145
  99.8 7.5 %collective-permute-start.5 = (f32[24,512]{1,0:T(8,128)S(1)}, f32[24,512]{1,0:T(8,128)S(1)}, u32[]{:S(2)}, u32[]{:S(2)}) collective-permute-start(f32[24,512]{1,0:T(8,128)S(1)} %add.24), channel_id=1, source_target_pairs={{0,4},{2,6},{4,0},{6,2},{1,5},{3,7},{5,1},{7,3},{8,12},{10,14},{12... | collective-permute-start | bytes 147464 | tf_op jit(solution)/shard_map/ppermute | solution.py:145
  107.3 35.3 %copy-start.2 = (s32[32]{0:T(128)S(1)}, s32[32]{0:T(128)}, u32[]{:S(2)}) copy-start(s32[32]{0:T(128)} %constant.23.clone) | copy-start | bytes 388
  107.4 6.2 %collective-permute-start.6 = (bf16[16,512]{1,0:T(8,128)(2,1)S(1)}, bf16[16,512]{1,0:T(8,128)(2,1)S(1)}, u32[]{:S(2)}, u32[]{:S(2)}) collective-permute-start(bf16[16,512]{1,0:T(8,128)(2,1)S(1)} %slice.41), channel_id=1, source_target_pairs={{0,8},{8,0},{16,24},{24,16},{1,9},{9,1},{17,25},{25,17},{2,10},{10... | collective-permute-start | bytes 49160 | tf_op jit(solution)/shard_map/ppermute | solution.py:145
  113.6 6.7 %collective-permute-start.7 = (bf16[32,512]{1,0:T(8,128)(2,1)S(1)}, bf16[32,512]{1,0:T(8,128)(2,1)S(1)}, u32[]{:S(2)}, u32[]{:S(2)}) collective-permute-start(bf16[32,512]{1,0:T(8,128)(2,1)S(1)} %pad_maximum_fusion.4), channel_id=1, source_target_pairs={{0,16},{8,24},{16,0},{24,8},{1,17},{9,25},{17,1},{25,9},{2,18},{10... | collective-permute-start | bytes 98312 | tf_op jit(solution)/shard_map/ppermute | solution.py:145
  121.4 33.1 %copy-start = (bf16[512,512]{1,0:T(8,128)(2,1)S(1)}, bf16[512,512]{1,0:T(8,128)(2,1)}, u32[]{:S(2)}) copy-start(bf16[512,512]{1,0:T(8,128)(2,1)} %weight_ref.1) | copy-start | bytes 1572868
  121.4 33.1 %all-to-all-start.4 = ((bf16[4,128,512]{2,1,0:T(8,128)(2,1)}), bf16[4,128,512]{2,1,0:T(8,128)(2,1)S(1)}, u32[]{:S(2)}, u32[]{:S(2)}) async-start(bf16[4,128,512]{2,1,0:T(8,128)(2,1)} %bitcast.7), calls=%async_computation.4 | async-start | bytes 1048576 | tf_op jit(solution)/shard_map/all_to_all | solution.py:141
  126.2 7.7 %collective-permute-start.8 = (bf16[64,512]{1,0:T(8,128)(2,1)S(1)}, bf16[64,512]{1,0:T(8,128)(2,1)S(1)}, u32[]{:S(2)}, u32[]{:S(2)}) collective-permute-start(bf16[64,512]{1,0:T(8,128)(2,1)S(1)} %pad_maximum_fusion.3.refs_0_), channel_id=1, source_target_pairs={{0,64},{32,96},{64,0},{96,32},{1,65},{33,97},{65,1},{97,33},{2,66}... | collective-permute-start | bytes 196616 | tf_op jit(solution)/shard_map/ppermute | solution.py:145
  133.8 6.9 %collective-permute-start.9 = (bf16[128,512]{1,0:T(8,128)(2,1)S(1)}, bf16[128,512]{1,0:T(8,128)(2,1)S(1)}, u32[]{:S(2)}, u32[]{:S(2)}) collective-permute-start(bf16[128,512]{1,0:T(8,128)(2,1)S(1)} %pad_maximum_fusion.2), channel_id=1, source_target_pairs={{0,32},{32,0},{64,96},{96,64},{1,33},{33,1},{65,97},{97,65},{2,34}... | collective-permute-start | bytes 393224 | tf_op jit(solution)/shard_map/ppermute | solution.py:145
  140.7 3.4 %collective-permute-start.10 = (bf16[256,512]{1,0:T(8,128)(2,1)S(1)}, bf16[256,512]{1,0:T(8,128)(2,1)S(1)}, u32[]{:S(2)}, u32[]{:S(2)}) collective-permute-start(bf16[256,512]{1,0:T(8,128)(2,1)S(1)} %pad_maximum_fusion.1), channel_id=1, source_target_pairs={{0,1},{1,0},{2,3},{3,2},{4,5},{5,4},{6,7},{7,6},{8,9},{9,8},{10,11... | collective-permute-start | bytes 786440 | tf_op jit(solution)/shard_map/ppermute | solution.py:145

commit v12 on v11

--- a/solution.py
+++ b/solution.py
@@ -175,7 +175,7 @@
     other = lax.ppermute(own, "core", [(0, 1), (1, 0)])
     terms = swap(jnp.broadcast_to(terms, (n_zh,) + terms.shape), "zh")
     slots = adj_blocks.shape[2]
-    group = max(d for d in range(1, 9) if slots % d == 0)
+    group = max(d for d in range(1, 18) if slots % d == 0)
     sent, mark = call(
         functools.partial(tile_kernel, group=group, n_x=n_x),
         jax.ShapeDtypeStruct((n_y, n_zh * blk, n_feat), BF16),

time: 156 us -> 155 us (level)
  the two profiles are of different devices: /device:TPU:24 before, /device:TPU:1 now
where the time goes in v12:
time: 155 us; the launch traced here: 154 us
  starting transfers between devices  71.8 us (46%)
  waiting for transfers between devices  40.8 us (26%)
  blocking collectives  22 us (14%)
  Pallas kernels  12.2 us (8%)
  local copies, waits for them, and re-layouts  3.99 us (3%)
  between operations  1.56 us (1%)
    ppermute x10, starting transfers between devices, trade(): lax.ppermute(value, axis, [(i, i ^ bit) for i in range(lax.axis_size(axis...  36.4 us
    all_to_all x4, starting transfers between devices, swap(): return lax.all_to_all(value, axis, split_axis=0, concat_axis=0, tiled=True)  30.5 us
    ppermute x10, waiting for transfers between devices, trade(): lax.ppermute(value, axis, [(i, i ^ bit) for i in range(lax.axis_size(axis...  23 us
    all_to_all x1, blocking collectives, swap(): return lax.all_to_all(value, axis, split_axis=0, concat_axis=0, tiled=True)  22 us
    all_to_all x4, waiting for transfers between devices, swap(): return lax.all_to_all(value, axis, split_axis=0, concat_axis=0, tiled=True)  17.8 us
    pallas_call x1, Pallas kernels, body(): call(functools.partial(tile_kernel, group=group, n_x=n_x), jax.ShapeDtype...  7.47 us
    ppermute x1, starting transfers between devices, body(): other = lax.ppermute(own, 'core', [(0, 1), (1, 0)])  4.91 us
  transfers between devices with their start and end apart: 15, of which 13 were waited for; matrix products, arithmetic and copies ran while one was open for 1% of the time, Pallas kernels for 7%

profile of v12, /device:TPU:1, one launch (start us, length us, event | category | flops | bytes accessed | tf_op | source)
XLA Modules:
  0.0 153.7 jit_solution(4210732986917741619)
XLA Ops:
  2.9 22.0 %all_to_all.25.got_ref = bf16[4,160,512]{2,1,0:T(8,128)(2,1)S(1)} all-to-all(bf16[4,160,512]{2,1,0:T(8,128)(2,1)S(1)} %pad_maximum_fusion), channel_id=1, replica_groups=mesh['zh'=4,'y'=4,'zl'=4,'x'=4,'core'=2] {'zl'}, dimensions={0} | all-to-all | bytes 1310720 | tf_op jit(solution)/shard_map/all_to_all | solution.py:141
  26.4 4.7 %all-to-all-start.1 = ((bf16[4,512,512]{2,1,0:T(8,128)(2,1)}), bf16[4,512,512]{2,1,0:T(8,128)(2,1)S(1)}, u32[]{:S(2)}, u32[]{:S(2)}) async-start(bf16[4,512,512]{2,1,0:T(8,128)(2,1)} %broadcast_in_dim.13), calls=%async_computation.1 | async-start | bytes 4194304 | tf_op jit(solution)/shard_map/all_to_all | solution.py:141
  32.2 4.0 %collective-permute-start = (f32[72,512]{1,0:T(8,128)S(1)}, f32[72,512]{1,0:T(8,128)S(1)}, u32[]{:S(2)}, u32[]{:S(2)}) collective-permute-start(f32[72,512]{1,0:T(8,128)S(1)} %get-tuple-element.14), channel_id=1, source_target_pairs={{0,1},{1,0},{2,3},{3,2},{4,5},{5,4},{6,7},{7,6},{8,9},{9,8},{10,11... | collective-permute-start | bytes 442376 | tf_op jit(solution)/shard_map/ppermute | solution.py:145
  37.2 4.8 %collective-permute-start.1 = (f32[40,512]{1,0:T(8,128)S(1)}, f32[40,512]{1,0:T(8,128)S(1)}, u32[]{:S(2)}, u32[]{:S(2)}) collective-permute-start(f32[40,512]{1,0:T(8,128)S(1)} %concatenate.45), channel_id=1, source_target_pairs={{0,64},{32,96},{64,0},{96,32},{1,65},{33,97},{65,1},{97,33},{2,66}... | collective-permute-start | bytes 245768 | tf_op jit(solution)/shard_map/ppermute | solution.py:145
  42.1 2.2 %collective-permute-done.1 = f32[40,512]{1,0:T(8,128)S(1)} collective-permute-done((f32[40,512]{1,0:T(8,128)S(1)}, f32[40,512]{1,0:T(8,128)S(1)}, u32[]{:S(2)}, u32[]{:S(2)}) %collective-permute-start.1) | collective-permute-done | bytes 81952 | tf_op jit(solution)/shard_map/ppermute | solution.py:145
  44.3 3.2 %collective-permute-start.2 = (f32[24,512]{1,0:T(8,128)S(1)}, f32[24,512]{1,0:T(8,128)S(1)}, u32[]{:S(2)}, u32[]{:S(2)}) collective-permute-start(f32[24,512]{1,0:T(8,128)S(1)} %concatenate.46), channel_id=1, source_target_pairs={{0,32},{32,0},{64,96},{96,64},{1,33},{33,1},{65,97},{97,65},{2,34}... | collective-permute-start | bytes 147464 | tf_op jit(solution)/shard_map/ppermute | solution.py:145
  49.4 6.0 %all-to-all-done.1.own_ref = bf16[4,512,512]{2,1,0:T(8,128)(2,1)S(1)} async-done(((bf16[4,512,512]{2,1,0:T(8,128)(2,1)}), bf16[4,512,512]{2,1,0:T(8,128)(2,1)S(1)}, u32[]{:S(2)}, u32[]{:S(2)}) %all-to-all-start.1) | async-done | bytes 2097184 | tf_op jit(solution)/shard_map/all_to_all | solution.py:141
  55.4 4.9 %collective-permute-start.3 = (bf16[4,512,512]{2,1,0:T(8,128)(2,1)S(1)}, bf16[4,512,512]{2,1,0:T(8,128)(2,1)}, u32[]{:S(2)}, u32[]{:S(2)}) collective-permute-start(bf16[4,512,512]{2,1,0:T(8,128)(2,1)S(1)} %all-to-all-done.1.own_ref), channel_id=1, source_target_pairs={{0,1},{1,0},{2,3},{3,2},{4,5},{5,4},{6,7},{7,6},{8,9},{9,8},{10,11... | collective-permute-start | bytes 6291464 | tf_op jit(solution)/shard_map/ppermute | solution.py:175
  61.0 12.1 %all-to-all-start.2 = ((f32[4,24,512]{2,1,0:T(8,128)}), f32[4,24,512]{2,1,0:T(8,128)S(1)}, u32[]{:S(2)}, u32[]{:S(2)}) async-start(f32[4,24,512]{2,1,0:T(8,128)} %broadcast_in_dim.14), calls=%async_computation.2 | async-start | bytes 393216 | tf_op jit(solution)/shard_map/all_to_all | solution.py:141
  73.8 7.5 %shard_map.104 = (bf16[4,512,512]{2,1,0:T(8,128)(2,1)}, f32[8,128]{1,0:T(8,128)}) custom-call(s32[85]{0:T(128)} %bitcast.19, s32[1]{0:T(128)} %bitcast.13.live_ref, s32[1]{0:T(128)} %bitcast.2.core_ref, bf16[85,128,128]{2,1,0:T(8,128)(2,1)} %bitcast.14, bf16[4,512,512]{2,1,0:T(8,128)(2,1)} %copy-done.1, bf16[4,512,512]{2,1,0:T(8,128)(2,1)} %collective-permute-done.3.other_ref), custom_call_target="tpu_custom_call" | custom-call | flops 1426063360 | bytes 44564480 | tf_op jit(solution)/shard_map/pallas_call | solution.py:179
  81.3 5.1 %all-to-all-done.2 = f32[4,24,512]{2,1,0:T(8,128)S(1)} async-done(((f32[4,24,512]{2,1,0:T(8,128)}), f32[4,24,512]{2,1,0:T(8,128)S(1)}, u32[]{:S(2)}, u32[]{:S(2)}) %all-to-all-start.2) | async-done | bytes 196640 | tf_op jit(solution)/shard_map/all_to_all | solution.py:141
  86.3 4.2 %all-to-all-start.3 = ((bf16[4,512,512]{2,1,0:T(8,128)(2,1)}), bf16[4,512,512]{2,1,0:T(8,128)(2,1)S(1)}, u32[]{:S(2)}, u32[]{:S(2)}) async-start(bf16[4,512,512]{2,1,0:T(8,128)(2,1)} %get-tuple-element.19), calls=%async_computation.3 | async-start | bytes 4194304 | tf_op jit(solution)/shard_map/all_to_all | solution.py:141
  92.7 2.6 %collective-permute-done.4 = f32[24,512]{1,0:T(8,128)S(1)} collective-permute-done((f32[24,512]{1,0:T(8,128)S(1)}, f32[24,512]{1,0:T(8,128)S(1)}, u32[]{:S(2)}, u32[]{:S(2)}) %collective-permute-start.4) | collective-permute-done | bytes 49184 | tf_op jit(solution)/shard_map/ppermute | solution.py:145
  95.4 2.5 %collective-permute-start.5 = (f32[24,512]{1,0:T(8,128)S(1)}, f32[24,512]{1,0:T(8,128)S(1)}, u32[]{:S(2)}, u32[]{:S(2)}) collective-permute-start(f32[24,512]{1,0:T(8,128)S(1)} %add.24), channel_id=1, source_target_pairs={{0,4},{2,6},{4,0},{6,2},{1,5},{3,7},{5,1},{7,3},{8,12},{10,14},{12... | collective-permute-start | bytes 147464 | tf_op jit(solution)/shard_map/ppermute | solution.py:145
  97.9 3.8 %collective-permute-done.5 = f32[24,512]{1,0:T(8,128)S(1)} collective-permute-done((f32[24,512]{1,0:T(8,128)S(1)}, f32[24,512]{1,0:T(8,128)S(1)}, u32[]{:S(2)}, u32[]{:S(2)}) %collective-permute-start.5) | collective-permute-done | bytes 49184 | tf_op jit(solution)/shard_map/ppermute | solution.py:145
  101.8 4.5 %collective-permute-start.6 = (bf16[16,512]{1,0:T(8,128)(2,1)S(1)}, bf16[16,512]{1,0:T(8,128)(2,1)S(1)}, u32[]{:S(2)}, u32[]{:S(2)}) collective-permute-start(bf16[16,512]{1,0:T(8,128)(2,1)S(1)} %slice.41), channel_id=1, source_target_pairs={{0,8},{8,0},{16,24},{24,16},{1,9},{9,1},{17,25},{25,17},{2,10},{10... | collective-permute-start | bytes 49160 | tf_op jit(solution)/shard_map/ppermute | solution.py:145
  107.7 4.5 %collective-permute-start.7 = (bf16[32,512]{1,0:T(8,128)(2,1)S(1)}, bf16[32,512]{1,0:T(8,128)(2,1)S(1)}, u32[]{:S(2)}, u32[]{:S(2)}) collective-permute-start(bf16[32,512]{1,0:T(8,128)(2,1)S(1)} %pad_maximum_fusion.4), channel_id=1, source_target_pairs={{0,16},{8,24},{16,0},{24,8},{1,17},{9,25},{17,1},{25,9},{2,18},{10... | collective-permute-start | bytes 98312 | tf_op jit(solution)/shard_map/ppermute | solution.py:145
  114.9 9.5 %all-to-all-start.4 = ((bf16[4,128,512]{2,1,0:T(8,128)(2,1)}), bf16[4,128,512]{2,1,0:T(8,128)(2,1)S(1)}, u32[]{:S(2)}, u32[]{:S(2)}) async-start(bf16[4,128,512]{2,1,0:T(8,128)(2,1)} %bitcast.7), calls=%async_computation.4 | async-start | bytes 1048576 | tf_op jit(solution)/shard_map/all_to_all | solution.py:141
  124.4 2.3 %collective-permute-start.8 = (bf16[64,512]{1,0:T(8,128)(2,1)S(1)}, bf16[64,512]{1,0:T(8,128)(2,1)S(1)}, u32[]{:S(2)}, u32[]{:S(2)}) collective-permute-start(bf16[64,512]{1,0:T(8,128)(2,1)S(1)} %pad_maximum_fusion.3.refs_0_), channel_id=1, source_target_pairs={{0,64},{32,96},{64,0},{96,32},{1,65},{33,97},{65,1},{97,33},{2,66}... | collective-permute-start | bytes 196616 | tf_op jit(solution)/shard_map/ppermute | solution.py:145
  126.7 4.2 %collective-permute-done.8.refs_1_ = bf16[64,512]{1,0:T(8,128)(2,1)S(1)} collective-permute-done((bf16[64,512]{1,0:T(8,128)(2,1)S(1)}, bf16[64,512]{1,0:T(8,128)(2,1)S(1)}, u32[]{:S(2)}, u32[]{:S(2)}) %collective-permute-start.8) | collective-permute-done | bytes 65568 | tf_op jit(solution)/shard_map/ppermute | solution.py:145
  130.9 2.2 %collective-permute-start.9 = (bf16[128,512]{1,0:T(8,128)(2,1)S(1)}, bf16[128,512]{1,0:T(8,128)(2,1)S(1)}, u32[]{:S(2)}, u32[]{:S(2)}) collective-permute-start(bf16[128,512]{1,0:T(8,128)(2,1)S(1)} %pad_maximum_fusion.2), channel_id=1, source_target_pairs={{0,32},{32,0},{64,96},{96,64},{1,33},{33,1},{65,97},{97,65},{2,34}... | collective-permute-start | bytes 393224 | tf_op jit(solution)/shard_map/ppermute | solution.py:145
  133.1 3.8 %collective-permute-done.9.refs_2_ = bf16[128,512]{1,0:T(8,128)(2,1)S(1)} collective-permute-done((bf16[128,512]{1,0:T(8,128)(2,1)S(1)}, bf16[128,512]{1,0:T(8,128)(2,1)S(1)}, u32[]{:S(2)}, u32[]{:S(2)}) %collective-permute-start.9) | collective-permute-done | bytes 131104 | tf_op jit(solution)/shard_map/ppermute | solution.py:145
  136.9 6.2 %collective-permute-start.10 = (bf16[256,512]{1,0:T(8,128)(2,1)S(1)}, bf16[256,512]{1,0:T(8,128)(2,1)S(1)}, u32[]{:S(2)}, u32[]{:S(2)}) collective-permute-start(bf16[256,512]{1,0:T(8,128)(2,1)S(1)} %pad_maximum_fusion.1), channel_id=1, source_target_pairs={{0,1},{1,0},{2,3},{3,2},{4,5},{5,4},{6,7},{7,6},{8,9},{9,8},{10,11... | collective-permute-start | bytes 786440 | tf_op jit(solution)/shard_map/ppermute | solution.py:145
  145.8 6.8 %all-to-all-done.4.in_ref = bf16[4,128,512]{2,1,0:T(8,128)(2,1)S(1)} async-done(((bf16[4,128,512]{2,1,0:T(8,128)(2,1)}), bf16[4,128,512]{2,1,0:T(8,128)(2,1)S(1)}, u32[]{:S(2)}, u32[]{:S(2)}) %all-to-all-start.4) | async-done | bytes 524320 | tf_op jit(solution)/shard_map/all_to_all | solution.py:141
  (47 shorter events, 18.6 us)
Async XLA Ops:
  26.4 29.0 %all-to-all-start.1 = ((bf16[4,512,512]{2,1,0:T(8,128)(2,1)}), bf16[4,512,512]{2,1,0:T(8,128)(2,1)S(1)}, u32[]{:S(2)}, u32[]{:S(2)}) async-start(bf16[4,512,512]{2,1,0:T(8,128)(2,1)} %broadcast_in_dim.13), calls=%async_computation.1 | async-start | bytes 4194304 | tf_op jit(solution)/shard_map/all_to_all | solution.py:141
  32.2 5.0 %collective-permute-start = (f32[72,512]{1,0:T(8,128)S(1)}, f32[72,512]{1,0:T(8,128)S(1)}, u32[]{:S(2)}, u32[]{:S(2)}) collective-permute-start(f32[72,512]{1,0:T(8,128)S(1)} %get-tuple-element.14), channel_id=1, source_target_pairs={{0,1},{1,0},{2,3},{3,2},{4,5},{5,4},{6,7},{7,6},{8,9},{9,8},{10,11... | collective-permute-start | bytes 442376 | tf_op jit(solution)/shard_map/ppermute | solution.py:145
  37.2 7.1 %collective-permute-start.1 = (f32[40,512]{1,0:T(8,128)S(1)}, f32[40,512]{1,0:T(8,128)S(1)}, u32[]{:S(2)}, u32[]{:S(2)}) collective-permute-start(f32[40,512]{1,0:T(8,128)S(1)} %concatenate.45), channel_id=1, source_target_pairs={{0,64},{32,96},{64,0},{96,32},{1,65},{33,97},{65,1},{97,33},{2,66}... | collective-permute-start | bytes 245768 | tf_op jit(solution)/shard_map/ppermute | solution.py:145
  44.3 5.1 %collective-permute-start.2 = (f32[24,512]{1,0:T(8,128)S(1)}, f32[24,512]{1,0:T(8,128)S(1)}, u32[]{:S(2)}, u32[]{:S(2)}) collective-permute-start(f32[24,512]{1,0:T(8,128)S(1)} %concatenate.46), channel_id=1, source_target_pairs={{0,32},{32,0},{64,96},{96,64},{1,33},{33,1},{65,97},{97,65},{2,34}... | collective-permute-start | bytes 147464 | tf_op jit(solution)/shard_map/ppermute | solution.py:145
  55.4 18.4 %copy-start.1 = (bf16[4,512,512]{2,1,0:T(8,128)(2,1)}, bf16[4,512,512]{2,1,0:T(8,128)(2,1)S(1)}, u32[]{:S(2)}) copy-start(bf16[4,512,512]{2,1,0:T(8,128)(2,1)S(1)} %all-to-all-done.1.own_ref) | copy-start | bytes 6291460
  55.4 18.4 %collective-permute-start.3 = (bf16[4,512,512]{2,1,0:T(8,128)(2,1)S(1)}, bf16[4,512,512]{2,1,0:T(8,128)(2,1)}, u32[]{:S(2)}, u32[]{:S(2)}) collective-permute-start(bf16[4,512,512]{2,1,0:T(8,128)(2,1)S(1)} %all-to-all-done.1.own_ref), channel_id=1, source_target_pairs={{0,1},{1,0},{2,3},{3,2},{4,5},{5,4},{6,7},{7,6},{8,9},{9,8},{10,11... | collective-permute-start | bytes 6291464 | tf_op jit(solution)/shard_map/ppermute | solution.py:175
  61.0 25.3 %all-to-all-start.2 = ((f32[4,24,512]{2,1,0:T(8,128)}), f32[4,24,512]{2,1,0:T(8,128)S(1)}, u32[]{:S(2)}, u32[]{:S(2)}) async-start(f32[4,24,512]{2,1,0:T(8,128)} %broadcast_in_dim.14), calls=%async_computation.2 | async-start | bytes 393216 | tf_op jit(solution)/shard_map/all_to_all | solution.py:141
  86.3 27.5 %all-to-all-start.3 = ((bf16[4,512,512]{2,1,0:T(8,128)(2,1)}), bf16[4,512,512]{2,1,0:T(8,128)(2,1)S(1)}, u32[]{:S(2)}, u32[]{:S(2)}) async-start(bf16[4,512,512]{2,1,0:T(8,128)(2,1)} %get-tuple-element.19), calls=%async_computation.3 | async-start | bytes 4194304 | tf_op jit(solution)/shard_map/all_to_all | solution.py:141
  90.5 4.8 %collective-permute-start.4 = (f32[24,512]{1,0:T(8,128)S(1)}, f32[24,512]{1,0:T(8,128)S(1)}, u32[]{:S(2)}, u32[]{:S(2)}) collective-permute-start(f32[24,512]{1,0:T(8,128)S(1)} %reduce_sum.9), channel_id=1, source_target_pairs={{0,2},{2,0},{4,6},{6,4},{1,3},{3,1},{5,7},{7,5},{8,10},{10,8},{12,... | collective-permute-start | bytes 147464 | tf_op jit(solution)/shard_map/ppermute | solution.py:145
  95.4 6.3 %collective-permute-start.5 = (f32[24,512]{1,0:T(8,128)S(1)}, f32[24,512]{1,0:T(8,128)S(1)}, u32[]{:S(2)}, u32[]{:S(2)}) collective-permute-start(f32[24,512]{1,0:T(8,128)S(1)} %add.24), channel_id=1, source_target_pairs={{0,4},{2,6},{4,0},{6,2},{1,5},{3,7},{5,1},{7,3},{8,12},{10,14},{12... | collective-permute-start | bytes 147464 | tf_op jit(solution)/shard_map/ppermute | solution.py:145
  101.7 41.4 %copy-start.2 = (s32[32]{0:T(128)S(1)}, s32[32]{0:T(128)}, u32[]{:S(2)}) copy-start(s32[32]{0:T(128)} %constant.23.clone) | copy-start | bytes 388
  101.8 5.9 %collective-permute-start.6 = (bf16[16,512]{1,0:T(8,128)(2,1)S(1)}, bf16[16,512]{1,0:T(8,128)(2,1)S(1)}, u32[]{:S(2)}, u32[]{:S(2)}) collective-permute-start(bf16[16,512]{1,0:T(8,128)(2,1)S(1)} %slice.41), channel_id=1, source_target_pairs={{0,8},{8,0},{16,24},{24,16},{1,9},{9,1},{17,25},{25,17},{2,10},{10... | collective-permute-start | bytes 49160 | tf_op jit(solution)/shard_map/ppermute | solution.py:145
  107.7 6.1 %collective-permute-start.7 = (bf16[32,512]{1,0:T(8,128)(2,1)S(1)}, bf16[32,512]{1,0:T(8,128)(2,1)S(1)}, u32[]{:S(2)}, u32[]{:S(2)}) collective-permute-start(bf16[32,512]{1,0:T(8,128)(2,1)S(1)} %pad_maximum_fusion.4), channel_id=1, source_target_pairs={{0,16},{8,24},{16,0},{24,8},{1,17},{9,25},{17,1},{25,9},{2,18},{10... | collective-permute-start | bytes 98312 | tf_op jit(solution)/shard_map/ppermute | solution.py:145
  114.9 37.7 %copy-start = (bf16[512,512]{1,0:T(8,128)(2,1)S(1)}, bf16[512,512]{1,0:T(8,128)(2,1)}, u32[]{:S(2)}) copy-start(bf16[512,512]{1,0:T(8,128)(2,1)} %weight_ref.1) | copy-start | bytes 1572868
  114.9 37.7 %all-to-all-start.4 = ((bf16[4,128,512]{2,1,0:T(8,128)(2,1)}), bf16[4,128,512]{2,1,0:T(8,128)(2,1)S(1)}, u32[]{:S(2)}, u32[]{:S(2)}) async-start(bf16[4,128,512]{2,1,0:T(8,128)(2,1)} %bitcast.7), calls=%async_computation.4 | async-start | bytes 1048576 | tf_op jit(solution)/shard_map/all_to_all | solution.py:141
  124.4 6.5 %collective-permute-start.8 = (bf16[64,512]{1,0:T(8,128)(2,1)S(1)}, bf16[64,512]{1,0:T(8,128)(2,1)S(1)}, u32[]{:S(2)}, u32[]{:S(2)}) collective-permute-start(bf16[64,512]{1,0:T(8,128)(2,1)S(1)} %pad_maximum_fusion.3.refs_0_), channel_id=1, source_target_pairs={{0,64},{32,96},{64,0},{96,32},{1,65},{33,97},{65,1},{97,33},{2,66}... | collective-permute-start | bytes 196616 | tf_op jit(solution)/shard_map/ppermute | solution.py:145
  130.9 6.0 %collective-permute-start.9 = (bf16[128,512]{1,0:T(8,128)(2,1)S(1)}, bf16[128,512]{1,0:T(8,128)(2,1)S(1)}, u32[]{:S(2)}, u32[]{:S(2)}) collective-permute-start(bf16[128,512]{1,0:T(8,128)(2,1)S(1)} %pad_maximum_fusion.2), channel_id=1, source_target_pairs={{0,32},{32,0},{64,96},{96,64},{1,33},{33,1},{65,97},{97,65},{2,34}... | collective-permute-start | bytes 393224 | tf_op jit(solution)/shard_map/ppermute | solution.py:145
  136.9 7.3 %collective-permute-start.10 = (bf16[256,512]{1,0:T(8,128)(2,1)S(1)}, bf16[256,512]{1,0:T(8,128)(2,1)S(1)}, u32[]{:S(2)}, u32[]{:S(2)}) collective-permute-start(bf16[256,512]{1,0:T(8,128)(2,1)S(1)} %pad_maximum_fusion.1), channel_id=1, source_target_pairs={{0,1},{1,0},{2,3},{3,2},{4,5},{5,4},{6,7},{7,6},{8,9},{9,8},{10,11... | collective-permute-start | bytes 786440 | tf_op jit(solution)/shard_map/ppermute | solution.py:145
